TPU v7x, 32 devices: a whole 2x2x4 slice. The times are simulated.
32 devices in a mesh: sec: 2 (over x), gx: 4 (over y, core), gy: 4 (over z).
Axes of the slice: x: 2, y: 2, z: 4, core: 2. Of those that a mesh axis runs over, the one named last changes fastest.
Arguments:
- pressure: float32 [50, 128, 512], P(None, ('sec', 'gx'), 'gy'), may hold values from -4 to 4
- pressure_old: float32 [50, 128, 512], P(None, ('sec', 'gx'), 'gy'), may hold values from -4 to 4
- conductivity: float32 [50, 128, 512], P(None, ('sec', 'gx'), 'gy'), may hold values from 0.3 to 3
- vg_alpha: float32 [50, 128, 512], P(None, ('sec', 'gx'), 'gy'), may hold values from 0.5 to 4
- porosity: float32 [50, 128, 512], P(None, ('sec', 'gx'), 'gy'), may hold values from 0.3 to 0.5
- land_mask: int32 [128, 512], P(('sec', 'gx'), 'gy'), may hold values 0 or 1
- nitrate: float32 [10, 8192], P(None, ('sec', 'gx', 'gy')), may hold values from 0.5 to 2
- patch_column: int32 [8192], P(('sec', 'gx', 'gy')), may hold values from 0 to 2047
- crop_type: int32 [8192], P(('sec', 'gx', 'gy')), may hold values from 0 to 7
- patch_weight: float32 [8192], P(('sec', 'gx', 'gy')), may hold values from 0.2 to 2
- rain: float32 [8192], P(('sec', 'gx', 'gy')), may hold values from 0.1 to 1
- root_decay: float32 [8], replicated, may hold values from 0.05 to 0.8
Outputs:
- residual: float32 [50, 128, 512], P(None, ('sec', 'gx'), 'gy')
- nitrate_out: float32 [10, 8192], P(None, ('sec', 'gx', 'gy'))
All inputs are finite; a program needn't handle non-finite values. No bound on the sum of `land_mask` on one device may be relied on, other than what follows from the above.
Results may differ from a plain program's by a relative error of at most 0.0003.
The roundings to bfloat16 on the way count: a program that leaves them out, or rounds other values in their place, can miss the bound.
Values may be sent and summed in bfloat16 or wider, within the bound.
No kernel may reach another device: no remote copies, remote signals or barrier semaphores. Data moves between devices by JAX's collectives and lax.ppermute only.
A program may use at most 192 MiB of HBM per device.

v0:
```python
import jax
import jax.numpy as jnp
from jax import lax
from jax.sharding import PartitionSpec as P

NSUB = 4


def with_halo(value, sides, width):
    for axis, dim in sides:
        peers, length = (lax.axis_size(axis), value.shape[dim])
        up = [(i, (i + 1) % peers) for i in range(peers - 1)]
        down = [(j, i) for i, j in up]
        last = lax.slice_in_dim(value, length - width, length, axis=dim)
        leading = lax.slice_in_dim(value, 0, width, axis=dim)
        before = lax.ppermute(last, axis, up)
        after = lax.ppermute(leading, axis, down)
        value = jnp.concatenate([before, value, after], axis=dim)
    return value


def saturation(head, alpha_field):
    suction = jax.nn.softplus(-head)
    scaled = alpha_field * suction
    return 1.0 / jnp.sqrt(1.0 + scaled * scaled)


def outflow(pressure, conduct, head_pad, cond_pad):
    head_x = head_pad[:, :, 1:-1]
    cond_x = cond_pad[:, :, 1:-1]
    flux_x = 0.5 * (cond_x[:, :-1] + cond_x[:, 1:]) * (head_x[:, :-1] - head_x[:, 1:])
    head_y = head_pad[:, 1:-1, :]
    cond_y = cond_pad[:, 1:-1, :]
    flux_y = 0.5 * (cond_y[:, :, :-1] + cond_y[:, :, 1:]) * (head_y[:, :, :-1] - head_y[:, :, 1:])
    flux_z = 0.5 * (conduct[:-1] + conduct[1:]) * (pressure[:-1] - pressure[1:] + 1.0)
    zero_top = jnp.zeros_like(conduct[:1])
    flux_z = jnp.concatenate([zero_top, flux_z, conduct[-1:]], 0)
    return (
        flux_x[:, 1:]
        - flux_x[:, :-1]
        + (flux_y[:, :, 1:] - flux_y[:, :, :-1])
        + (flux_z[1:] - flux_z[:-1])
    )


def deposit(values, targets, columns):
    slots = targets.shape[0]
    stride = 512 if slots % 512 == 0 else slots
    cells = jnp.arange(columns, dtype=jnp.int32)
    total = jnp.zeros((values.shape[0], columns), jnp.float32)
    for start in range(0, slots, stride):
        onehot = (targets[start : start + stride, None] == cells[None, :]).astype(jnp.float32)
        total = total + jnp.dot(
            values[:, start : start + stride],
            onehot,
            precision=lax.Precision.HIGHEST,
            preferred_element_type=jnp.float32,
        )
    return total


def patch_sources(sat_p, kinds_of, root_decay, weights, rainfall, top):
    kinds = jnp.arange(root_decay.shape[0], dtype=jnp.int32)
    decay = jnp.sum(
        jnp.where(kinds_of[None, :] == kinds[:, None], root_decay[:, None], 0.0), axis=0
    )
    levels = jnp.arange(top, dtype=jnp.float32) + 0.5
    profile = jnp.exp(-levels[:, None] * decay[None, :])
    profile = profile / jnp.sum(profile, axis=0, keepdims=True)
    extraction = weights[None, :] * profile * sat_p
    inflow = rainfall * (1.0 - sat_p[0])
    return jnp.concatenate([(inflow - extraction[0])[None], -extraction[1:]], 0)


def per_device(
    pressure,
    pressure_old,
    conductivity,
    vg_alpha,
    porosity,
    land_mask,
    nitrate,
    patch_column,
    crop_type,
    patch_weight,
    rain,
    root_decay,
):
    layers, width_x, width_y = pressure.shape
    top = nitrate.shape[0]
    kind_count = root_decay.shape[0]
    columns = width_x * width_y
    slots = patch_column.shape[0]
    owners = lax.axis_size(("gx", "gy"))
    per_block = slots // owners
    wet = saturation(pressure, vg_alpha)
    wet_old = saturation(pressure_old, vg_alpha)
    conduct = conductivity * wet * wet * wet
    sat_top = wet[:top].reshape(top, columns).astype(jnp.bfloat16)
    coded = patch_column * kind_count + crop_type
    codes_in = lax.all_to_all(
        coded.reshape(1, slots), ("gx", "gy"), split_axis=1, concat_axis=1, tiled=True
    )[0]
    ids_in = codes_in // kind_count
    whole = lax.all_gather(sat_top, ("gx", "gy"), axis=1, tiled=True)
    offsets = jnp.arange(slots, dtype=jnp.int32) // per_block * columns
    patch_sat = jnp.take(whole, offsets + patch_column, axis=1)
    sat_p = patch_sat.astype(jnp.float32)
    sources = patch_sources(sat_p, crop_type, root_decay, patch_weight, rain, top)
    received = lax.all_to_all(
        sources.astype(jnp.bfloat16), ("gx", "gy"), split_axis=1, concat_axis=1, tiled=True
    ).astype(sources.dtype)
    nitrogen = nitrate
    for step in range(NSUB):
        upper = jnp.concatenate([nitrogen[:1], nitrogen[:-1]], 0)
        lower = jnp.concatenate([nitrogen[1:], nitrogen[-1:]], 0)
        nitrogen = (
            nitrogen + 0.2 * (upper + lower - 2.0 * nitrogen) - 0.3 * sat_p * sat_p * nitrogen
        )
    stacked = jnp.stack([pressure, conduct])
    padded = with_halo(stacked, ((("sec", "gx"), 2), ("gy", 3)), 1)
    residual = porosity * (wet - wet_old) + outflow(pressure, conduct, padded[0], padded[1])
    column_source = deposit(received, ids_in, columns).reshape(top, width_x, width_y)
    column_source = column_source * land_mask.astype(jnp.float32)[None]
    residual = jnp.concatenate([residual[:top] - column_source, residual[top:]], 0)
    return (residual, nitrogen)


def solution(mesh):
    placed = (
        P(None, ("sec", "gx"), "gy"),
        P(None, ("sec", "gx"), "gy"),
        P(None, ("sec", "gx"), "gy"),
        P(None, ("sec", "gx"), "gy"),
        P(None, ("sec", "gx"), "gy"),
        P(("sec", "gx"), "gy"),
        P(None, ("sec", "gx", "gy")),
        P(("sec", "gx", "gy")),
        P(("sec", "gx", "gy")),
        P(("sec", "gx", "gy")),
        P(("sec", "gx", "gy")),
        P(),
    )
    return jax.shard_map(
        per_device,
        mesh=mesh,
        in_specs=placed,
        out_specs=(P(None, ("sec", "gx"), "gy"), P(None, ("sec", "gx", "gy"))),
        check_vma=False,
    )
```

profile of v0, /device:TPU:0, one launch (start us, length us, event | category | flops | bytes accessed | tf_op | source)
XLA Modules:
  0.0 239.4 jit_solution(622747574008032368)
XLA Ops:
  0.7 1.8 multiply_multiply_fusion
  2.5 1.3 collective-permute-start.1
  3.8 3.0 %collective-permute-start = (f32[2,50,1,128]{3,1,2,0:T(8,128)S(1)}, f32[2,50,1,128]{3,1,2,0:T(8,128)S(1)}, u32[]{:S(2)}, u32[]{:S(2)}) collective-permute-start(f32[2,50,1,128]{3,1,2,0:T(8,128)S(1)} %get-tuple-element.22), channel_id=1, source_target_pairs={{0,4},{4,8},{8,12},{12,16},{16,20},{20,24},{24,28},{1,5},{5,9},{9,... | collective-permute-start | bytes 153608 | tf_op jit(solution)/shard_map/ppermute | solution.py:16
  6.9 0.7 all_to_all.14
  7.6 9.0 %all-to-all-start.1 = ((s32[1,16,16]{2,0,1:T(1,128)}), s32[1,16,16]{2,0,1:T(1,128)S(1)}, u32[]{:S(2)}, u32[]{:S(2)}) async-start(s32[1,16,16]{2,0,1:T(1,128)} %all_to_all.14), calls=%async_computation.1 | async-start | bytes 16384 | tf_op jit(solution)/shard_map/all_to_all | solution.py:101
  16.9 190.1 %all_gather.3 = bf16[10,32768]{0,1:T(8,128)(2,1)} all-gather(bf16[10,2048]{0,1:T(8,128)(2,1)S(1)} %bitcast.27), channel_id=1, replica_groups=mesh['sec'=2,'gx'=4,'gy'=4] {'gx','gy'}, dimensions={1}, use_global_device_ids=true | all-gather | bytes 696320 | tf_op jit(solution)/shard_map/all_gather | solution.py:105
  207.0 5.2 %gather_fusion = bf16[256,10]{1,0:T(8,128)(2,1)S(1)} fusion(bf16[10,32768]{0,1:T(8,128)(2,1)} %all_gather.3, s32[1024]{0:T(1024)S(1)} %pad_clamp_fusion), kind=kCustom, calls=%fused_computation | custom fusion | bytes 11264 | tf_op jit(solution)/shard_map/jit(_take)/gather | solution.py:107
  212.7 0.6 fusion.46
  213.4 0.9 fusion.26
  214.5 0.7 pad_maximum_fusion.3
  215.2 0.6 multiply_add_fusion
  215.8 0.6 slice.219
  216.4 0.6 convert_element_type.16
  217.0 3.5 %all-to-all-start = ((bf16[10,16,16]{2,0,1:T(8,128)(2,1)}), bf16[10,16,16]{2,0,1:T(8,128)(2,1)S(1)}, u32[]{:S(2)}, u32[]{:S(2)}) async-start(bf16[10,16,16]{2,0,1:T(8,128)(2,1)} %pad_maximum_fusion.3), calls=%async_computation | async-start | bytes 131072 | tf_op jit(solution)/shard_map/all_to_all | solution.py:110
  221.7 0.6 copy-done.4
  222.3 0.6 copy-done.6
  223.3 1.0 copy.195
  224.4 1.3 collective-permute-start.3
  226.1 5.1 %collective-permute-start.2 = (f32[2,50,18,1]{1,0,3,2:T(2,128)S(1)}, f32[2,50,18,1]{1,0,3,2:T(2,128)}, u32[]{:S(2)}, u32[]{:S(2)}) collective-permute-start(f32[2,50,18,1]{1,0,3,2:T(2,128)S(1)} %copy.194), channel_id=1, source_target_pairs={{0,1},{1,2},{2,3},{4,5},{5,6},{6,7},{8,9},{9,10},{10,11},{12,13},{... | collective-permute-start | bytes 21608 | tf_op jit(solution)/shard_map/ppermute | solution.py:16
  231.9 0.7 reshape.92
  233.0 1.2 copy.196
  234.3 0.9 pad_maximum_fusion
  237.2 0.7 fusion.24
  238.6 0.8 copy.206
  (88 shorter events, 6.7 us)
Async XLA Ops:
  0.6 6.2 %copy-start.14 = (s32[256]{0:T(256)S(1)}, s32[256]{0:T(256)}, u32[]{:S(2)}) copy-start(s32[256]{0:T(256)} %param.19) | copy-start | bytes 3076
  0.6 6.2 %copy-start.15 = (s32[256]{0:T(256)S(1)}, s32[256]{0:T(256)}, u32[]{:S(2)}) copy-start(s32[256]{0:T(256)} %param.20) | copy-start | bytes 3076
  0.7 15.9 %copy-start.8 = (f32[10,256]{1,0:T(8,128)S(1)}, f32[10,256]{1,0:T(8,128)}, u32[]{:S(2)}) copy-start(f32[10,256]{1,0:T(8,128)} %param.18) | copy-start | bytes 30724
  2.5 219.2 %collective-permute-start.1 = (f32[2,50,1,128]{3,1,2,0:T(8,128)S(1)}, f32[2,50,1,128]{3,1,2,0:T(8,128)S(1)}, u32[]{:S(2)}, u32[]{:S(2)}) collective-permute-start(f32[2,50,1,128]{3,1,2,0:T(8,128)S(1)} %get-tuple-element.23), channel_id=1, source_target_pairs={{4,0},{8,4},{12,8},{16,12},{20,16},{24,20},{28,24},{5,1},{9,5},{13... | collective-permute-start | bytes 153608 | tf_op jit(solution)/shard_map/ppermute | solution.py:17
  3.8 217.9 %collective-permute-start = (f32[2,50,1,128]{3,1,2,0:T(8,128)S(1)}, f32[2,50,1,128]{3,1,2,0:T(8,128)S(1)}, u32[]{:S(2)}, u32[]{:S(2)}) collective-permute-start(f32[2,50,1,128]{3,1,2,0:T(8,128)S(1)} %get-tuple-element.22), channel_id=1, source_target_pairs={{0,4},{4,8},{8,12},{12,16},{16,20},{20,24},{24,28},{1,5},{5,9},{9,... | collective-permute-start | bytes 153608 | tf_op jit(solution)/shard_map/ppermute | solution.py:16
  7.6 209.4 %all-to-all-start.1 = ((s32[1,16,16]{2,0,1:T(1,128)}), s32[1,16,16]{2,0,1:T(1,128)S(1)}, u32[]{:S(2)}, u32[]{:S(2)}) async-start(s32[1,16,16]{2,0,1:T(1,128)} %all_to_all.14), calls=%async_computation.1 | async-start | bytes 16384 | tf_op jit(solution)/shard_map/all_to_all | solution.py:101
  16.9 195.6 %copy-start.19 = (f32[8]{0:T(128)S(1)}, f32[8]{0:T(128)}, u32[]{:S(2)}) copy-start(f32[8]{0:T(128)} %param.23) | copy-start | bytes 100
  16.9 195.8 %copy-start.16 = (f32[256]{0:T(256)S(1)}, f32[256]{0:T(256)}, u32[]{:S(2)}) copy-start(f32[256]{0:T(256)} %param.21) | copy-start | bytes 3076
  207.0 7.4 %copy-start.17 = (f32[256]{0:T(256)S(1)}, f32[256]{0:T(256)}, u32[]{:S(2)}) copy-start(f32[256]{0:T(256)} %param.22) | copy-start | bytes 3076
  207.0 9.4 %copy-start.10 = (s32[16,128]{1,0:T(8,128)S(1)}, s32[16,128]{1,0:T(8,128)}, u32[]{:S(2)}) copy-start(s32[16,128]{1,0:T(8,128)} %param.17) | copy-start | bytes 24580
  217.0 14.8 %all-to-all-start = ((bf16[10,16,16]{2,0,1:T(8,128)(2,1)}), bf16[10,16,16]{2,0,1:T(8,128)(2,1)S(1)}, u32[]{:S(2)}, u32[]{:S(2)}) async-start(bf16[10,16,16]{2,0,1:T(8,128)(2,1)} %pad_maximum_fusion.3), calls=%async_computation | async-start | bytes 131072 | tf_op jit(solution)/shard_map/all_to_all | solution.py:110
  224.4 8.2 %collective-permute-start.3 = (f32[2,50,18,1]{1,0,3,2:T(2,128)}, f32[2,50,18,1]{1,0,3,2:T(2,128)S(1)}, u32[]{:S(2)}, u32[]{:S(2)}) collective-permute-start(f32[2,50,18,1]{1,0,3,2:T(2,128)} %copy.195), channel_id=1, source_target_pairs={{1,0},{2,1},{3,2},{5,4},{6,5},{7,6},{9,8},{10,9},{11,10},{13,12},{... | collective-permute-start | bytes 21608 | tf_op jit(solution)/shard_map/ppermute | solution.py:17
  226.1 7.0 %collective-permute-start.2 = (f32[2,50,18,1]{1,0,3,2:T(2,128)S(1)}, f32[2,50,18,1]{1,0,3,2:T(2,128)}, u32[]{:S(2)}, u32[]{:S(2)}) collective-permute-start(f32[2,50,18,1]{1,0,3,2:T(2,128)S(1)} %copy.194), channel_id=1, source_target_pairs={{0,1},{1,2},{2,3},{4,5},{5,6},{6,7},{8,9},{9,10},{10,11},{12,13},{... | collective-permute-start | bytes 21608 | tf_op jit(solution)/shard_map/ppermute | solution.py:16
  231.8 2.4 %copy-start.5 = (f32[2,50,1,128]{3,1,2,0:T(8,128)S(1)}, f32[2,50,1,128]{3,1,2,0:T(8,128)}, u32[]{:S(2)}) copy-start(f32[2,50,1,128]{3,1,2,0:T(8,128)} %copy-done.4) | copy-start | bytes 153604
  231.8 2.4 %copy-start.7 = (f32[2,50,1,128]{3,1,2,0:T(8,128)S(1)}, f32[2,50,1,128]{3,1,2,0:T(8,128)}, u32[]{:S(2)}) copy-start(f32[2,50,1,128]{3,1,2,0:T(8,128)} %copy-done.6) | copy-start | bytes 153604
  235.8 1.0 copy-start
  235.8 1.1 copy-start.1
  235.9 1.2 copy-start.2
  235.9 1.4 copy-start.3
  235.9 1.4 copy-start.9
  237.2 0.8 copy-start.11
  237.2 0.8 copy-start.12
  237.2 0.8 copy-start.13
  237.2 0.8 copy-start.18
  (2 other events, 1.2 us)
where the time goes:
time: 240 us; the launch traced here: 239 us
  blocking collectives  190 us (79%)
  starting transfers between devices  23.2 us (10%)
  local copies, waits for them, and re-layouts  15 us (6%)
  other arithmetic  9.55 us (4%)
    all_gather x1, blocking collectives, per_device(): whole = lax.all_gather(sat_top, ('gx', 'gy'), axis=1, tiled=True)  190 us
    all_to_all x1, starting transfers between devices, per_device(): lax.all_to_all(coded.reshape(1, slots), ('gx', 'gy'), split_axis=1, conca...  8.96 us
    ppermute x2, starting transfers between devices, with_halo(): before = lax.ppermute(last, axis, up)  8.17 us
    gather x2, local copies, waits for them, and re-layouts, per_device(): patch_sat = jnp.take(whole, offsets + patch_column, axis=1)  5.28 us
  transfers between devices with their start and end apart: 6, of which 0 were waited for; matrix products, arithmetic and copies ran while one was open for 6% of the time, Pallas kernels for 0%

commit v1 on v0

v1 whole, which is shorter than its diff:
```python
import jax
import jax.numpy as jnp
from jax import lax
from jax.sharding import PartitionSpec as P

NSUB = 4


def swap_pairs(size, first):
    pairs = []
    for i in range(first, size - 1, 2):
        pairs += [(i, i + 1), (i + 1, i)]
    return pairs


def neighbours(value, axis, dim):
    size, length = (lax.axis_size(axis), value.shape[dim])
    even = lax.axis_index(axis) % 2 == 0
    leading = lax.slice_in_dim(value, 0, 1, axis=dim)
    last = lax.slice_in_dim(value, length - 1, length, axis=dim)
    first_swap = lax.ppermute(jnp.where(even, last, leading), axis, swap_pairs(size, 0))
    second_swap = lax.ppermute(jnp.where(even, leading, last), axis, swap_pairs(size, 1))
    before = jnp.where(even, second_swap, first_swap)
    after = jnp.where(even, first_swap, second_swap)
    return before, after


def saturation(head, alpha_field):
    suction = jax.nn.softplus(-head)
    scaled = alpha_field * suction
    return 1.0 / jnp.sqrt(1.0 + scaled * scaled)


def outflow(pressure, conduct, sides_x, sides_y):
    def flux(head, cond, before, after, dim):
        head = jnp.concatenate([before[0], head, after[0]], dim)
        cond = jnp.concatenate([before[1], cond, after[1]], dim)
        size = head.shape[dim]
        low = lambda v: lax.slice_in_dim(v, 0, size - 1, axis=dim)
        high = lambda v: lax.slice_in_dim(v, 1, size, axis=dim)
        face = 0.5 * (low(cond) + high(cond)) * (low(head) - high(head))
        return lax.slice_in_dim(face, 1, size - 1, axis=dim) - lax.slice_in_dim(face, 0, size - 2, axis=dim)

    flux_z = 0.5 * (conduct[:-1] + conduct[1:]) * (pressure[:-1] - pressure[1:] + 1.0)
    flux_z = jnp.concatenate([jnp.zeros_like(conduct[:1]), flux_z, conduct[-1:]], 0)
    return (
        flux(pressure, conduct, *sides_x, 1)
        + flux(pressure, conduct, *sides_y, 2)
        + (flux_z[1:] - flux_z[:-1])
    )


def deposit(values, row_hot, lane_hot):
    spread = values[:, None, :] * row_hot[None]
    top, width_x, slots = spread.shape
    total = lax.dot_general(
        spread.reshape(top * width_x, slots),
        lane_hot,
        (((1,), (1,)), ((), ())),
        precision=lax.Precision.HIGHEST,
        preferred_element_type=jnp.float32,
    )
    return total.reshape(top, width_x, lane_hot.shape[0])


def patch_sources(sat_p, kinds_of, root_decay, weights, rainfall, top):
    kinds = jnp.arange(root_decay.shape[0], dtype=jnp.int32)
    decay = jnp.sum(
        jnp.where(kinds_of[None, :] == kinds[:, None], root_decay[:, None], 0.0), axis=0
    )
    levels = jnp.arange(top, dtype=jnp.float32) + 0.5
    profile = jnp.exp(-levels[:, None] * decay[None, :])
    profile = profile / jnp.sum(profile, axis=0, keepdims=True)
    extraction = weights[None, :] * profile * sat_p
    inflow = rainfall * (1.0 - sat_p[0])
    return jnp.concatenate([(inflow - extraction[0])[None], -extraction[1:]], 0)


def per_device(
    pressure,
    pressure_old,
    conductivity,
    vg_alpha,
    porosity,
    land_mask,
    nitrate,
    patch_column,
    crop_type,
    patch_weight,
    rain,
    root_decay,
):
    layers, width_x, width_y = pressure.shape
    top = nitrate.shape[0]
    slots = patch_column.shape[0]
    owners = lax.axis_size(("gx", "gy"))
    per_block = slots // owners
    wet = saturation(pressure, vg_alpha)
    wet_old = saturation(pressure_old, vg_alpha)
    conduct = conductivity * wet * wet * wet
    sat_top = wet[:top].astype(jnp.bfloat16)
    group = ("gx", "gy")
    sent = jnp.stack([patch_column.astype(jnp.float32), crop_type.astype(jnp.float32), patch_weight, rain])
    sent = sent.reshape(4, owners, per_block).transpose(1, 0, 2).reshape(owners, 4 * per_block)
    got = lax.all_to_all(sent, group, split_axis=0, concat_axis=0, tiled=True)
    got = got.reshape(owners, 4, per_block).transpose(1, 0, 2).reshape(4, slots)
    ids = got[0].astype(jnp.int32)
    row_hot = (ids // width_y)[None, :] == jnp.arange(width_x, dtype=jnp.int32)[:, None]
    lane_hot = (ids % width_y)[None, :] == jnp.arange(width_y, dtype=jnp.int32)[:, None]
    picked = jnp.dot(
        sat_top.reshape(top * width_x, width_y),
        lane_hot.astype(jnp.bfloat16),
        preferred_element_type=jnp.float32,
    ).reshape(top, width_x, slots)
    patch_sat = jnp.sum(jnp.where(row_hot[None], picked, 0.0), 1)
    back = patch_sat.astype(jnp.bfloat16).reshape(top, owners, per_block).transpose(1, 0, 2).reshape(owners, top * per_block)
    back = lax.all_to_all(back, group, split_axis=0, concat_axis=0, tiled=True)
    sat_p = back.reshape(owners, top, per_block).transpose(1, 0, 2).reshape(top, slots).astype(jnp.float32)
    sources = patch_sources(patch_sat, got[1].astype(jnp.int32), root_decay, got[2], got[3], top)
    nitrogen = nitrate
    for step in range(NSUB):
        upper = jnp.concatenate([nitrogen[:1], nitrogen[:-1]], 0)
        lower = jnp.concatenate([nitrogen[1:], nitrogen[-1:]], 0)
        nitrogen = (
            nitrogen + 0.2 * (upper + lower - 2.0 * nitrogen) - 0.3 * sat_p * sat_p * nitrogen
        )
    stacked = jnp.stack([pressure, conduct])
    sides_x = neighbours(stacked, ("sec", "gx"), 2)
    sides_y = neighbours(stacked, "gy", 3)
    residual = porosity * (wet - wet_old) + outflow(pressure, conduct, sides_x, sides_y)
    column_source = deposit(sources, row_hot.astype(jnp.float32), lane_hot.astype(jnp.float32))
    column_source = column_source * land_mask.astype(jnp.float32)[None]
    residual = jnp.concatenate([residual[:top] - column_source, residual[top:]], 0)
    return (residual, nitrogen)


def solution(mesh):
    placed = (
        P(None, ("sec", "gx"), "gy"),
        P(None, ("sec", "gx"), "gy"),
        P(None, ("sec", "gx"), "gy"),
        P(None, ("sec", "gx"), "gy"),
        P(None, ("sec", "gx"), "gy"),
        P(("sec", "gx"), "gy"),
        P(None, ("sec", "gx", "gy")),
        P(("sec", "gx", "gy")),
        P(("sec", "gx", "gy")),
        P(("sec", "gx", "gy")),
        P(("sec", "gx", "gy")),
        P(),
    )
    return jax.shard_map(
        per_device,
        mesh=mesh,
        in_specs=placed,
        out_specs=(P(None, ("sec", "gx"), "gy"), P(None, ("sec", "gx", "gy"))),
        check_vma=False,
    )
```

time: 240 us -> 49.4 us (0.21)
  blocking collectives: 190 us -> 0 us
  waiting for transfers between devices: 0.02 us -> 6.43 us
  starting transfers between devices: 23.2 us -> 19.6 us
  local copies, waits for them, and re-layouts: 15 us -> 11.9 us
    all_gather x1 -> x0, blocking collectives: 190 us -> none  [per_device(): whole = lax.all_gather(sat_top, ('gx', 'gy'), axis=1, tiled=True)]
    all_to_all x2, waiting for transfers between devices: 0.01 us -> 6.42 us  [the longest x1 6.41 us: per_device(): back = lax.all_to_all(back, group, split_axis=0, concat_axis=0, tiled=True)]
    ppermute x4, starting transfers between devices: 10.7 us -> 4.44 us  [the longest x2 3.13 us: neighbours(): lax.ppermute(jnp.where(even, last, leading), axis, swap_pairs(size, 0))]
    gather x2 -> x0, local copies, waits for them, and re-layouts: 5.28 us -> none  [per_device(): patch_sat = jnp.take(whole, offsets + patch_column, axis=1)]
    all_to_all x2, starting transfers between devices: 12.5 us -> 15.1 us  [the longest x1 9.18 us: per_device(): got = lax.all_to_all(sent, group, split_axis=0, concat_axis=0, tiled=True)]
  transfers between devices with their start and end apart: 6 -> 6, of which waited for: 0 -> 1; matrix products, arithmetic and copies ran while one was open for 6% -> 24% of each run, Pallas kernels for 0% -> 0%
where the time goes in v1:
time: 49.4 us; the launch traced here: 48.9 us
  starting transfers between devices  19.6 us (40%)
  local copies, waits for them, and re-layouts  11.9 us (24%)
  other arithmetic  8.43 us (17%)
  waiting for transfers between devices  6.43 us (13%)
  matrix products  1.38 us (3%)
  between operations  1.12 us (2%)
    all_to_all x1, starting transfers between devices, per_device(): got = lax.all_to_all(sent, group, split_axis=0, concat_axis=0, tiled=True)  9.18 us
    all_to_all x1, waiting for transfers between devices, per_device(): back = lax.all_to_all(back, group, split_axis=0, concat_axis=0, tiled=True)  6.41 us
    all_to_all x1, starting transfers between devices, per_device(): back = lax.all_to_all(back, group, split_axis=0, concat_axis=0, tiled=True)  5.95 us
    unnamed x30, local copies, waits for them, and re-layouts  4.19 us
    ppermute x2, starting transfers between devices, neighbours(): lax.ppermute(jnp.where(even, last, leading), axis, swap_pairs(size, 0))  3.13 us
    mul x1, other arithmetic, per_device(): conduct = conductivity * wet * wet * wet  1.63 us
    all_to_all x1, other arithmetic, per_device(): got = lax.all_to_all(sent, group, split_axis=0, concat_axis=0, tiled=True)  1.37 us
    ppermute x2, starting transfers between devices, neighbours(): lax.ppermute(jnp.where(even, leading, last), axis, swap_pairs(size, 1))  1.32 us
  transfers between devices with their start and end apart: 6, of which 1 were waited for; matrix products, arithmetic and copies ran while one was open for 24% of the time, Pallas kernels for 0%

profile of v1, /device:TPU:0, one launch (start us, length us, event | category | flops | bytes accessed | tf_op | source)
XLA Modules:
  0.0 48.9 jit_solution(9769095217460091976)
XLA Ops:
  0.7 1.6 %multiply_multiply_fusion = f32[50,16,128]{2,1,0:T(8,128)S(1)} fusion(f32[50,16,128]{2,1,0:T(8,128)} %param.14, f32[50,16,128]{2,1,0:T(8,128)} %param.15, f32[50,16,128]{2,1,0:T(8,128)} %param.12), kind=kLoop, calls=%fused_computation.18 | loop fusion | flops 1331200 | bytes 1638400 | tf_op jit(solution)/shard_map/mul | solution.py:100
  3.0 3.1 %collective-permute-start.3 = (f32[2,50,16,1]{1,2,3,0:T(8,128)S(1)}, f32[2,50,16,1]{1,2,3,0:T(8,128)S(1)}, u32[]{:S(2)}, u32[]{:S(2)}) collective-permute-start(f32[2,50,16,1]{1,2,3,0:T(8,128)S(1)} %copy.88), channel_id=1, source_target_pairs={{0,1},{1,0},{2,3},{3,2},{4,5},{5,4},{6,7},{7,6},{8,9},{9,8},{10,11... | collective-permute-start | bytes 19208 | tf_op jit(solution)/shard_map/ppermute | solution.py:21
  6.5 0.7 %collective-permute-start.2 = (f32[2,50,16,1]{1,2,3,0:T(8,128)S(1)}, f32[2,50,16,1]{1,2,3,0:T(8,128)S(1)}, u32[]{:S(2)}, u32[]{:S(2)}) collective-permute-start(f32[2,50,16,1]{1,2,3,0:T(8,128)S(1)} %copy.87), channel_id=1, source_target_pairs={{1,2},{2,1},{5,6},{6,5},{9,10},{10,9},{13,14},{14,13},{17,18},{18,... | collective-permute-start | bytes 19208 | tf_op jit(solution)/shard_map/ppermute | solution.py:22
  7.4 0.7 %collective-permute-start = (f32[2,50,1,128]{3,2,1,0:T(1,128)S(1)}, f32[2,50,1,128]{3,2,1,0:T(1,128)S(1)}, u32[]{:S(2)}, u32[]{:S(2)}) collective-permute-start(f32[2,50,1,128]{3,2,1,0:T(1,128)S(1)} %broadcast_select_fusion.5), channel_id=1, source_target_pairs={{4,8},{8,4},{12,16},{16,12},{20,24},{24,20},{5,9},{9,5},{13,17},{1... | collective-permute-start | bytes 153608 | tf_op jit(solution)/shard_map/ppermute | solution.py:22
  8.3 0.6 %copy-done.11 = s32[256]{0:T(256)S(1)} copy-done((s32[256]{0:T(256)S(1)}, s32[256]{0:T(256)}, u32[]{:S(2)}) %copy-start.11) | copy-done | bytes 1048
  9.0 0.6 %copy-done.12 = s32[256]{0:T(256)S(1)} copy-done((s32[256]{0:T(256)S(1)}, s32[256]{0:T(256)}, u32[]{:S(2)}) %copy-start.12) | copy-done | bytes 1048
  9.7 0.7 %all_to_all.12 = f32[16,1,64]{2,0,1:T(8,128)} reshape(f32[16,4,16]{2,1,0:T(4,128)S(1)} %maximum_bitcast_fusion) | data formatting | bytes 8192 | tf_op jit(solution)/shard_map/all_to_all | solution.py:105
  10.4 9.2 %all-to-all-start = ((f32[16,1,64]{2,1,0:T(1,128)}), f32[16,1,64]{2,1,0:T(1,128)}, u32[]{:S(2)}, u32[]{:S(2)}) async-start(f32[16,1,64]{2,1,0:T(1,128)} %bitcast.11), calls=%async_computation | async-start | bytes 16384 | tf_op jit(solution)/shard_map/all_to_all | solution.py:105
  19.6 0.8 %fusion.22 = f32[49,16,128]{2,1,0:T(8,128)} fusion(f32[50,16,128]{2,1,0:T(8,128)S(1)} %multiply_multiply_fusion, f32[50,16,128]{2,1,0:T(8,128)S(1)} %copy-done), kind=kLoop, calls=%fused_computation.40 | loop fusion | flops 501760 | bytes 2007040 | tf_op jit(solution)/shard_map/mul | solution.py:44
  20.4 0.6 %fusion.64 = (f32[1,256]{1,0:T(1,128)}, f32[1,256]{1,0:T(1,128)}) fusion(f32[10,256]{1,0:T(8,128)S(1)} %copy-done.5), kind=kLoop, calls=%fused_computation.118 | loop fusion | bytes 4096 | tf_op jit(solution)/shard_map/slice | solution.py:123
  21.0 0.6 %add_negate_fusion = f32[10]{0:T(128)} fusion(), kind=kLoop, calls=%fused_computation.104 | loop fusion | flops 20 | bytes 40 | tf_op jit(solution)/shard_map/neg | solution.py:72
  21.6 0.7 %copy-done.6 = s32[16,128]{1,0:T(8,128)S(1)} copy-done((s32[16,128]{1,0:T(8,128)S(1)}, s32[16,128]{1,0:T(8,128)}, u32[]{:S(2)}) %copy-start.6) | copy-done | bytes 8216
  26.2 0.5 %broadcast.176 = f32[]{:T(128)} broadcast(f32[]{:T(128)} %constant.87), dimensions={} | broadcast | bytes 8 | tf_op jit(solution)/shard_map/all_to_all | solution.py:105
  26.7 1.4 %reduce.21 = f32[16,64]{1,0:T(8,128)S(1)} reduce(f32[16,1,64]{2,1,0:T(1,128)} %all-to-all-done, f32[]{:T(128)} %broadcast.176), dimensions={1}, to_apply=%all_to_all.13.reduce_sub_computation.3 | reduce | bytes 8196 | tf_op jit(solution)/shard_map/all_to_all | solution.py:105
  28.6 1.1 %fusion = f32[10,256]{1,0:T(8,128)S(1)} fusion(pred[16,256]{1,0:T(8,128)(4,1)S(1)} %get-tuple-element.43, s32[256]{0:T(256)S(1)} %get-tuple-element.41, f32[50,16,128]{2,1,0:T(8,128)} %param.15, f32[50,16,128]{2,1,0:T(8,128)S(1)} %copy-done), kind=kOutput, calls=%fused_computation.3 | convolution fusion | flops 11724288 | bytes 834560 | tf_op jit(solution)/shard_map/dot_general | solution.py:110
  29.8 0.6 %copy-done.13 = f32[10]{0:T(128)S(1)} copy-done((f32[10]{0:T(128)S(1)}, f32[10]{0:T(128)}, u32[]{:S(2)}) %copy-start.13) | copy-done | bytes 64
  30.8 0.7 %all_to_all.16 = bf16[16,1,160]{2,1,0:T(2,128)(2,1)} reshape(bf16[16,10,16]{2,1,0:T(8,128)(2,1)S(1)} %copy.102) | data formatting | bytes 10240 | tf_op jit(solution)/shard_map/all_to_all | solution.py:117
  31.5 5.9 %all-to-all-start.1 = ((bf16[16,1,160]{2,1,0:T(2,128)(2,1)}), bf16[16,1,160]{2,1,0:T(2,128)(2,1)S(1)}, u32[]{:S(2)}, u32[]{:S(2)}) async-start(bf16[16,1,160]{2,1,0:T(2,128)(2,1)} %all_to_all.16), calls=%async_computation.1 | async-start | bytes 32768 | tf_op jit(solution)/shard_map/all_to_all | solution.py:117
  37.5 6.4 %all-to-all-done.1 = bf16[16,1,160]{2,1,0:T(2,128)(2,1)S(1)} async-done(((bf16[16,1,160]{2,1,0:T(2,128)(2,1)}), bf16[16,1,160]{2,1,0:T(2,128)(2,1)S(1)}, u32[]{:S(2)}, u32[]{:S(2)}) %all-to-all-start.1) | async-done | bytes 5152 | tf_op jit(solution)/shard_map/all_to_all | solution.py:117
  44.2 0.5 %copy-done.8 = f32[1,256]{1,0:T(1,128)S(1)} copy-done((f32[1,256]{1,0:T(1,128)S(1)}, f32[1,256]{1,0:T(1,128)}, u32[]{:S(2)}) %copy-start.8) | copy-done | bytes 1048
  45.0 0.6 %fusion.47 = f32[10,256]{1,0:T(8,128)} fusion(f32[10,256]{1,0:T(8,128)S(1)} %fusion.43, f32[9,256]{1,0:T(8,128)S(1)} %get-tuple-element.24, f32[1,256]{1,0:T(1,128)S(1)} %get-tuple-element.26, f32[1,256]{1,0:T(1,128)S(1)} %get-tuple-element.25, f32[9,256]{1,0:T(8,128)S(1)} %get-tuple-element.23, f32[10,256]{1,0:T(8,128)S(1)} %reshape.146), kind=kLoop, calls=%fused_computation.82 | loop fusion | flops 28160 | bytes 51200 | tf_op jit(solution)/shard_map/sub | solution.py:125
  46.0 0.6 %copy-done.4 = f32[50,16,128]{2,1,0:T(8,128)S(1)} copy-done((f32[50,16,128]{2,1,0:T(8,128)S(1)}, f32[50,16,128]{2,1,0:T(8,128)}, u32[]{:S(2)}) %copy-start.4) | copy-done | bytes 409624
  47.0 0.8 %fusion.18 = f32[50,16,128]{2,1,0:T(8,128)S(1)} fusion(f32[50,16,128]{2,1,0:T(8,128)S(1)} %copy-done.3, f32[50,16,128]{2,1,0:T(8,128)S(1)} %copy-done.1, f32[50,16,129]{2,1,0:T(8,128)S(1)} %fusion.3, f32[50,17,128]{2,1,0:T(8,128)S(1)} %fusion.7, f32[1,16,128]{2,1,0:T(8,128)S(1)} %slice.229, f32[49,16,128]{2,1,0:T(8,128)S(1)} %copy-done.2, ...), kind=kLoop, calls=%fused_computation.29 | loop fusion | flops 2969600 | bytes 4096000 | tf_op jit(solution)/shard_map/add | solution.py:130
  48.1 0.8 %pad_maximum_fusion.1 = f32[50,16,128]{2,1,0:T(8,128)} fusion(f32[40,16,128]{2,1,0:T(8,128)S(1)} %slice.238, f32[10,16,128]{2,1,0:T(8,128)S(1)} %fusion.1), kind=kLoop, calls=%fused_computation.35 | loop fusion | flops 102400 | bytes 819200 | tf_op jit(solution)/shard_map/concatenate | solution.py:133
  (93 shorter events, 8.0 us)
Async XLA Ops:
  0.6 1.6 %copy-start = (f32[50,16,128]{2,1,0:T(8,128)S(1)}, f32[50,16,128]{2,1,0:T(8,128)}, u32[]{:S(2)}) copy-start(f32[50,16,128]{2,1,0:T(8,128)} %param.12) | copy-start | bytes 1228804
  3.0 19.3 %collective-permute-start.3 = (f32[2,50,16,1]{1,2,3,0:T(8,128)S(1)}, f32[2,50,16,1]{1,2,3,0:T(8,128)S(1)}, u32[]{:S(2)}, u32[]{:S(2)}) collective-permute-start(f32[2,50,16,1]{1,2,3,0:T(8,128)S(1)} %copy.88), channel_id=1, source_target_pairs={{0,1},{1,0},{2,3},{3,2},{4,5},{5,4},{6,7},{7,6},{8,9},{9,8},{10,11... | collective-permute-start | bytes 19208 | tf_op jit(solution)/shard_map/ppermute | solution.py:21
  6.5 16.3 %collective-permute-start.2 = (f32[2,50,16,1]{1,2,3,0:T(8,128)S(1)}, f32[2,50,16,1]{1,2,3,0:T(8,128)S(1)}, u32[]{:S(2)}, u32[]{:S(2)}) collective-permute-start(f32[2,50,16,1]{1,2,3,0:T(8,128)S(1)} %copy.87), channel_id=1, source_target_pairs={{1,2},{2,1},{5,6},{6,5},{9,10},{10,9},{13,14},{14,13},{17,18},{18,... | collective-permute-start | bytes 19208 | tf_op jit(solution)/shard_map/ppermute | solution.py:22
  7.2 38.4 %collective-permute-start.1 = (f32[2,50,1,128]{3,2,1,0:T(1,128)S(1)}, f32[2,50,1,128]{3,2,1,0:T(1,128)S(1)}, u32[]{:S(2)}, u32[]{:S(2)}) collective-permute-start(f32[2,50,1,128]{3,2,1,0:T(1,128)S(1)} %get-tuple-element.6), channel_id=1, source_target_pairs={{0,4},{4,0},{8,12},{12,8},{16,20},{20,16},{24,28},{28,24},{1,5},{5... | collective-permute-start | bytes 153608 | tf_op jit(solution)/shard_map/ppermute | solution.py:21
  7.3 0.8 %copy-start.9 = (f32[256]{0:T(256)S(1)}, f32[256]{0:T(256)}, u32[]{:S(2)}) copy-start(f32[256]{0:T(256)} %param.22) | copy-start | bytes 3076
  7.4 0.8 %copy-start.10 = (f32[256]{0:T(256)S(1)}, f32[256]{0:T(256)}, u32[]{:S(2)}) copy-start(f32[256]{0:T(256)} %param.21) | copy-start | bytes 3076
  7.4 38.2 %collective-permute-start = (f32[2,50,1,128]{3,2,1,0:T(1,128)S(1)}, f32[2,50,1,128]{3,2,1,0:T(1,128)S(1)}, u32[]{:S(2)}, u32[]{:S(2)}) collective-permute-start(f32[2,50,1,128]{3,2,1,0:T(1,128)S(1)} %broadcast_select_fusion.5), channel_id=1, source_target_pairs={{4,8},{8,4},{12,16},{16,12},{20,24},{24,20},{5,9},{9,5},{13,17},{1... | collective-permute-start | bytes 153608 | tf_op jit(solution)/shard_map/ppermute | solution.py:22
  8.2 0.7 %copy-start.11 = (s32[256]{0:T(256)S(1)}, s32[256]{0:T(256)}, u32[]{:S(2)}) copy-start(s32[256]{0:T(256)} %param.20) | copy-start | bytes 3076
  8.9 0.7 %copy-start.12 = (s32[256]{0:T(256)S(1)}, s32[256]{0:T(256)}, u32[]{:S(2)}) copy-start(s32[256]{0:T(256)} %param.19) | copy-start | bytes 3076
  10.4 15.8 %all-to-all-start = ((f32[16,1,64]{2,1,0:T(1,128)}), f32[16,1,64]{2,1,0:T(1,128)}, u32[]{:S(2)}, u32[]{:S(2)}) async-start(f32[16,1,64]{2,1,0:T(1,128)} %bitcast.11), calls=%async_computation | async-start | bytes 16384 | tf_op jit(solution)/shard_map/all_to_all | solution.py:105
  19.6 0.8 %copy-start.5 = (f32[10,256]{1,0:T(8,128)S(1)}, f32[10,256]{1,0:T(8,128)}, u32[]{:S(2)}) copy-start(f32[10,256]{1,0:T(8,128)} %param.18) | copy-start | bytes 30724
  21.6 0.7 %copy-start.6 = (s32[16,128]{1,0:T(8,128)S(1)}, s32[16,128]{1,0:T(8,128)}, u32[]{:S(2)}) copy-start(s32[16,128]{1,0:T(8,128)} %param.17) | copy-start | bytes 24580
  28.6 1.1 %copy-start.14 = (f32[8]{0:T(128)S(1)}, f32[8]{0:T(128)}, u32[]{:S(2)}) copy-start(f32[8]{0:T(128)} %param.23) | copy-start | bytes 100
  29.7 0.7 %copy-start.13 = (f32[10]{0:T(128)S(1)}, f32[10]{0:T(128)}, u32[]{:S(2)}) copy-start(f32[10]{0:T(128)} %add_negate_fusion) | copy-start | bytes 124
  31.5 12.4 %all-to-all-start.1 = ((bf16[16,1,160]{2,1,0:T(2,128)(2,1)}), bf16[16,1,160]{2,1,0:T(2,128)(2,1)S(1)}, u32[]{:S(2)}, u32[]{:S(2)}) async-start(bf16[16,1,160]{2,1,0:T(2,128)(2,1)} %all_to_all.16), calls=%async_computation.1 | async-start | bytes 32768 | tf_op jit(solution)/shard_map/all_to_all | solution.py:117
  44.1 0.7 %copy-start.8 = (f32[1,256]{1,0:T(1,128)S(1)}, f32[1,256]{1,0:T(1,128)}, u32[]{:S(2)}) copy-start(f32[1,256]{1,0:T(1,128)} %get-tuple-element.40) | copy-start | bytes 3076
  44.2 0.7 %copy-start.7 = (f32[1,256]{1,0:T(1,128)S(1)}, f32[1,256]{1,0:T(1,128)}, u32[]{:S(2)}) copy-start(f32[1,256]{1,0:T(1,128)} %get-tuple-element.39) | copy-start | bytes 3076
  45.6 1.0 %copy-start.4 = (f32[50,16,128]{2,1,0:T(8,128)S(1)}, f32[50,16,128]{2,1,0:T(8,128)}, u32[]{:S(2)}) copy-start(f32[50,16,128]{2,1,0:T(8,128)} %param.13) | copy-start | bytes 1228804
  45.7 1.0 %copy-start.1 = (f32[50,16,128]{2,1,0:T(8,128)S(1)}, f32[50,16,128]{2,1,0:T(8,128)}, u32[]{:S(2)}) copy-start(f32[50,16,128]{2,1,0:T(8,128)} %param.15) | copy-start | bytes 1228804
  45.8 1.2 %copy-start.2 = (f32[49,16,128]{2,1,0:T(8,128)S(1)}, f32[49,16,128]{2,1,0:T(8,128)}, u32[]{:S(2)}) copy-start(f32[49,16,128]{2,1,0:T(8,128)} %fusion.22) | copy-start | bytes 1204228
  45.8 1.3 %copy-start.3 = (f32[50,16,128]{2,1,0:T(8,128)S(1)}, f32[50,16,128]{2,1,0:T(8,128)}, u32[]{:S(2)}) copy-start(f32[50,16,128]{2,1,0:T(8,128)} %param.16) | copy-start | bytes 1228804

commit v2 on v0

v2 whole, which is shorter than its diff:
```python
import functools

import jax
import jax.numpy as jnp
from jax import lax
from jax.experimental import pallas as pl
from jax.experimental.pallas import tpu as pltpu
from jax.sharding import PartitionSpec as P

NSUB = 4
LANES = 128
CHUNK = 10
VMEM_LIMIT = 48 * 1024 * 1024


def call(body, outs, name, smem=(), count=0, flops=100000, exps=0):
    specs = [
        pl.BlockSpec(memory_space=pltpu.SMEM if i in smem else pltpu.VMEM) for i in range(count)
    ]
    return pl.pallas_call(
        body,
        out_shape=outs,
        in_specs=specs,
        name=name,
        compiler_params=pltpu.CompilerParams(vmem_limit_bytes=VMEM_LIMIT),
        cost_estimate=pl.CostEstimate(flops=flops, bytes_accessed=1000000, transcendentals=exps),
    )


def iota(shape, dim):
    return lax.broadcasted_iota(jnp.int32, shape, dim)


def saturation(head, alpha_field):
    suction = jnp.maximum(-head, 0.0) + jnp.log1p(jnp.exp(-jnp.abs(head)))
    scaled = alpha_field * suction
    return lax.rsqrt(1.0 + scaled * scaled)


def join_blocks(rows, per_block, slot):
    height = LANES // per_block
    if slot:
        rows = pltpu.roll(rows, LANES - slot * per_block, 1)
    moved = pltpu.roll(rows, 0, 1, stride=per_block, stride_axis=0)
    own = iota((height, LANES), 1) // per_block == iota((height, LANES), 0)
    return jnp.sum(jnp.where(own, moved, 0.0), axis=0, keepdims=True)


def pack_kernel(per_block, column, crop, weight, rain, out):
    height = LANES // per_block
    for h in range(column.shape[0]):
        rows = [ref[h : h + 1, :].astype(jnp.float32) for ref in (column, crop, weight, rain)]
        rows.append(jnp.zeros((height - len(rows), LANES), jnp.float32))
        rows = jnp.concatenate(rows, axis=0)
        for j in range(height):
            out[h * height + j : h * height + j + 1, :] = join_blocks(rows, per_block, j)


def even_place(axes):
    index = 0
    for axis in axes:
        index = index * lax.axis_size(axis) + lax.axis_index(axis)
    return index % 2 == 0


def wet_kernel(top, axes_x, axes_y, pressure, alpha, conductivity, sat, conduct, wet_out, *sends):
    x_first, x_second, y_first, y_second = sends
    layers, width_x, width_y = pressure.shape
    for start in range(0, layers, CHUNK):
        part = slice(start, min(layers, start + CHUNK))
        wet = saturation(pressure[part], alpha[part])
        conduct[part] = conductivity[part] * wet * wet * wet
        wet_out[part] = wet
        if part.start < top:
            stop = min(part.stop, top)
            kept = wet[: stop - part.start].reshape((stop - part.start) * width_x, width_y)
            sat[part.start * width_x : stop * width_x, :] = kept.astype(jnp.bfloat16)
    even = even_place(axes_x)
    for field, ref in enumerate((pressure, conduct)):
        rows = slice(field * layers, (field + 1) * layers)
        low, high = ref[:, 0, :], ref[:, width_x - 1, :]
        x_first[rows, :] = jnp.where(even, high, low)
        x_second[rows, :] = jnp.where(even, low, high)
    even = even_place(axes_y)
    lane = iota((width_x, width_y), 1)
    low = jnp.zeros((width_x, width_y), jnp.float32)
    high = jnp.zeros((width_x, width_y), jnp.float32)
    for field, ref in enumerate((pressure, conduct)):
        for k in range(layers):
            place = field * layers + k
            value = ref[k]
            low = jnp.where(lane == place, pltpu.roll(value, place, 1), low)
            high = jnp.where(lane == place, pltpu.roll(value, (place + 1) % width_y, 1), high)
    y_first[...] = jnp.where(even, high, low)
    y_second[...] = jnp.where(even, low, high)


def hot(ids, size):
    return iota((size, LANES), 0) == ids


def pick_kernel(per_block, top, width_x, got, sat, back, patch_sat):
    height = LANES // per_block
    width_y = sat.shape[1]
    for h in range(got.shape[0] // height):
        rows = slice(h * height, (h + 1) * height)
        ids = join_blocks(got[rows, :], per_block, 0).astype(jnp.int32)
        lane_hot = hot(lax.rem(ids, width_y), width_y).astype(jnp.float32).astype(jnp.bfloat16)
        row_hot = hot(lax.div(ids, width_y), width_x)
        picked = jnp.dot(sat[...], lane_hot, preferred_element_type=jnp.float32)
        patch_sat[h] = jnp.zeros(patch_sat.shape[1:], jnp.float32)
        for k in range(top):
            one = picked[k * width_x : (k + 1) * width_x]
            patch_sat[h, k : k + 1, :] = jnp.sum(
                jnp.where(row_hot, one, 0.0), axis=0, keepdims=True
            )
        for i in range(back.shape[1] // LANES):
            block = patch_sat[h, i * height : (i + 1) * height, :]
            for j in range(height):
                row = slice(h * height + j, h * height + j + 1)
                back[row, i * LANES : (i + 1) * LANES] = join_blocks(block, per_block, j)


def column_sources(per_block, top, width_x, width_y, got, patch_sat, root_decay):
    height = LANES // per_block
    total = jnp.zeros((top * width_x, width_y), jnp.float32)
    for h in range(got.shape[0] // height):
        rows = got[h * height : (h + 1) * height, :]
        ids, crop, weight, rain = (join_blocks(rows, per_block, slot) for slot in range(4))
        ids = ids.astype(jnp.int32)
        crop = crop.astype(jnp.int32)
        decay = jnp.zeros((1, LANES), jnp.float32)
        for kind in range(root_decay.shape[0]):
            decay = jnp.where(crop == kind, root_decay[kind], decay)
        level = iota((top, LANES), 0)
        profile = jnp.exp(-(level.astype(jnp.float32) + 0.5) * decay)
        profile = profile / jnp.sum(profile, axis=0, keepdims=True)
        sat = patch_sat[h][:top]
        inflow = jnp.where(level == 0, rain * (1.0 - sat), 0.0)
        sources = inflow - weight * profile * sat
        lane_hot = hot(lax.rem(ids, width_y), width_y).astype(jnp.float32)
        row_hot = hot(lax.div(ids, width_y), width_x)
        spread = jnp.concatenate(
            [jnp.where(row_hot, sources[k : k + 1], 0.0) for k in range(top)], axis=0
        )
        total = total + lax.dot_general(
            spread,
            lane_hot,
            (((1,), (1,)), ((), ())),
            precision=lax.Precision.HIGHEST,
            preferred_element_type=jnp.float32,
        )
    return total


def balance_kernel(per_block, top, axes_x, axes_y, *refs):
    pressure, pressure_old, alpha, porosity, conduct, wet = refs[:6]
    got, patch_sat, root_decay, land = refs[6:10]
    x_sent, x_got, y_sent, y_got = refs[10:12], refs[12:14], refs[14:16], refs[16:18]
    out, x_faces = refs[18:]
    layers, width_x, width_y = pressure.shape
    sources = column_sources(per_block, top, width_x, width_y, got, patch_sat, root_decay)
    sources = sources.reshape(top, width_x, width_y) * land[...].astype(jnp.float32)[None]

    def sides(even, sent, got):
        low, high = jnp.where(even, sent[1], sent[0]), jnp.where(even, sent[0], sent[1])
        before, after = jnp.where(even, got[1], got[0]), jnp.where(even, got[0], got[1])
        return low, high, before, after

    even = even_place(axes_x)
    heads = sides(even, [r[:layers, :] for r in x_sent], [r[:layers, :] for r in x_got])
    conds = sides(even, [r[layers:, :] for r in x_sent], [r[layers:, :] for r in x_got])
    x_faces[0] = 0.5 * (conds[2] + conds[0]) * (heads[2] - heads[0])
    x_faces[1] = 0.5 * (conds[1] + conds[3]) * (heads[1] - heads[3])
    even = even_place(axes_y)
    heads = sides(even, [r[...] for r in y_sent], [r[...] for r in y_got])
    conds = [pltpu.roll(v, width_y - layers, 1) for v in heads]
    y_before = 0.5 * (conds[2] + conds[0]) * (heads[2] - heads[0])
    y_after = 0.5 * (conds[1] + conds[3]) * (heads[1] - heads[3])

    for start in range(0, layers, CHUNK):
        stop = min(layers, start + CHUNK)
        shape = (stop - start, width_x, width_y)
        head, cond = pressure[start:stop], conduct[start:stop]
        row, lane = iota(shape, 1), iota(shape, 2)
        wet_old = saturation(pressure_old[start:stop], alpha[start:stop])
        total = porosity[start:stop] * (wet[start:stop] - wet_old)
        for axis, place, size in ((1, row, width_x), (2, lane, width_y)):
            face = (
                0.5
                * (cond + pltpu.roll(cond, size - 1, axis))
                * (head - pltpu.roll(head, size - 1, axis))
            )
            face = jnp.where(place == size - 1, 0.0, face)
            total = total + (face - pltpu.roll(face, 1, axis))
        below = min(layers, stop + 1)
        head, cond = pressure[max(0, start - 1) : below], conduct[max(0, start - 1) : below]
        down = 0.5 * (cond[:-1] + cond[1:]) * (head[:-1] - head[1:] + 1.0)
        if start == 0:
            down = jnp.concatenate([jnp.zeros_like(cond[:1]), down], 0)
        if stop == layers:
            down = jnp.concatenate([down, cond[-1:]], 0)
        total = total + (down[1:] - down[:-1])
        row, lane = row[0], lane[0]
        for k in range(start, stop):
            edge = jnp.where(row == 0, -x_faces[0, k : k + 1, :], 0.0)
            edge = edge + jnp.where(row == width_x - 1, x_faces[1, k : k + 1, :], 0.0)
            low = pltpu.roll(y_before, (width_y - k) % width_y, 1)
            high = pltpu.roll(y_after, (width_y - 1 - k) % width_y, 1)
            edge = edge - jnp.where(lane == 0, low, 0.0) + jnp.where(lane == width_y - 1, high, 0.0)
            one = total[k - start] + edge
            out[k] = one - sources[k] if k < top else one


def nitrate_kernel(per_block, back, nitrate, out, sat):
    height = LANES // per_block
    top = nitrate.shape[0]
    for h in range(back.shape[0] // height):
        rows = slice(h * height, (h + 1) * height)
        lanes = slice(h * LANES, (h + 1) * LANES)
        for k in range(top):
            where, slot = divmod(k, height)
            block = back[rows, where * LANES : (where + 1) * LANES]
            sat[k : k + 1, :] = join_blocks(block, per_block, slot)
        loss = 0.3 * sat[...] * sat[...]
        value = nitrate[:, lanes]
        for _ in range(NSUB):
            upper = jnp.concatenate([value[:1], value[:-1]], 0)
            lower = jnp.concatenate([value[1:], value[-1:]], 0)
            value = value + 0.2 * (upper + lower - 2.0 * value) - loss * value
        out[:, lanes] = value


def swap_pairs(size, first):
    pairs = []
    for i in range(first, size - 1, 2):
        pairs += [(i, i + 1), (i + 1, i)]
    return pairs


def per_device(
    pressure,
    pressure_old,
    conductivity,
    vg_alpha,
    porosity,
    land_mask,
    nitrate,
    patch_column,
    crop_type,
    patch_weight,
    rain,
    root_decay,
):
    layers, width_x, width_y = pressure.shape
    top, slots = nitrate.shape
    group, axes_x, axes_y = ("gx", "gy"), ("sec", "gx"), ("gy",)
    owners = lax.axis_size(group)
    per_block = slots // owners
    if LANES % per_block or slots % LANES or 4 * per_block >= LANES:
        raise ValueError("block size")
    if width_y != LANES or width_x % 8 or 2 * layers > LANES:
        raise ValueError("grid size")
    height = LANES // per_block
    f32 = jnp.float32
    shape = jax.ShapeDtypeStruct
    field = shape((layers, width_x, width_y), f32)

    flat = [v.reshape(slots // LANES, LANES) for v in (patch_column, crop_type, patch_weight, rain)]
    sent = call(
        functools.partial(pack_kernel, per_block), shape((owners, LANES), f32), "pack", count=4
    )(*flat)
    got = lax.all_to_all(sent, group, split_axis=0, concat_axis=0, tiled=True)

    x_edge, y_edge = shape((2 * layers, width_y), f32), shape((width_x, width_y), f32)
    sat, conduct, wet, *edges = call(
        functools.partial(wet_kernel, top, axes_x, axes_y),
        (shape((top * width_x, width_y), jnp.bfloat16), field, field, x_edge, x_edge, y_edge, y_edge),
        "wet",
        count=3,
        exps=500000,
    )(pressure, vg_alpha, conductivity)

    x_size, y_size = lax.axis_size(axes_x), lax.axis_size(axes_y)
    x_got = [lax.ppermute(edges[i], axes_x, swap_pairs(x_size, i)) for i in (0, 1)]
    y_got = [lax.ppermute(edges[2 + i], axes_y, swap_pairs(y_size, i)) for i in (0, 1)]

    wide = -(-top // height) * LANES
    back, patch_sat = call(
        functools.partial(pick_kernel, per_block, top, width_x),
        (shape((owners, wide), f32), shape((slots // LANES, wide * height // LANES, LANES), f32)),
        "pick",
        count=2,
    )(got, sat)
    back = lax.all_to_all(back, group, split_axis=0, concat_axis=0, tiled=True)

    operands = [pressure, pressure_old, vg_alpha, porosity, conduct, wet, got, patch_sat]
    operands += [root_decay, land_mask, *edges[:2], *x_got, *edges[2:], *y_got]
    residual = pl.pallas_call(
        functools.partial(balance_kernel, per_block, top, axes_x, axes_y),
        out_shape=field,
        in_specs=[
            pl.BlockSpec(memory_space=pltpu.SMEM if i == 8 else pltpu.VMEM)
            for i in range(len(operands))
        ],
        scratch_shapes=[pltpu.VMEM((2, layers, width_y), f32)],
        name="balance",
        compiler_params=pltpu.CompilerParams(vmem_limit_bytes=VMEM_LIMIT),
        cost_estimate=pl.CostEstimate(flops=5000000, bytes_accessed=3000000, transcendentals=200000),
    )(*operands)
    nitrate_out = pl.pallas_call(
        functools.partial(nitrate_kernel, per_block),
        out_shape=shape((top, slots), f32),
        in_specs=[pl.BlockSpec(memory_space=pltpu.VMEM)] * 2,
        scratch_shapes=[pltpu.VMEM((top, LANES), f32)],
        name="nitrate",
        compiler_params=pltpu.CompilerParams(vmem_limit_bytes=VMEM_LIMIT),
    )(back, nitrate)
    return (residual, nitrate_out)


def solution(mesh):
    placed = (
        P(None, ("sec", "gx"), "gy"),
        P(None, ("sec", "gx"), "gy"),
        P(None, ("sec", "gx"), "gy"),
        P(None, ("sec", "gx"), "gy"),
        P(None, ("sec", "gx"), "gy"),
        P(("sec", "gx"), "gy"),
        P(None, ("sec", "gx", "gy")),
        P(("sec", "gx", "gy")),
        P(("sec", "gx", "gy")),
        P(("sec", "gx", "gy")),
        P(("sec", "gx", "gy")),
        P(),
    )
    return jax.shard_map(
        per_device,
        mesh=mesh,
        in_specs=placed,
        out_specs=(P(None, ("sec", "gx"), "gy"), P(None, ("sec", "gx", "gy"))),
        check_vma=False,
    )
```

time: 240 us -> 38.1 us (0.16)
  blocking collectives: 190 us -> 15.5 us
  starting transfers between devices: 23.2 us -> 7.25 us
  other arithmetic: 9.55 us -> 0 us
  local copies, waits for them, and re-layouts: 15 us -> 5.91 us
  Pallas kernels: 0 us -> 4.37 us
  waiting for transfers between devices: 0.02 us -> 3.79 us
    all_gather x1 -> x0, blocking collectives: 190 us -> none  [per_device(): whole = lax.all_gather(sat_top, ('gx', 'gy'), axis=1, tiled=True)]
    all_to_all x0 -> x1, blocking collectives: none -> 15.5 us  [per_device(): got = lax.all_to_all(sent, group, split_axis=0, concat_axis=0, tiled=True)]
    all_to_all x2 -> x1, starting transfers between devices: 12.5 us -> 3.49 us  [per_device(): back = lax.all_to_all(back, group, split_axis=0, concat_axis=0, tiled=True)]
    ppermute x4, starting transfers between devices: 10.7 us -> 3.76 us  [the longest x2 2.59 us: per_device(): lax.ppermute(edges[2 + i], axes_y, swap_pairs(y_size, i))]
    gather x2 -> x0, local copies, waits for them, and re-layouts: 5.28 us -> none  [per_device(): patch_sat = jnp.take(whole, offsets + patch_column, axis=1)]
    pallas_call x0 -> x5, Pallas kernels: none -> 4.37 us  [the longest x1 2.37 us: per_device(): pl.pallas_call(functools.partial(balance_kernel, per_block, top, axes_x,...]
    mul x4 -> x0, other arithmetic: 3.86 us -> none  [the longest x1 1.84 us: per_device(): conduct = conductivity * wet * wet * wet]
    all_to_all x2 -> x1, waiting for transfers between devices: 0.01 us -> 3.78 us  [per_device(): back = lax.all_to_all(back, group, split_axis=0, concat_axis=0, tiled=True)]
  transfers between devices with their start and end apart: 6 -> 5, of which waited for: 0 -> 1; matrix products, arithmetic and copies ran while one was open for 6% -> 2% of each run, Pallas kernels for 0% -> 4%
where the time goes in v2:
time: 38.1 us; the launch traced here: 37.6 us
  blocking collectives  15.5 us (41%)
  starting transfers between devices  7.25 us (19%)
  local copies, waits for them, and re-layouts  5.91 us (16%)
  Pallas kernels  4.37 us (11%)
  waiting for transfers between devices  3.79 us (10%)
  between operations  0.8 us (2%)
    all_to_all x1, blocking collectives, per_device(): got = lax.all_to_all(sent, group, split_axis=0, concat_axis=0, tiled=True)  15.5 us
    unnamed x29, local copies, waits for them, and re-layouts  5.29 us
    all_to_all x1, waiting for transfers between devices, per_device(): back = lax.all_to_all(back, group, split_axis=0, concat_axis=0, tiled=True)  3.78 us
    all_to_all x1, starting transfers between devices, per_device(): back = lax.all_to_all(back, group, split_axis=0, concat_axis=0, tiled=True)  3.49 us
    ppermute x2, starting transfers between devices, per_device(): lax.ppermute(edges[2 + i], axes_y, swap_pairs(y_size, i))  2.59 us
    pallas_call x1, Pallas kernels, per_device(): pl.pallas_call(functools.partial(balance_kernel, per_block, top, axes_x,...  2.37 us
    ppermute x2, starting transfers between devices, per_device(): lax.ppermute(edges[i], axes_x, swap_pairs(x_size, i))  1.17 us
    pallas_call x1, Pallas kernels, per_device(): pl.pallas_call(functools.partial(nitrate_kernel, per_block), out_shape=sh...  0.8 us
  transfers between devices with their start and end apart: 5, of which 1 were waited for; matrix products, arithmetic and copies ran while one was open for 2% of the time, Pallas kernels for 4%

profile of v2, /device:TPU:0, one launch (start us, length us, event | category | flops | bytes accessed | tf_op | source)
XLA Modules:
  0.0 37.6 jit_solution(90349634364762542)
XLA Ops:
  0.6 1.0 %copy-done = f32[50,16,128]{2,1,0:T(8,128)S(1)} copy-done((f32[50,16,128]{2,1,0:T(8,128)S(1)}, f32[50,16,128]{2,1,0:T(8,128)}, u32[]{:S(2)}) %copy-start) | copy-done | bytes 409624
  1.6 1.0 %copy-done.2 = f32[50,16,128]{2,1,0:T(8,128)S(1)} copy-done((f32[50,16,128]{2,1,0:T(8,128)S(1)}, f32[50,16,128]{2,1,0:T(8,128)}, u32[]{:S(2)}) %copy-start.2) | copy-done | bytes 409624
  2.6 1.0 %copy-done.4 = f32[50,16,128]{2,1,0:T(8,128)S(1)} copy-done((f32[50,16,128]{2,1,0:T(8,128)S(1)}, f32[50,16,128]{2,1,0:T(8,128)}, u32[]{:S(2)}) %copy-start.4) | copy-done | bytes 409624
  3.7 0.6 %wet.1 = (bf16[160,128]{1,0:T(8,128)(2,1)S(1)}, f32[50,16,128]{2,1,0:T(8,128)S(1)}, f32[50,16,128]{2,1,0:T(8,128)S(1)}, f32[100,128]{1,0:T(8,128)S(1)}, f32[100,...) custom-call(f32[50,16,128]{2,1,0:T(8,128)S(1)} %copy-done, f32[50,16,128]{2,1,0:T(8,128)S(1)} %copy-done.2, ...), custom_call_target="tpu_custom_call" | custom-call | flops 100000 | bytes 1000000 | tf_op jit(solution)/shard_map/wet/pallas_call | solution.py:276
  4.3 0.5 %collective-permute-start = (f32[100,128]{1,0:T(8,128)S(1)}, f32[100,128]{1,0:T(8,128)S(1)}, u32[]{:S(2)}, u32[]{:S(2)}) collective-permute-start(f32[100,128]{1,0:T(8,128)S(1)} %get-tuple-element.15.refs_10_), channel_id=1, source_target_pairs={{0,4},{4,0},{8,12},{12,8},{16,20},{20,16},{24,28},{28,24},{1,5},{5... | collective-permute-start | bytes 153608 | tf_op jit(solution)/shard_map/ppermute | solution.py:285
  4.8 0.7 %collective-permute-start.1 = (f32[100,128]{1,0:T(8,128)S(1)}, f32[100,128]{1,0:T(8,128)S(1)}, u32[]{:S(2)}, u32[]{:S(2)}) collective-permute-start(f32[100,128]{1,0:T(8,128)S(1)} %get-tuple-element.16.refs_11_), channel_id=1, source_target_pairs={{4,8},{8,4},{12,16},{16,12},{20,24},{24,20},{5,9},{9,5},{13,17},{1... | collective-permute-start | bytes 153608 | tf_op jit(solution)/shard_map/ppermute | solution.py:285
  5.5 0.0 copy-start.9
  5.5 0.6 %copy-done.9 = s32[256]{0:T(256)S(1)} copy-done((s32[256]{0:T(256)S(1)}, s32[256]{0:T(256)}, u32[]{:S(2)}) %copy-start.9) | copy-done | bytes 1048
  6.2 0.2 pack.1
  6.3 15.5 %all_to_all.22 = f32[16,1,128]{2,1,0:T(1,128)S(1)} all-to-all(f32[16,1,128]{2,1,0:T(1,128)S(1)} %bitcast.15), channel_id=1, replica_groups=mesh['sec'=2,'gx'=4,'gy'=4] {'gx','gy'}, dimensions={0} | all-to-all | bytes 16384 | tf_op jit(solution)/shard_map/all_to_all | solution.py:273
  21.9 0.4 %pick.1 = (f32[16,256]{1,0:T(8,128)S(1)}, f32[2,16,128]{2,1,0:T(8,128)S(1)}) custom-call(f32[16,128]{1,0:T(8,128)S(1)} %bitcast.12, bf16[160,128]{1,0:T(8,128)(2,1)S(1)} %get-tuple-element.13.sat), custom_call_target="tpu_custom_call" | custom-call | flops 100000 | bytes 1000000 | tf_op jit(solution)/shard_map/pick/pallas_call | solution.py:289
  22.3 0.6 %copy.15 = f32[16,1,256]{2,1,0:T(1,128)} copy(f32[16,1,256]{2,0,1:T(8,128)S(1)} %bitcast.16) | data formatting | bytes 32768 | tf_op jit(solution)/shard_map/all_to_all | solution.py:295
  22.9 3.5 %all-to-all-start.1 = ((f32[16,1,256]{2,1,0:T(1,128)}), f32[16,1,256]{2,1,0:T(1,128)S(1)}, u32[]{:S(2)}, u32[]{:S(2)}) async-start(f32[16,1,256]{2,1,0:T(1,128)} %copy.15), calls=%async_computation.1 | async-start | bytes 32768 | tf_op jit(solution)/shard_map/all_to_all | solution.py:295
  26.4 1.8 %collective-permute-start.2 = (f32[16,128]{1,0:T(8,128)S(1)}, f32[16,128]{1,0:T(8,128)S(1)}, u32[]{:S(2)}, u32[]{:S(2)}) collective-permute-start(f32[16,128]{1,0:T(8,128)S(1)} %get-tuple-element.17.refs_14_), channel_id=1, source_target_pairs={{0,1},{1,0},{2,3},{3,2},{4,5},{5,4},{6,7},{7,6},{8,9},{9,8},{10,11... | collective-permute-start | bytes 24584 | tf_op jit(solution)/shard_map/ppermute | solution.py:286
  28.2 0.8 %collective-permute-start.3 = (f32[16,128]{1,0:T(8,128)S(1)}, f32[16,128]{1,0:T(8,128)S(1)}, u32[]{:S(2)}, u32[]{:S(2)}) collective-permute-start(f32[16,128]{1,0:T(8,128)S(1)} %get-tuple-element.18.refs_15_), channel_id=1, source_target_pairs={{1,2},{2,1},{5,6},{6,5},{9,10},{10,9},{13,14},{14,13},{17,18},{18,... | collective-permute-start | bytes 24584 | tf_op jit(solution)/shard_map/ppermute | solution.py:286
  29.0 3.8 %all-to-all-done.1 = f32[16,1,256]{2,1,0:T(1,128)S(1)} async-done(((f32[16,1,256]{2,1,0:T(1,128)}), f32[16,1,256]{2,1,0:T(1,128)S(1)}, u32[]{:S(2)}, u32[]{:S(2)}) %all-to-all-start.1) | async-done | bytes 16416 | tf_op jit(solution)/shard_map/all_to_all | solution.py:295
  32.8 0.8 %nitrate.2 = f32[10,256]{1,0:T(8,128)} custom-call(f32[16,256]{1,0:T(8,128)S(1)} %bitcast.14, f32[10,256]{1,0:T(8,128)S(1)} %copy-done.7), custom_call_target="tpu_custom_call" | custom-call | tf_op jit(solution)/shard_map/nitrate/pallas_call | solution.py:311
  33.6 0.0 collective-permute-done.2.refs_16_
  33.6 0.0 collective-permute-done.3.refs_17_
  33.6 0.0 collective-permute-done.refs_12_
  33.6 0.0 copy-start.13
  33.7 0.6 %copy-done.13 = f32[8]{0:T(128)S(1)} copy-done((f32[8]{0:T(128)S(1)}, f32[8]{0:T(128)}, u32[]{:S(2)}) %copy-start.13) | copy-done | bytes 56
  34.3 1.0 %copy-done.6 = f32[50,16,128]{2,1,0:T(8,128)S(1)} copy-done((f32[50,16,128]{2,1,0:T(8,128)S(1)}, f32[50,16,128]{2,1,0:T(8,128)}, u32[]{:S(2)}) %copy-start.6) | copy-done | bytes 409624
  35.3 2.4 %balance.1 = f32[50,16,128]{2,1,0:T(8,128)} custom-call(f32[50,16,128]{2,1,0:T(8,128)S(1)} %copy-done.1, f32[50,16,128]{2,1,0:T(8,128)S(1)} %copy-done.5, f32[50,16,128]{2,1,0:T(8,128)S(1)} %copy-done.3, f32[50,16,128]{2,1,0:T(8,128)S(1)} %copy-done.6, f32[50,16,128]{2,1,0:T(8,128)S(1)} %get-tuple-element.11.refs_4_, ...), custom_call_target="tpu_custom_call" | custom-call | flops 5000000 | bytes 3000000 | tf_op jit(solution)/shard_map/balance/pallas_call | solution.py:299
  (22 shorter events, 0.0 us)
Async XLA Ops:
  0.6 1.0 %copy-start = (f32[50,16,128]{2,1,0:T(8,128)S(1)}, f32[50,16,128]{2,1,0:T(8,128)}, u32[]{:S(2)}) copy-start(f32[50,16,128]{2,1,0:T(8,128)} %refs_0_.1) | copy-start | bytes 1228804
  1.6 1.0 %copy-start.2 = (f32[50,16,128]{2,1,0:T(8,128)S(1)}, f32[50,16,128]{2,1,0:T(8,128)}, u32[]{:S(2)}) copy-start(f32[50,16,128]{2,1,0:T(8,128)} %refs_2_.1) | copy-start | bytes 1228804
  2.6 1.0 %copy-start.4 = (f32[50,16,128]{2,1,0:T(8,128)S(1)}, f32[50,16,128]{2,1,0:T(8,128)}, u32[]{:S(2)}) copy-start(f32[50,16,128]{2,1,0:T(8,128)} %conductivity.1) | copy-start | bytes 1228804
  3.6 1.8 %copy-start.10 = (s32[256]{0:T(256)S(1)}, s32[256]{0:T(256)}, u32[]{:S(2)}) copy-start(s32[256]{0:T(256)} %param.20) | copy-start | bytes 3076
  3.6 1.9 %copy-start.11 = (f32[256]{0:T(256)S(1)}, f32[256]{0:T(256)}, u32[]{:S(2)}) copy-start(f32[256]{0:T(256)} %param.21) | copy-start | bytes 3076
  3.6 1.9 %copy-start.12 = (f32[256]{0:T(256)S(1)}, f32[256]{0:T(256)}, u32[]{:S(2)}) copy-start(f32[256]{0:T(256)} %param.22) | copy-start | bytes 3076
  3.6 30.0 %copy-start.1 = (f32[50,16,128]{2,1,0:T(8,128)S(1)}, f32[50,16,128]{2,1,0:T(8,128)}, u32[]{:S(2)}) copy-start(f32[50,16,128]{2,1,0:T(8,128)} %refs_0_.1) | copy-start | bytes 1228804
  3.6 30.0 %copy-start.3 = (f32[50,16,128]{2,1,0:T(8,128)S(1)}, f32[50,16,128]{2,1,0:T(8,128)}, u32[]{:S(2)}) copy-start(f32[50,16,128]{2,1,0:T(8,128)} %refs_2_.1) | copy-start | bytes 1228804
  3.7 30.0 %copy-start.5 = (f32[50,16,128]{2,1,0:T(8,128)S(1)}, f32[50,16,128]{2,1,0:T(8,128)}, u32[]{:S(2)}) copy-start(f32[50,16,128]{2,1,0:T(8,128)} %refs_1_.1) | copy-start | bytes 1228804
  4.3 29.3 %collective-permute-start = (f32[100,128]{1,0:T(8,128)S(1)}, f32[100,128]{1,0:T(8,128)S(1)}, u32[]{:S(2)}, u32[]{:S(2)}) collective-permute-start(f32[100,128]{1,0:T(8,128)S(1)} %get-tuple-element.15.refs_10_), channel_id=1, source_target_pairs={{0,4},{4,0},{8,12},{12,8},{16,20},{20,16},{24,28},{28,24},{1,5},{5... | collective-permute-start | bytes 153608 | tf_op jit(solution)/shard_map/ppermute | solution.py:285
  4.8 28.8 %collective-permute-start.1 = (f32[100,128]{1,0:T(8,128)S(1)}, f32[100,128]{1,0:T(8,128)S(1)}, u32[]{:S(2)}, u32[]{:S(2)}) collective-permute-start(f32[100,128]{1,0:T(8,128)S(1)} %get-tuple-element.16.refs_11_), channel_id=1, source_target_pairs={{4,8},{8,4},{12,16},{16,12},{20,24},{24,20},{5,9},{9,5},{13,17},{1... | collective-permute-start | bytes 153608 | tf_op jit(solution)/shard_map/ppermute | solution.py:285
  5.5 0.7 %copy-start.9 = (s32[256]{0:T(256)S(1)}, s32[256]{0:T(256)}, u32[]{:S(2)}) copy-start(s32[256]{0:T(256)} %param.19) | copy-start | bytes 3076
  22.9 9.9 %all-to-all-start.1 = ((f32[16,1,256]{2,1,0:T(1,128)}), f32[16,1,256]{2,1,0:T(1,128)S(1)}, u32[]{:S(2)}, u32[]{:S(2)}) async-start(f32[16,1,256]{2,1,0:T(1,128)} %copy.15), calls=%async_computation.1 | async-start | bytes 32768 | tf_op jit(solution)/shard_map/all_to_all | solution.py:295
  26.4 7.2 %collective-permute-start.2 = (f32[16,128]{1,0:T(8,128)S(1)}, f32[16,128]{1,0:T(8,128)S(1)}, u32[]{:S(2)}, u32[]{:S(2)}) collective-permute-start(f32[16,128]{1,0:T(8,128)S(1)} %get-tuple-element.17.refs_14_), channel_id=1, source_target_pairs={{0,1},{1,0},{2,3},{3,2},{4,5},{5,4},{6,7},{7,6},{8,9},{9,8},{10,11... | collective-permute-start | bytes 24584 | tf_op jit(solution)/shard_map/ppermute | solution.py:286
  28.2 4.6 %copy-start.7 = (f32[10,256]{1,0:T(8,128)S(1)}, f32[10,256]{1,0:T(8,128)}, u32[]{:S(2)}) copy-start(f32[10,256]{1,0:T(8,128)} %nitrate.3) | copy-start | bytes 30724
  28.2 5.4 %collective-permute-start.3 = (f32[16,128]{1,0:T(8,128)S(1)}, f32[16,128]{1,0:T(8,128)S(1)}, u32[]{:S(2)}, u32[]{:S(2)}) collective-permute-start(f32[16,128]{1,0:T(8,128)S(1)} %get-tuple-element.18.refs_15_), channel_id=1, source_target_pairs={{1,2},{2,1},{5,6},{6,5},{9,10},{10,9},{13,14},{14,13},{17,18},{18,... | collective-permute-start | bytes 24584 | tf_op jit(solution)/shard_map/ppermute | solution.py:286
  32.8 0.9 %copy-start.8 = (s32[16,128]{1,0:T(8,128)S(1)}, s32[16,128]{1,0:T(8,128)}, u32[]{:S(2)}) copy-start(s32[16,128]{1,0:T(8,128)} %refs_9_.1) | copy-start | bytes 24580
  33.6 0.7 %copy-start.13 = (f32[8]{0:T(128)S(1)}, f32[8]{0:T(128)}, u32[]{:S(2)}) copy-start(f32[8]{0:T(128)} %refs_8_.1) | copy-start | bytes 100
  34.3 1.0 %copy-start.6 = (f32[50,16,128]{2,1,0:T(8,128)S(1)}, f32[50,16,128]{2,1,0:T(8,128)}, u32[]{:S(2)}) copy-start(f32[50,16,128]{2,1,0:T(8,128)} %refs_3_.1) | copy-start | bytes 1228804

commit v3 on v2

v3 whole, which is shorter than its diff:
```python
import functools

import jax
import jax.numpy as jnp
from jax import lax
from jax.experimental import pallas as pl
from jax.experimental.pallas import tpu as pltpu
from jax.sharding import PartitionSpec as P

NSUB = 4
LANES = 128
CHUNK = 10
FIELD_LANE = 104
VMEM_LIMIT = 24 * 1024 * 1024


def iota(shape, dim):
    return lax.broadcasted_iota(jnp.int32, shape, dim)


def place_of(axes):
    index = 0
    for axis in axes:
        index = index * lax.axis_size(axis) + lax.axis_index(axis)
    return index


def parts_of(layers):
    return [(i, min(layers, i + CHUNK)) for i in range(0, layers, CHUNK)]


def saturation(head, alpha_field):
    suction = jnp.maximum(-head, 0.0) + jnp.log1p(jnp.exp(-jnp.abs(head)))
    scaled = alpha_field * suction
    return lax.rsqrt(1.0 + scaled * scaled)


def join_blocks(rows, per_block, slot):
    height = LANES // per_block
    if slot:
        rows = pltpu.roll(rows, LANES - slot * per_block, 1)
    moved = pltpu.roll(rows, 0, 1, stride=per_block, stride_axis=0)
    own = iota((height, LANES), 1) // per_block == iota((height, LANES), 0)
    return jnp.sum(jnp.where(own, moved, 0.0), axis=0, keepdims=True)


def front_kernel(per_block, top, axes_x, axes_y, *refs):
    fields, grids = refs[:4], refs[4:7]
    sent, sat, head, alpha, conduct, wet_out, x_first, x_second, y_edges = refs[7:16]
    fields_in, perm, sent_in, small_sems, sems, sent_sem = refs[16:]
    layers, width_x, width_y = head.shape
    height = LANES // per_block
    small = [pltpu.make_async_copy(fields[i], fields_in[i], small_sems.at[i]) for i in range(4)]
    for copy in small:
        copy.start()
    parts = parts_of(layers)
    large = []
    for i, (start, stop) in enumerate(parts):
        rows = pl.ds(start, stop - start)
        for j, (source, target) in enumerate(zip(grids, (head, alpha, perm))):
            copy = pltpu.make_async_copy(source.at[rows], target.at[rows], sems.at[i, j])
            copy.start()
            large.append(copy)
    for copy in small:
        copy.wait()
    for h in range(sent_in.shape[0] // height):
        rows = [ref[h : h + 1, :].astype(jnp.float32) for ref in fields_in]
        rows.append(jnp.zeros((4, LANES), jnp.float32))
        rows = [jnp.zeros((FIELD_LANE, LANES), jnp.float32), jnp.concatenate(rows, axis=0)]
        rows.append(jnp.zeros((LANES - FIELD_LANE - 8, LANES), jnp.float32))
        turned = jnp.concatenate(rows, axis=0).T
        sent_in[h * height : (h + 1) * height] = turned.reshape(height, per_block, LANES)
    lane = iota((width_x, width_y), 1)
    low = jnp.zeros((width_x, width_y), jnp.float32)
    high = jnp.zeros((width_x, width_y), jnp.float32)
    for i, (start, stop) in enumerate(parts):
        for copy in large[3 * i : 3 * i + 3]:
            copy.wait()
        part = slice(start, stop)
        wet = saturation(head[part], alpha[part])
        cond = perm[part] * wet * wet * wet
        conduct[part] = cond
        wet_out[part] = wet
        if start < top:
            last = min(stop, top)
            kept = wet[: last - start].reshape((last - start) * width_x, width_y)
            sat[start * width_x : last * width_x, :] = kept.astype(jnp.bfloat16)
        for first, values in ((0, head[part]), (layers, cond)):
            for k in range(start, stop):
                place = first + k
                value = values[k - start]
                low = jnp.where(lane == place, pltpu.roll(value, place, 1), low)
                high = jnp.where(lane == place, pltpu.roll(value, (place + 1) % width_y, 1), high)
    y_edges[0] = low
    y_edges[1] = high
    y_place, y_size = place_of(axes_y), lax.axis_size(axes_y)
    base = place_of(("gx", "gy"))

    @pl.when(y_place > 0)
    def _():
        sent_in[base - 1] = sent_in[base - 1] + low

    @pl.when(y_place < y_size - 1)
    def _():
        sent_in[base + 1] = sent_in[base + 1] + high

    send = pltpu.make_async_copy(sent_in, sent, sent_sem)
    send.start()
    even = place_of(axes_x) % 2 == 0
    for field, ref in enumerate((head, conduct)):
        rows = slice(field * layers, (field + 1) * layers)
        low, high = ref[:, 0, :], ref[:, width_x - 1, :]
        x_first[rows, :] = jnp.where(even, high, low)
        x_second[rows, :] = jnp.where(even, low, high)
    send.wait()


def hot(ids, size):
    return iota((size, LANES), 0) == ids


def pick_kernel(per_block, top, width_x, got, sat, back, patch_sat, fields):
    height = LANES // per_block
    width_y = sat.shape[1]
    for h in range(got.shape[0] // height):
        turned = got[h * height : (h + 1) * height].reshape(LANES, LANES).T
        rows = turned[FIELD_LANE : FIELD_LANE + 8]
        fields[h] = rows
        ids = rows[0:1].astype(jnp.int32)
        lane_hot = hot(lax.rem(ids, width_y), width_y).astype(jnp.float32).astype(jnp.bfloat16)
        row_hot = hot(lax.div(ids, width_y), width_x)
        picked = jnp.dot(sat[...], lane_hot, preferred_element_type=jnp.float32)
        patch_sat[h] = jnp.zeros(patch_sat.shape[1:], jnp.float32)
        for k in range(top):
            one = picked[k * width_x : (k + 1) * width_x]
            patch_sat[h, k : k + 1, :] = jnp.sum(
                jnp.where(row_hot, one, 0.0), axis=0, keepdims=True
            )
        for i in range(back.shape[1]):
            block = patch_sat[h, i * height : (i + 1) * height, :]
            for j in range(height):
                row = slice(h * height + j, h * height + j + 1)
                back[row, i, :] = join_blocks(block, per_block, j)


def column_sources(top, width_x, width_y, fields, patch_sat, root_decay):
    total = jnp.zeros((top * width_x, width_y), jnp.float32)
    for h in range(fields.shape[0]):
        ids, crop, weight, rain = (fields[h, i : i + 1, :] for i in range(4))
        ids = ids.astype(jnp.int32)
        crop = crop.astype(jnp.int32)
        decay = jnp.zeros((1, LANES), jnp.float32)
        for kind in range(root_decay.shape[0]):
            decay = jnp.where(crop == kind, root_decay[kind], decay)
        level = iota((top, LANES), 0)
        profile = jnp.exp(-(level.astype(jnp.float32) + 0.5) * decay)
        profile = profile / jnp.sum(profile, axis=0, keepdims=True)
        sat = patch_sat[h][:top]
        inflow = jnp.where(level == 0, rain * (1.0 - sat), 0.0)
        sources = inflow - weight * profile * sat
        lane_hot = hot(lax.rem(ids, width_y), width_y).astype(jnp.float32)
        row_hot = hot(lax.div(ids, width_y), width_x)
        spread = jnp.concatenate(
            [jnp.where(row_hot, sources[k : k + 1], 0.0) for k in range(top)], axis=0
        )
        total = total + lax.dot_general(
            spread,
            lane_hot,
            (((1,), (1,)), ((), ())),
            precision=lax.Precision.HIGHEST,
            preferred_element_type=jnp.float32,
        )
    return total


def balance_kernel(top, axes_x, axes_y, *refs):
    grids = refs[:2]
    head, alpha, conduct, wet, got, fields, patch_sat, root_decay, land = refs[2:11]
    x_sent, x_got, y_edges = refs[11:13], refs[13:15], refs[15]
    residual, order = refs[16:18]
    head_old, porosity, out, x_faces, sems, out_sems = refs[18:]
    layers, width_x, width_y = head.shape
    parts = parts_of(layers)
    copies = []
    for i, (start, stop) in enumerate(parts):
        rows = pl.ds(start, stop - start)
        for j, (source, target) in enumerate(zip(grids, (head_old, porosity))):
            copy = pltpu.make_async_copy(source.at[rows], target.at[rows], sems.at[i, j])
            copy.start()
            copies.append(copy)
    order[...] = jnp.zeros(order.shape, order.dtype)
    sources = column_sources(top, width_x, width_y, fields, patch_sat, root_decay)
    sources = sources.reshape(top, width_x, width_y) * land[...].astype(jnp.float32)[None]

    even = place_of(axes_x) % 2 == 0
    faces = []
    for rows in (slice(0, layers), slice(layers, 2 * layers)):
        first, second = (r[rows, :] for r in x_sent)
        low, high = jnp.where(even, second, first), jnp.where(even, first, second)
        first, second = (r[rows, :] for r in x_got)
        before, after = jnp.where(even, second, first), jnp.where(even, first, second)
        faces.append((low, high, before, after))
    heads, conds = faces
    x_faces[0] = 0.5 * (conds[2] + conds[0]) * (heads[2] - heads[0])
    x_faces[1] = 0.5 * (conds[1] + conds[3]) * (heads[1] - heads[3])
    y_place, y_size = place_of(axes_y), lax.axis_size(axes_y)
    base = place_of(("gx", "gy"))
    before = jnp.where(y_place > 0, got[jnp.maximum(base - 1, 0)], 0.0)
    after = jnp.where(y_place < y_size - 1, got[jnp.minimum(base + 1, got.shape[0] - 1)], 0.0)
    heads = (y_edges[0], y_edges[1], before, after)
    conds = [pltpu.roll(v, width_y - layers, 1) for v in heads]
    y_before = 0.5 * (conds[2] + conds[0]) * (heads[2] - heads[0])
    y_after = 0.5 * (conds[1] + conds[3]) * (heads[1] - heads[3])

    writes = []
    for i, (start, stop) in enumerate(parts):
        for copy in copies[2 * i : 2 * i + 2]:
            copy.wait()
        shape = (stop - start, width_x, width_y)
        part, cond = head[start:stop], conduct[start:stop]
        row, lane = iota(shape, 1), iota(shape, 2)
        wet_old = saturation(head_old[start:stop], alpha[start:stop])
        total = porosity[start:stop] * (wet[start:stop] - wet_old)
        for axis, place, size in ((1, row, width_x), (2, lane, width_y)):
            face = (
                0.5
                * (cond + pltpu.roll(cond, size - 1, axis))
                * (part - pltpu.roll(part, size - 1, axis))
            )
            face = jnp.where(place == size - 1, 0.0, face)
            total = total + (face - pltpu.roll(face, 1, axis))
        below = min(layers, stop + 1)
        part, cond = head[max(0, start - 1) : below], conduct[max(0, start - 1) : below]
        down = 0.5 * (cond[:-1] + cond[1:]) * (part[:-1] - part[1:] + 1.0)
        if start == 0:
            down = jnp.concatenate([jnp.zeros_like(cond[:1]), down], 0)
        if stop == layers:
            down = jnp.concatenate([down, cond[-1:]], 0)
        total = total + (down[1:] - down[:-1])
        row, lane = row[0], lane[0]
        for k in range(start, stop):
            edge = jnp.where(row == 0, -x_faces[0, k : k + 1, :], 0.0)
            edge = edge + jnp.where(row == width_x - 1, x_faces[1, k : k + 1, :], 0.0)
            low = pltpu.roll(y_before, (width_y - k) % width_y, 1)
            high = pltpu.roll(y_after, (width_y - 1 - k) % width_y, 1)
            edge = edge - jnp.where(lane == 0, low, 0.0) + jnp.where(lane == width_y - 1, high, 0.0)
            one = total[k - start] + edge
            out[k] = one - sources[k] if k < top else one
        rows = pl.ds(start, stop - start)
        copy = pltpu.make_async_copy(out.at[rows], residual.at[rows], out_sems.at[i])
        copy.start()
        writes.append(copy)
    for copy in writes:
        copy.wait()


def nitrate_kernel(per_block, back, nitrate, order, out, sat):
    height = LANES // per_block
    top = nitrate.shape[0]
    for h in range(back.shape[0] // height):
        rows = slice(h * height, (h + 1) * height)
        lanes = slice(h * LANES, (h + 1) * LANES)
        for k in range(top):
            where, slot = divmod(k, height)
            sat[k : k + 1, :] = join_blocks(back[rows, where, :], per_block, slot)
        loss = 0.3 * sat[...] * sat[...]
        value = nitrate[:, lanes]
        for _ in range(NSUB):
            upper = jnp.concatenate([value[:1], value[:-1]], 0)
            lower = jnp.concatenate([value[1:], value[-1:]], 0)
            value = value + 0.2 * (upper + lower - 2.0 * value) - loss * value
        out[:, lanes] = value


def swap_pairs(size, first):
    pairs = []
    for i in range(first, size - 1, 2):
        pairs += [(i, i + 1), (i + 1, i)]
    return pairs


def call(body, name, ins, outs, scratch=()):
    space = {"V": pltpu.VMEM, "S": pltpu.SMEM, "H": pltpu.HBM}
    return pl.pallas_call(
        body,
        out_shape=tuple(shape for shape, _ in outs),
        in_specs=[pl.BlockSpec(memory_space=space[i]) for i in ins],
        out_specs=tuple(pl.BlockSpec(memory_space=space[i]) for _, i in outs),
        scratch_shapes=scratch,
        name=name,
        compiler_params=pltpu.CompilerParams(vmem_limit_bytes=VMEM_LIMIT),
        cost_estimate=pl.CostEstimate(flops=1000, bytes_accessed=1000, transcendentals=0),
    )


def per_device(
    pressure,
    pressure_old,
    conductivity,
    vg_alpha,
    porosity,
    land_mask,
    nitrate,
    patch_column,
    crop_type,
    patch_weight,
    rain,
    root_decay,
):
    layers, width_x, width_y = pressure.shape
    top, slots = nitrate.shape
    group, axes_x, axes_y = ("gx", "gy"), ("sec", "gx"), ("gy",)
    owners = lax.axis_size(group)
    per_block = slots // owners
    if LANES % per_block or slots % LANES or per_block != width_x:
        raise ValueError("block size")
    if width_y != LANES or width_x % 8 or 2 * layers > FIELD_LANE:
        raise ValueError("grid size")
    height = LANES // per_block
    banks = slots // LANES
    wide = -(-top // height)
    f32 = jnp.float32
    shape, dma = jax.ShapeDtypeStruct, pltpu.SemaphoreType.DMA
    field = shape((layers, width_x, width_y), f32)
    field_in = pltpu.VMEM((layers, width_x, width_y), f32)
    count = len(parts_of(layers))

    flat = [v.reshape(banks, LANES) for v in (patch_column, crop_type, patch_weight, rain)]
    x_edge = shape((2 * layers, width_y), f32)
    sent, sat, head, alpha, conduct, wet, *x_sent, y_edges = call(
        functools.partial(front_kernel, per_block, top, axes_x, axes_y),
        "front",
        "HHHHHHH",
        (
            (shape((owners, per_block, LANES), f32), "H"),
            (shape((top * width_x, width_y), jnp.bfloat16), "V"),
            (field, "V"),
            (field, "V"),
            (field, "V"),
            (field, "V"),
            (x_edge, "V"),
            (x_edge, "V"),
            (shape((2, width_x, width_y), f32), "V"),
        ),
        (
            [pltpu.VMEM((banks, LANES), v.dtype) for v in flat],
            field_in,
            pltpu.VMEM((owners, per_block, LANES), f32),
            dma((4,)),
            dma((count, 3)),
            dma,
        ),
    )(*flat, pressure, vg_alpha, conductivity)
    got = lax.all_to_all(sent, group, split_axis=0, concat_axis=0, tiled=True)

    x_size = lax.axis_size(axes_x)
    x_got = [lax.ppermute(x_sent[i], axes_x, swap_pairs(x_size, i)) for i in (0, 1)]

    back, patch_sat, fields = call(
        functools.partial(pick_kernel, per_block, top, width_x),
        "pick",
        "VV",
        (
            (shape((owners, wide, LANES), f32), "V"),
            (shape((banks, wide * height, LANES), f32), "V"),
            (shape((banks, 8, LANES), f32), "V"),
        ),
    )(got, sat)
    back = lax.all_to_all(back, group, split_axis=0, concat_axis=0, tiled=True)

    residual, order = call(
        functools.partial(balance_kernel, top, axes_x, axes_y),
        "balance",
        "HHVVVVVVVSVVVVVV",
        ((field, "H"), (shape((8, LANES), f32), "V")),
        (
            field_in,
            field_in,
            field_in,
            pltpu.VMEM((2, layers, width_y), f32),
            dma((count, 2)),
            dma((count,)),
        ),
    )(
        pressure_old, porosity, head, alpha, conduct, wet, got, fields, patch_sat,
        root_decay, land_mask, *x_sent, *x_got, y_edges,
    )
    (nitrate_out,) = call(
        functools.partial(nitrate_kernel, per_block),
        "nitrate",
        "VVV",
        ((shape((top, slots), f32), "V"),),
        (pltpu.VMEM((top, LANES), f32),),
    )(back, nitrate, order)
    return (residual, nitrate_out)


def solution(mesh):
    placed = (
        P(None, ("sec", "gx"), "gy"),
        P(None, ("sec", "gx"), "gy"),
        P(None, ("sec", "gx"), "gy"),
        P(None, ("sec", "gx"), "gy"),
        P(None, ("sec", "gx"), "gy"),
        P(("sec", "gx"), "gy"),
        P(None, ("sec", "gx", "gy")),
        P(("sec", "gx", "gy")),
        P(("sec", "gx", "gy")),
        P(("sec", "gx", "gy")),
        P(("sec", "gx", "gy")),
        P(),
    )
    return jax.shard_map(
        per_device,
        mesh=mesh,
        in_specs=placed,
        out_specs=(P(None, ("sec", "gx"), "gy"), P(None, ("sec", "gx", "gy"))),
        check_vma=False,
    )
```

time: 38.1 us -> 34.8 us (0.913)
  blocking collectives: 15.5 us -> 0 us
  Pallas kernels: 4.37 us -> 9.26 us
  starting transfers between devices: 7.25 us -> 12.1 us
  waiting for transfers between devices: 3.79 us -> 7.85 us
  local copies, waits for them, and re-layouts: 5.91 us -> 4.36 us
    all_to_all x1 -> x0, blocking collectives: 15.5 us -> none  [per_device(): got = lax.all_to_all(sent, group, split_axis=0, concat_axis=0, tiled=True)]
    all_to_all x0 -> x1, starting transfers between devices: none -> 7.53 us  [per_device(): got = lax.all_to_all(sent, group, split_axis=0, concat_axis=0, tiled=True)]
    all_to_all x0 -> x1, waiting for transfers between devices: none -> 6.28 us  [per_device(): got = lax.all_to_all(sent, group, split_axis=0, concat_axis=0, tiled=True)]
    pallas_call x5 -> x4, Pallas kernels: 4.37 us -> 9.26 us  [the longest x1 4.09 us: per_device(): call(functools.partial(balance_kernel, top, axes_x, axes_y), 'balance', '...]
    ppermute x4 -> x2, starting transfers between devices: 3.76 us -> 1.06 us  [per_device(): lax.ppermute(x_sent[i], axes_x, swap_pairs(x_size, i))]
    all_to_all x1, waiting for transfers between devices: 3.78 us -> 1.57 us  [per_device(): back = lax.all_to_all(back, group, split_axis=0, concat_axis=0, tiled=True)]
    unnamed x29 -> x24, local copies, waits for them, and re-layouts: 5.29 us -> 4.36 us
    all_to_all x1 -> x0, local copies, waits for them, and re-layouts: 0.62 us -> none  [per_device(): back = lax.all_to_all(back, group, split_axis=0, concat_axis=0, tiled=True)]
  transfers between devices with their start and end apart: 5 -> 4, of which waited for: 1 -> 2; matrix products, arithmetic and copies ran while one was open for 2% -> 0% of each run, Pallas kernels for 4% -> 15%
where the time goes in v3:
time: 34.8 us; the launch traced here: 34.3 us
  starting transfers between devices  12.1 us (35%)
  Pallas kernels  9.26 us (27%)
  waiting for transfers between devices  7.85 us (23%)
  local copies, waits for them, and re-layouts  4.36 us (13%)
  between operations  0.77 us (2%)
    all_to_all x1, starting transfers between devices, per_device(): got = lax.all_to_all(sent, group, split_axis=0, concat_axis=0, tiled=True)  7.53 us
    all_to_all x1, waiting for transfers between devices, per_device(): got = lax.all_to_all(sent, group, split_axis=0, concat_axis=0, tiled=True)  6.28 us
    unnamed x24, local copies, waits for them, and re-layouts  4.36 us
    pallas_call x1, Pallas kernels, per_device(): call(functools.partial(balance_kernel, top, axes_x, axes_y), 'balance', '...  4.09 us
    all_to_all x1, starting transfers between devices, per_device(): back = lax.all_to_all(back, group, split_axis=0, concat_axis=0, tiled=True)  3.49 us
    pallas_call x1, Pallas kernels, per_device(): call(functools.partial(front_kernel, per_block, top, axes_x, axes_y), 'fr...  3.3 us
    all_to_all x1, waiting for transfers between devices, per_device(): back = lax.all_to_all(back, group, split_axis=0, concat_axis=0, tiled=True)  1.57 us
    ppermute x2, starting transfers between devices, per_device(): lax.ppermute(x_sent[i], axes_x, swap_pairs(x_size, i))  1.06 us
  transfers between devices with their start and end apart: 4, of which 2 were waited for; matrix products, arithmetic and copies ran while one was open for 0% of the time, Pallas kernels for 15%

profile of v3, /device:TPU:0, one launch (start us, length us, event | category | flops | bytes accessed | tf_op | source)
XLA Modules:
  0.0 34.3 jit_solution(16800039965833459499)
XLA Ops:
  0.6 0.0 copy-start.10
  0.7 0.6 %copy-done.10 = f32[256]{0:T(256)S(1)} copy-done((f32[256]{0:T(256)S(1)}, f32[256]{0:T(256)}, u32[]{:S(2)}) %copy-start.10) | copy-done | bytes 1048
  1.3 0.0 copy-done.8
  1.3 0.0 copy-done.9
  1.3 0.0 copy-done.7
  1.4 1.0 %copy-done.2 = f32[50,16,128]{2,1,0:T(8,128)S(1)} copy-done((f32[50,16,128]{2,1,0:T(8,128)S(1)}, f32[50,16,128]{2,1,0:T(8,128)}, u32[]{:S(2)}) %copy-start.2) | copy-done | bytes 409624
  2.4 1.0 %copy-done.3 = f32[50,16,128]{2,1,0:T(8,128)S(1)} copy-done((f32[50,16,128]{2,1,0:T(8,128)S(1)}, f32[50,16,128]{2,1,0:T(8,128)}, u32[]{:S(2)}) %copy-start.3) | copy-done | bytes 409624
  3.4 1.0 %copy-done.4 = f32[50,16,128]{2,1,0:T(8,128)S(1)} copy-done((f32[50,16,128]{2,1,0:T(8,128)S(1)}, f32[50,16,128]{2,1,0:T(8,128)}, u32[]{:S(2)}) %copy-start.4) | copy-done | bytes 409624
  4.4 3.3 %front.1 = (f32[16,16,128]{2,1,0:T(8,128)}, bf16[160,128]{1,0:T(8,128)(2,1)S(1)}, f32[50,16,128]{2,1,0:T(8,128)S(1)}, f32[50,16,128]{2,1,0:T(8,128)S(1)}, f32[50...) custom-call(s32[2,128]{1,0:T(2,128)S(1)} %bitcast.4, ...), custom_call_target="tpu_custom_call" | custom-call | flops 1000 | bytes 1000 | tf_op jit(solution)/shard_map/front/pallas_call | solution.py:330
  7.7 0.0 copy-start
  7.7 7.5 %all-to-all-start = ((f32[16,16,128]{2,1,0:T(8,128)}), f32[16,16,128]{2,1,0:T(8,128)S(1)}, u32[]{:S(2)}, u32[]{:S(2)}) async-start(f32[16,16,128]{2,1,0:T(8,128)} %get-tuple-element.20), calls=%async_computation | async-start | bytes 262144 | tf_op jit(solution)/shard_map/all_to_all | solution.py:354
  15.2 0.4 %collective-permute-start = (f32[100,128]{1,0:T(8,128)S(1)}, f32[100,128]{1,0:T(8,128)S(1)}, u32[]{:S(2)}, u32[]{:S(2)}) collective-permute-start(f32[100,128]{1,0:T(8,128)S(1)} %get-tuple-element.24.refs_11_), channel_id=1, source_target_pairs={{0,4},{4,0},{8,12},{12,8},{16,20},{20,16},{24,28},{28,24},{1,5},{5... | collective-permute-start | bytes 153608 | tf_op jit(solution)/shard_map/ppermute | solution.py:357
  15.6 0.7 %collective-permute-start.1 = (f32[100,128]{1,0:T(8,128)S(1)}, f32[100,128]{1,0:T(8,128)S(1)}, u32[]{:S(2)}, u32[]{:S(2)}) collective-permute-start(f32[100,128]{1,0:T(8,128)S(1)} %get-tuple-element.25.refs_12_), channel_id=1, source_target_pairs={{4,8},{8,4},{12,16},{16,12},{20,24},{24,20},{5,9},{9,5},{13,17},{1... | collective-permute-start | bytes 153608 | tf_op jit(solution)/shard_map/ppermute | solution.py:357
  16.3 6.3 %all-to-all-done.got.refs_6_ = f32[16,16,128]{2,1,0:T(8,128)S(1)} async-done(((f32[16,16,128]{2,1,0:T(8,128)}), f32[16,16,128]{2,1,0:T(8,128)S(1)}, u32[]{:S(2)}, u32[]{:S(2)}) %all-to-all-start) | async-done | bytes 131104 | tf_op jit(solution)/shard_map/all_to_all | solution.py:354
  22.6 1.1 %pick.1 = (f32[16,2,128]{2,1,0:T(2,128)}, f32[2,16,128]{2,1,0:T(8,128)S(1)}, f32[2,8,128]{2,1,0:T(8,128)S(1)}) custom-call(f32[16,16,128]{2,1,0:T(8,128)S(1)} %all-to-all-done.got.refs_6_, bf16[160,128]{1,0:T(8,128)(2,1)S(1)} %get-tuple-element.21.sat), custom_call_target="tpu_custom_call" | custom-call | flops 1000 | bytes 1000 | tf_op jit(solution)/shard_map/pick/pallas_call | solution.py:359
  23.6 3.5 %all-to-all-start.1 = ((f32[16,2,128]{2,1,0:T(2,128)}), f32[16,2,128]{2,1,0:T(2,128)S(1)}, u32[]{:S(2)}, u32[]{:S(2)}) async-start(f32[16,2,128]{2,1,0:T(2,128)} %get-tuple-element.28), calls=%async_computation.1 | async-start | bytes 32768 | tf_op jit(solution)/shard_map/all_to_all | solution.py:369
  27.1 0.0 copy-start.6
  27.1 0.0 collective-permute-done.refs_13_
  27.2 0.0 collective-permute-done.1.refs_14_
  27.2 0.0 copy-start.11
  27.2 0.6 %copy-done.6 = s32[16,128]{1,0:T(8,128)S(1)} copy-done((s32[16,128]{1,0:T(8,128)S(1)}, s32[16,128]{1,0:T(8,128)}, u32[]{:S(2)}) %copy-start.6) | copy-done | bytes 8216
  27.8 4.1 %balance.1 = (f32[50,16,128]{2,1,0:T(8,128)}, f32[8,128]{1,0:T(8,128)S(1)}) custom-call(f32[50,16,128]{2,1,0:T(8,128)S(1)} %copy-done, f32[50,16,128]{2,1,0:T(8,128)S(1)} %copy-done.1, f32[50,16,128]{2,1,0:T(8,128)S(1)} %get-tuple-element.16.refs_2_, f32[50,16,128]{2,1,0:T(8,128)S(1)} %get-tuple-element.17.refs_3_, ...), custom_call_target="tpu_custom_call" | custom-call | flops 1000 | bytes 1000 | tf_op jit(solution)/shard_map/balance/pallas_call | solution.py:371
  31.9 1.6 %all-to-all-done.1.back = f32[16,2,128]{2,1,0:T(2,128)S(1)} async-done(((f32[16,2,128]{2,1,0:T(2,128)}), f32[16,2,128]{2,1,0:T(2,128)S(1)}, u32[]{:S(2)}, u32[]{:S(2)}) %all-to-all-start.1) | async-done | bytes 16416 | tf_op jit(solution)/shard_map/all_to_all | solution.py:369
  33.5 0.8 %nitrate.2 = f32[10,256]{1,0:T(8,128)} custom-call(f32[16,2,128]{2,1,0:T(2,128)S(1)} %all-to-all-done.1.back, f32[10,256]{1,0:T(8,128)S(1)} %copy-done.5, f32[8,128]{1,0:T(8,128)S(1)} %get-tuple-element.29.order), custom_call_target="tpu_custom_call" | custom-call | flops 1000 | bytes 1000 | tf_op jit(solution)/shard_map/nitrate/pallas_call | solution.py:388
  (12 shorter events, 0.0 us)
Async XLA Ops:
  0.6 0.7 %copy-start.10 = (f32[256]{0:T(256)S(1)}, f32[256]{0:T(256)}, u32[]{:S(2)}) copy-start(f32[256]{0:T(256)} %param.22) | copy-start | bytes 3076
  0.6 0.7 %copy-start.8 = (s32[256]{0:T(256)S(1)}, s32[256]{0:T(256)}, u32[]{:S(2)}) copy-start(s32[256]{0:T(256)} %param.20) | copy-start | bytes 3076
  0.7 0.7 %copy-start.9 = (f32[256]{0:T(256)S(1)}, f32[256]{0:T(256)}, u32[]{:S(2)}) copy-start(f32[256]{0:T(256)} %param.21) | copy-start | bytes 3076
  0.7 0.7 %copy-start.7 = (s32[256]{0:T(256)S(1)}, s32[256]{0:T(256)}, u32[]{:S(2)}) copy-start(s32[256]{0:T(256)} %param.19) | copy-start | bytes 3076
  1.4 1.0 %copy-start.2 = (f32[50,16,128]{2,1,0:T(8,128)S(1)}, f32[50,16,128]{2,1,0:T(8,128)}, u32[]{:S(2)}) copy-start(f32[50,16,128]{2,1,0:T(8,128)} %refs_4_.1) | copy-start | bytes 1228804
  2.4 1.0 %copy-start.3 = (f32[50,16,128]{2,1,0:T(8,128)S(1)}, f32[50,16,128]{2,1,0:T(8,128)}, u32[]{:S(2)}) copy-start(f32[50,16,128]{2,1,0:T(8,128)} %refs_5_.1) | copy-start | bytes 1228804
  3.4 1.0 %copy-start.4 = (f32[50,16,128]{2,1,0:T(8,128)S(1)}, f32[50,16,128]{2,1,0:T(8,128)}, u32[]{:S(2)}) copy-start(f32[50,16,128]{2,1,0:T(8,128)} %refs_6_.1) | copy-start | bytes 1228804
  4.4 22.8 %copy-start.1 = (f32[50,16,128]{2,1,0:T(8,128)S(1)}, f32[50,16,128]{2,1,0:T(8,128)}, u32[]{:S(2)}) copy-start(f32[50,16,128]{2,1,0:T(8,128)} %refs_1_.1) | copy-start | bytes 1228804
  7.7 19.5 %copy-start = (f32[50,16,128]{2,1,0:T(8,128)S(1)}, f32[50,16,128]{2,1,0:T(8,128)}, u32[]{:S(2)}) copy-start(f32[50,16,128]{2,1,0:T(8,128)} %refs_0_.1) | copy-start | bytes 1228804
  7.7 14.9 %all-to-all-start = ((f32[16,16,128]{2,1,0:T(8,128)}), f32[16,16,128]{2,1,0:T(8,128)S(1)}, u32[]{:S(2)}, u32[]{:S(2)}) async-start(f32[16,16,128]{2,1,0:T(8,128)} %get-tuple-element.20), calls=%async_computation | async-start | bytes 262144 | tf_op jit(solution)/shard_map/all_to_all | solution.py:354
  15.2 11.9 %collective-permute-start = (f32[100,128]{1,0:T(8,128)S(1)}, f32[100,128]{1,0:T(8,128)S(1)}, u32[]{:S(2)}, u32[]{:S(2)}) collective-permute-start(f32[100,128]{1,0:T(8,128)S(1)} %get-tuple-element.24.refs_11_), channel_id=1, source_target_pairs={{0,4},{4,0},{8,12},{12,8},{16,20},{20,16},{24,28},{28,24},{1,5},{5... | collective-permute-start | bytes 153608 | tf_op jit(solution)/shard_map/ppermute | solution.py:357
  15.6 11.5 %collective-permute-start.1 = (f32[100,128]{1,0:T(8,128)S(1)}, f32[100,128]{1,0:T(8,128)S(1)}, u32[]{:S(2)}, u32[]{:S(2)}) collective-permute-start(f32[100,128]{1,0:T(8,128)S(1)} %get-tuple-element.25.refs_12_), channel_id=1, source_target_pairs={{4,8},{8,4},{12,16},{16,12},{20,24},{24,20},{5,9},{9,5},{13,17},{1... | collective-permute-start | bytes 153608 | tf_op jit(solution)/shard_map/ppermute | solution.py:357
  23.6 9.9 %all-to-all-start.1 = ((f32[16,2,128]{2,1,0:T(2,128)}), f32[16,2,128]{2,1,0:T(2,128)S(1)}, u32[]{:S(2)}, u32[]{:S(2)}) async-start(f32[16,2,128]{2,1,0:T(2,128)} %get-tuple-element.28), calls=%async_computation.1 | async-start | bytes 32768 | tf_op jit(solution)/shard_map/all_to_all | solution.py:369
  27.1 0.7 %copy-start.6 = (s32[16,128]{1,0:T(8,128)S(1)}, s32[16,128]{1,0:T(8,128)}, u32[]{:S(2)}) copy-start(s32[16,128]{1,0:T(8,128)} %refs_10_.1) | copy-start | bytes 24580
  27.2 0.7 %copy-start.11 = (f32[8]{0:T(128)S(1)}, f32[8]{0:T(128)}, u32[]{:S(2)}) copy-start(f32[8]{0:T(128)} %refs_9_.1) | copy-start | bytes 100
  27.8 5.7 %copy-start.5 = (f32[10,256]{1,0:T(8,128)S(1)}, f32[10,256]{1,0:T(8,128)}, u32[]{:S(2)}) copy-start(f32[10,256]{1,0:T(8,128)} %nitrate.3) | copy-start | bytes 30724

commit v4 on v3

--- a/solution.py
+++ b/solution.py
@@ -44,10 +44,10 @@
     return jnp.sum(jnp.where(own, moved, 0.0), axis=0, keepdims=True)
 
 
-def front_kernel(per_block, top, axes_x, axes_y, *refs):
+def front_kernel(per_block, *refs):
     fields, grids = refs[:4], refs[4:7]
-    sent, sat, head, alpha, conduct, wet_out, x_first, x_second, y_edges = refs[7:16]
-    fields_in, perm, sent_in, small_sems, sems, sent_sem = refs[16:]
+    sent, head, alpha, perm, y_edges = refs[7:12]
+    fields_in, sent_in, small_sems, sems, sent_sem = refs[12:]
     layers, width_x, width_y = head.shape
     height = LANES // per_block
     small = [pltpu.make_async_copy(fields[i], fields_in[i], small_sems.at[i]) for i in range(4)]
@@ -71,48 +71,63 @@
         turned = jnp.concatenate(rows, axis=0).T
         sent_in[h * height : (h + 1) * height] = turned.reshape(height, per_block, LANES)
     lane = iota((width_x, width_y), 1)
-    low = jnp.zeros((width_x, width_y), jnp.float32)
-    high = jnp.zeros((width_x, width_y), jnp.float32)
+    borders = [jnp.zeros((width_x, width_y), jnp.float32)] * 3
     for i, (start, stop) in enumerate(parts):
         for copy in large[3 * i : 3 * i + 3]:
             copy.wait()
+        for k in range(start, stop):
+            own = lane // 2 == k
+            for j, ref in enumerate((head, alpha, perm)):
+                moved = pltpu.roll(ref[k], (2 * k + 1) % width_y, 1)
+                borders[j] = jnp.where(own, moved, borders[j])
+    wet = saturation(borders[0], borders[1])
+    cond = borders[2] * wet * wet * wet
+    y_edges[0] = borders[0]
+    y_edges[1] = cond
+    even = lane % 2 == 0
+    y_place, y_size = place_of(("gy",)), lax.axis_size("gy")
+    base = place_of(("gx", "gy"))
+
+    @pl.when(y_place > 0)
+    def _():
+        first = jnp.where(even, pltpu.roll(borders[0], width_y - 1, 1), cond)
+        sent_in[base - 1] = sent_in[base - 1] + first
+
+    @pl.when(y_place < y_size - 1)
+    def _():
+        last = jnp.where(even, cond, pltpu.roll(borders[0], 1, 1))
+        sent_in[base + 1] = sent_in[base + 1] + last
+
+    send = pltpu.make_async_copy(sent_in, sent, sent_sem)
+    send.start()
+    send.wait()
+
+
+def wet_kernel(top, axes_x, *refs):
+    head, alpha, perm = refs[:3]
+    extra, (sat, conduct, wet_out, x_first, x_second) = refs[3:5], refs[5:10]
+    extra_out, sems = refs[10:12], refs[12]
+    layers, width_x, width_y = head.shape
+    late = [pltpu.make_async_copy(extra[i], extra_out[i], sems.at[i]) for i in range(2)]
+    for copy in late:
+        copy.start()
+    for start, stop in parts_of(layers):
         part = slice(start, stop)
         wet = saturation(head[part], alpha[part])
-        cond = perm[part] * wet * wet * wet
-        conduct[part] = cond
+        conduct[part] = perm[part] * wet * wet * wet
         wet_out[part] = wet
         if start < top:
             last = min(stop, top)
             kept = wet[: last - start].reshape((last - start) * width_x, width_y)
             sat[start * width_x : last * width_x, :] = kept.astype(jnp.bfloat16)
-        for first, values in ((0, head[part]), (layers, cond)):
-            for k in range(start, stop):
-                place = first + k
-                value = values[k - start]
-                low = jnp.where(lane == place, pltpu.roll(value, place, 1), low)
-                high = jnp.where(lane == place, pltpu.roll(value, (place + 1) % width_y, 1), high)
-    y_edges[0] = low
-    y_edges[1] = high
-    y_place, y_size = place_of(axes_y), lax.axis_size(axes_y)
-    base = place_of(("gx", "gy"))
-
-    @pl.when(y_place > 0)
-    def _():
-        sent_in[base - 1] = sent_in[base - 1] + low
-
-    @pl.when(y_place < y_size - 1)
-    def _():
-        sent_in[base + 1] = sent_in[base + 1] + high
-
-    send = pltpu.make_async_copy(sent_in, sent, sent_sem)
-    send.start()
     even = place_of(axes_x) % 2 == 0
     for field, ref in enumerate((head, conduct)):
         rows = slice(field * layers, (field + 1) * layers)
         low, high = ref[:, 0, :], ref[:, width_x - 1, :]
         x_first[rows, :] = jnp.where(even, high, low)
         x_second[rows, :] = jnp.where(even, low, high)
-    send.wait()
+    for copy in late:
+        copy.wait()
 
 
 def hot(ids, size):
@@ -145,13 +160,14 @@
 
 def column_sources(top, width_x, width_y, fields, patch_sat, root_decay):
     total = jnp.zeros((top * width_x, width_y), jnp.float32)
+    table = root_decay[...]
     for h in range(fields.shape[0]):
         ids, crop, weight, rain = (fields[h, i : i + 1, :] for i in range(4))
         ids = ids.astype(jnp.int32)
         crop = crop.astype(jnp.int32)
         decay = jnp.zeros((1, LANES), jnp.float32)
-        for kind in range(root_decay.shape[0]):
-            decay = jnp.where(crop == kind, root_decay[kind], decay)
+        for kind in range(table.shape[1]):
+            decay = jnp.where(crop == kind, table[:, kind : kind + 1], decay)
         level = iota((top, LANES), 0)
         profile = jnp.exp(-(level.astype(jnp.float32) + 0.5) * decay)
         profile = profile / jnp.sum(profile, axis=0, keepdims=True)
@@ -173,7 +189,7 @@
     return total
 
 
-def balance_kernel(top, axes_x, axes_y, *refs):
+def balance_kernel(top, axes_x, *refs):
     grids = refs[:2]
     head, alpha, conduct, wet, got, fields, patch_sat, root_decay, land = refs[2:11]
     x_sent, x_got, y_edges = refs[11:13], refs[13:15], refs[15]
@@ -203,14 +219,16 @@
     heads, conds = faces
     x_faces[0] = 0.5 * (conds[2] + conds[0]) * (heads[2] - heads[0])
     x_faces[1] = 0.5 * (conds[1] + conds[3]) * (heads[1] - heads[3])
-    y_place, y_size = place_of(axes_y), lax.axis_size(axes_y)
+    y_place, y_size = place_of(("gy",)), lax.axis_size("gy")
     base = place_of(("gx", "gy"))
     before = jnp.where(y_place > 0, got[jnp.maximum(base - 1, 0)], 0.0)
     after = jnp.where(y_place < y_size - 1, got[jnp.minimum(base + 1, got.shape[0] - 1)], 0.0)
-    heads = (y_edges[0], y_edges[1], before, after)
-    conds = [pltpu.roll(v, width_y - layers, 1) for v in heads]
-    y_before = 0.5 * (conds[2] + conds[0]) * (heads[2] - heads[0])
-    y_after = 0.5 * (conds[1] + conds[3]) * (heads[1] - heads[3])
+    part, cond = y_edges[0], y_edges[1]
+    last = 0.5 * (cond + pltpu.roll(after, width_y - 1, 1)) * (part - after)
+    first = 0.5 * (cond + pltpu.roll(before, 1, 1)) * (part - before)
+    lane = iota((width_x, width_y), 1)
+    y_flux = jnp.where(lane % 2 == 0, last, first)
+    y_border = (lane == 0) | (lane == width_y - 1)
 
     writes = []
     for i, (start, stop) in enumerate(parts):
@@ -237,13 +255,11 @@
         if stop == layers:
             down = jnp.concatenate([down, cond[-1:]], 0)
         total = total + (down[1:] - down[:-1])
-        row, lane = row[0], lane[0]
+        row = row[0]
         for k in range(start, stop):
             edge = jnp.where(row == 0, -x_faces[0, k : k + 1, :], 0.0)
             edge = edge + jnp.where(row == width_x - 1, x_faces[1, k : k + 1, :], 0.0)
-            low = pltpu.roll(y_before, (width_y - k) % width_y, 1)
-            high = pltpu.roll(y_after, (width_y - 1 - k) % width_y, 1)
-            edge = edge - jnp.where(lane == 0, low, 0.0) + jnp.where(lane == width_y - 1, high, 0.0)
+            edge = edge + jnp.where(y_border, pltpu.roll(y_flux, width_y - 1 - 2 * k, 1), 0.0)
             one = total[k - start] + edge
             out[k] = one - sources[k] if k < top else one
         rows = pl.ds(start, stop - start)
@@ -281,7 +297,7 @@
 
 def call(body, name, ins, outs, scratch=()):
     space = {"V": pltpu.VMEM, "S": pltpu.SMEM, "H": pltpu.HBM}
-    return pl.pallas_call(
+    kernel = pl.pallas_call(
         body,
         out_shape=tuple(shape for shape, _ in outs),
         in_specs=[pl.BlockSpec(memory_space=space[i]) for i in ins],
@@ -291,6 +307,16 @@
         compiler_params=pltpu.CompilerParams(vmem_limit_bytes=VMEM_LIMIT),
         cost_estimate=pl.CostEstimate(flops=1000, bytes_accessed=1000, transcendentals=0),
     )
+
+    def run(*args):
+        return kernel(
+            *(
+                pltpu.with_memory_space_constraint(arg, pltpu.HBM) if i == "H" else arg
+                for i, arg in zip(ins, args)
+            )
+        )
+
+    return run
 
 
 def per_device(
@@ -309,7 +335,7 @@
 ):
     layers, width_x, width_y = pressure.shape
     top, slots = nitrate.shape
-    group, axes_x, axes_y = ("gx", "gy"), ("sec", "gx"), ("gy",)
+    group, axes_x = ("gx", "gy"), ("sec", "gx")
     owners = lax.axis_size(group)
     per_block = slots // owners
     if LANES % per_block or slots % LANES or per_block != width_x:
@@ -327,30 +353,40 @@
 
     flat = [v.reshape(banks, LANES) for v in (patch_column, crop_type, patch_weight, rain)]
     x_edge = shape((2 * layers, width_y), f32)
-    sent, sat, head, alpha, conduct, wet, *x_sent, y_edges = call(
-        functools.partial(front_kernel, per_block, top, axes_x, axes_y),
+    sent, head, alpha, perm, y_edges = call(
+        functools.partial(front_kernel, per_block),
         "front",
         "HHHHHHH",
         (
             (shape((owners, per_block, LANES), f32), "H"),
-            (shape((top * width_x, width_y), jnp.bfloat16), "V"),
             (field, "V"),
             (field, "V"),
             (field, "V"),
-            (field, "V"),
-            (x_edge, "V"),
-            (x_edge, "V"),
             (shape((2, width_x, width_y), f32), "V"),
         ),
         (
             [pltpu.VMEM((banks, LANES), v.dtype) for v in flat],
-            field_in,
             pltpu.VMEM((owners, per_block, LANES), f32),
             dma((4,)),
             dma((count, 3)),
             dma,
         ),
     )(*flat, pressure, vg_alpha, conductivity)
+    sat, conduct, wet, *x_sent, land, table = call(
+        functools.partial(wet_kernel, top, axes_x),
+        "wet",
+        "VVVHH",
+        (
+            (shape((top * width_x, width_y), jnp.bfloat16), "V"),
+            (field, "V"),
+            (field, "V"),
+            (x_edge, "V"),
+            (x_edge, "V"),
+            (shape((width_x, width_y), land_mask.dtype), "V"),
+            (shape((1, root_decay.shape[0]), f32), "V"),
+        ),
+        (dma((2,)),),
+    )(head, alpha, perm, land_mask, root_decay.reshape(1, -1))
     got = lax.all_to_all(sent, group, split_axis=0, concat_axis=0, tiled=True)
 
     x_size = lax.axis_size(axes_x)
@@ -369,9 +405,9 @@
     back = lax.all_to_all(back, group, split_axis=0, concat_axis=0, tiled=True)
 
     residual, order = call(
-        functools.partial(balance_kernel, top, axes_x, axes_y),
+        functools.partial(balance_kernel, top, axes_x),
         "balance",
-        "HHVVVVVVVSVVVVVV",
+        "HHVVVVVVVVVVVVVV",
         ((field, "H"), (shape((8, LANES), f32), "V")),
         (
             field_in,
@@ -383,7 +419,7 @@
         ),
     )(
         pressure_old, porosity, head, alpha, conduct, wet, got, fields, patch_sat,
-        root_decay, land_mask, *x_sent, *x_got, y_edges,
+        table, land, *x_sent, *x_got, y_edges,
     )
     (nitrate_out,) = call(
         functools.partial(nitrate_kernel, per_block),

time: 34.8 us -> 30.3 us (0.87)
  local copies, waits for them, and re-layouts: 4.36 us -> 0.01 us
  waiting for transfers between devices: 7.85 us -> 8.75 us
  Pallas kernels: 9.26 us -> 8.48 us
    unnamed x24 -> x2, local copies, waits for them, and re-layouts: 4.36 us -> 0.01 us
    all_to_all x1, waiting for transfers between devices: 1.57 us -> 3.25 us  [per_device(): back = lax.all_to_all(back, group, split_axis=0, concat_axis=0, tiled=True)]
    all_to_all x1, waiting for transfers between devices: 6.28 us -> 5.49 us  [per_device(): got = lax.all_to_all(sent, group, split_axis=0, concat_axis=0, tiled=True)]
    pallas_call x4 -> x5, Pallas kernels: 9.26 us -> 8.48 us  [run(): kernel(*(pltpu.with_memory_space_constraint(arg, pltpu.HBM) if i == 'H' e...]
  transfers between devices with their start and end apart: 4 -> 4, of which waited for: 2 -> 2; matrix products, arithmetic and copies ran while one was open for 0% -> 0% of each run, Pallas kernels for 15% -> 16%
where the time goes in v4:
time: 30.3 us; the launch traced here: 29.9 us
  starting transfers between devices  12 us (40%)
  waiting for transfers between devices  8.75 us (29%)
  Pallas kernels  8.48 us (28%)
  between operations  0.71 us (2%)
    pallas_call x5, Pallas kernels, run(): kernel(*(pltpu.with_memory_space_constraint(arg, pltpu.HBM) if i == 'H' e...  8.48 us
    all_to_all x1, starting transfers between devices, per_device(): got = lax.all_to_all(sent, group, split_axis=0, concat_axis=0, tiled=True)  7.35 us
    all_to_all x1, waiting for transfers between devices, per_device(): got = lax.all_to_all(sent, group, split_axis=0, concat_axis=0, tiled=True)  5.49 us
    all_to_all x1, starting transfers between devices, per_device(): back = lax.all_to_all(back, group, split_axis=0, concat_axis=0, tiled=True)  3.49 us
    all_to_all x1, waiting for transfers between devices, per_device(): back = lax.all_to_all(back, group, split_axis=0, concat_axis=0, tiled=True)  3.25 us
    ppermute x2, starting transfers between devices, per_device(): lax.ppermute(x_sent[i], axes_x, swap_pairs(x_size, i))  1.12 us
  transfers between devices with their start and end apart: 4, of which 2 were waited for; matrix products, arithmetic and copies ran while one was open for 0% of the time, Pallas kernels for 16%

profile of v4, /device:TPU:0, one launch (start us, length us, event | category | flops | bytes accessed | tf_op | source)
XLA Modules:
  0.0 29.9 jit_solution(7062120388969787086)
XLA Ops:
  0.6 2.8 %front.1 = (f32[16,16,128]{2,1,0:T(8,128)}, f32[50,16,128]{2,1,0:T(8,128)S(1)}, f32[50,16,128]{2,1,0:T(8,128)S(1)}, f32[50,16,128]{2,1,0:T(8,128)S(1)}, f32[2,16,128]{2,1,0:T(8,128)S(1)}) custom-call(s32[2,128]{1,0:T(2,128)} %bitcast.5, s32[2,128]{1,0:T(2,128)} %bitcast.6, f32[2,128]{1,0:T(2,128)} %bitcast.7, f32[2,128]{1,0:T(2,128)} %bitcast.8, ...), custom_call_target="tpu_custom_call" | custom-call | flops 1000 | bytes 1000 | tf_op jit(solution)/shard_map/front/pallas_call | solution.py:312
  3.5 7.4 %all-to-all-start = ((f32[16,16,128]{2,1,0:T(8,128)}), f32[16,16,128]{2,1,0:T(8,128)S(1)}, u32[]{:S(2)}, u32[]{:S(2)}) async-start(f32[16,16,128]{2,1,0:T(8,128)} %get-tuple-element.24), calls=%async_computation | async-start | bytes 262144 | tf_op jit(solution)/shard_map/all_to_all | solution.py:390
  10.8 0.7 %wet.1 = (bf16[160,128]{1,0:T(8,128)(2,1)S(1)}, f32[50,16,128]{2,1,0:T(8,128)S(1)}, f32[50,16,128]{2,1,0:T(8,128)S(1)}, f32[100,128]{1,0:T(8,128)S(1)}, f32[100,...) custom-call(f32[50,16,128]{2,1,0:T(8,128)S(1)} %get-tuple-element.19.refs_0_.refs_2_, ...), custom_call_target="tpu_custom_call" | custom-call | flops 1000 | bytes 1000 | tf_op jit(solution)/shard_map/wet/pallas_call | solution.py:312
  11.5 0.5 %collective-permute-start = (f32[100,128]{1,0:T(8,128)S(1)}, f32[100,128]{1,0:T(8,128)S(1)}, u32[]{:S(2)}, u32[]{:S(2)}) collective-permute-start(f32[100,128]{1,0:T(8,128)S(1)} %get-tuple-element.30.refs_11_), channel_id=1, source_target_pairs={{0,4},{4,0},{8,12},{12,8},{16,20},{20,16},{24,28},{28,24},{1,5},{5... | collective-permute-start | bytes 153608 | tf_op jit(solution)/shard_map/ppermute | solution.py:393
  12.0 0.7 %collective-permute-start.1 = (f32[100,128]{1,0:T(8,128)S(1)}, f32[100,128]{1,0:T(8,128)S(1)}, u32[]{:S(2)}, u32[]{:S(2)}) collective-permute-start(f32[100,128]{1,0:T(8,128)S(1)} %get-tuple-element.31.refs_12_), channel_id=1, source_target_pairs={{4,8},{8,4},{12,16},{16,12},{20,24},{24,20},{5,9},{9,5},{13,17},{1... | collective-permute-start | bytes 153608 | tf_op jit(solution)/shard_map/ppermute | solution.py:393
  12.7 5.5 %all-to-all-done.got.refs_6_ = f32[16,16,128]{2,1,0:T(8,128)S(1)} async-done(((f32[16,16,128]{2,1,0:T(8,128)}), f32[16,16,128]{2,1,0:T(8,128)S(1)}, u32[]{:S(2)}, u32[]{:S(2)}) %all-to-all-start) | async-done | bytes 131104 | tf_op jit(solution)/shard_map/all_to_all | solution.py:390
  18.2 1.1 %pick.1 = (f32[16,2,128]{2,1,0:T(2,128)}, f32[2,16,128]{2,1,0:T(8,128)S(1)}, f32[2,8,128]{2,1,0:T(8,128)S(1)}) custom-call(f32[16,16,128]{2,1,0:T(8,128)S(1)} %all-to-all-done.got.refs_6_, bf16[160,128]{1,0:T(8,128)(2,1)S(1)} %get-tuple-element.25.sat), custom_call_target="tpu_custom_call" | custom-call | flops 1000 | bytes 1000 | tf_op jit(solution)/shard_map/pick/pallas_call | solution.py:312
  19.2 3.5 %all-to-all-start.1 = ((f32[16,2,128]{2,1,0:T(2,128)}), f32[16,2,128]{2,1,0:T(2,128)S(1)}, u32[]{:S(2)}, u32[]{:S(2)}) async-start(f32[16,2,128]{2,1,0:T(2,128)} %get-tuple-element.34), calls=%async_computation.1 | async-start | bytes 32768 | tf_op jit(solution)/shard_map/all_to_all | solution.py:405
  22.7 0.0 collective-permute-done.refs_13_
  22.7 0.0 collective-permute-done.1.refs_14_
  22.7 0.0 copy-start
  22.8 3.1 %balance.1 = (f32[50,16,128]{2,1,0:T(8,128)}, f32[8,128]{1,0:T(8,128)S(1)}) custom-call(f32[50,16,128]{2,1,0:T(8,128)} %refs_0_.1, f32[50,16,128]{2,1,0:T(8,128)} %refs_1_.1, f32[50,16,128]{2,1,0:T(8,128)S(1)} %get-tuple-element.19.refs_0_.refs_2_, f32[50,16,128]{2,1,0:T(8,128)S(1)} %get-tuple-element.20.refs_1_.refs_3_, ...), custom_call_target="tpu_custom_call" | custom-call | flops 1000 | bytes 1000 | tf_op jit(solution)/shard_map/balance/pallas_call | solution.py:312
  25.9 3.2 %all-to-all-done.1.back = f32[16,2,128]{2,1,0:T(2,128)S(1)} async-done(((f32[16,2,128]{2,1,0:T(2,128)}), f32[16,2,128]{2,1,0:T(2,128)S(1)}, u32[]{:S(2)}, u32[]{:S(2)}) %all-to-all-start.1) | async-done | bytes 16416 | tf_op jit(solution)/shard_map/all_to_all | solution.py:405
  29.1 0.0 copy-done
  29.1 0.8 %nitrate.2 = f32[10,256]{1,0:T(8,128)} custom-call(f32[16,2,128]{2,1,0:T(2,128)S(1)} %all-to-all-done.1.back, f32[10,256]{1,0:T(8,128)S(1)} %copy-done, f32[8,128]{1,0:T(8,128)S(1)} %get-tuple-element.35.order), custom_call_target="tpu_custom_call" | custom-call | flops 1000 | bytes 1000 | tf_op jit(solution)/shard_map/nitrate/pallas_call | solution.py:312
Async XLA Ops:
  3.5 14.7 %all-to-all-start = ((f32[16,16,128]{2,1,0:T(8,128)}), f32[16,16,128]{2,1,0:T(8,128)S(1)}, u32[]{:S(2)}, u32[]{:S(2)}) async-start(f32[16,16,128]{2,1,0:T(8,128)} %get-tuple-element.24), calls=%async_computation | async-start | bytes 262144 | tf_op jit(solution)/shard_map/all_to_all | solution.py:390
  11.5 11.2 %collective-permute-start = (f32[100,128]{1,0:T(8,128)S(1)}, f32[100,128]{1,0:T(8,128)S(1)}, u32[]{:S(2)}, u32[]{:S(2)}) collective-permute-start(f32[100,128]{1,0:T(8,128)S(1)} %get-tuple-element.30.refs_11_), channel_id=1, source_target_pairs={{0,4},{4,0},{8,12},{12,8},{16,20},{20,16},{24,28},{28,24},{1,5},{5... | collective-permute-start | bytes 153608 | tf_op jit(solution)/shard_map/ppermute | solution.py:393
  12.0 10.7 %collective-permute-start.1 = (f32[100,128]{1,0:T(8,128)S(1)}, f32[100,128]{1,0:T(8,128)S(1)}, u32[]{:S(2)}, u32[]{:S(2)}) collective-permute-start(f32[100,128]{1,0:T(8,128)S(1)} %get-tuple-element.31.refs_12_), channel_id=1, source_target_pairs={{4,8},{8,4},{12,16},{16,12},{20,24},{24,20},{5,9},{9,5},{13,17},{1... | collective-permute-start | bytes 153608 | tf_op jit(solution)/shard_map/ppermute | solution.py:393
  19.2 9.9 %all-to-all-start.1 = ((f32[16,2,128]{2,1,0:T(2,128)}), f32[16,2,128]{2,1,0:T(2,128)S(1)}, u32[]{:S(2)}, u32[]{:S(2)}) async-start(f32[16,2,128]{2,1,0:T(2,128)} %get-tuple-element.34), calls=%async_computation.1 | async-start | bytes 32768 | tf_op jit(solution)/shard_map/all_to_all | solution.py:405
  22.7 6.4 %copy-start = (f32[10,256]{1,0:T(8,128)S(1)}, f32[10,256]{1,0:T(8,128)}, u32[]{:S(2)}) copy-start(f32[10,256]{1,0:T(8,128)} %nitrate.3) | copy-start | bytes 30724

commit v5 on v3

v5 whole, which is shorter than its diff:
```python
import functools

import jax
import jax.numpy as jnp
from jax import lax
from jax.experimental import pallas as pl
from jax.experimental.pallas import tpu as pltpu
from jax.sharding import PartitionSpec as P

NSUB = 4
LANES = 128
CHUNK = 10
FRONT_CHUNK = 25
FIELD_LANE = 104
VMEM_LIMIT = 24 * 1024 * 1024


def iota(shape, dim):
    return lax.broadcasted_iota(jnp.int32, shape, dim)


def place_of(axes):
    index = 0
    for axis in axes:
        index = index * lax.axis_size(axis) + lax.axis_index(axis)
    return index


def parts_of(layers, size=CHUNK):
    return [(i, min(layers, i + size)) for i in range(0, layers, size)]


def saturation(head, alpha_field):
    suction = jnp.maximum(-head, 0.0) + jnp.log1p(jnp.exp(-jnp.abs(head)))
    scaled = alpha_field * suction
    return lax.rsqrt(1.0 + scaled * scaled)


def fold_border(border, own_first):
    rows, width = border.shape
    upper, lower = border[: rows // 2], border[rows // 2 :]
    if own_first:
        upper = pltpu.roll(upper, width - 1, 1)
    else:
        lower = pltpu.roll(lower, 1, 1)
    return jnp.where(iota(upper.shape, 1) % 2 == 0, upper, lower)


def unfold_border(block, place):
    width = block.shape[1]
    moved = pltpu.roll(block, 1 if place else width - 1, 1)
    return jnp.concatenate([moved, block] if place else [block, moved], axis=0)


def add_border(blocks, border):
    y_place, y_size = place_of(("gy",)), lax.axis_size("gy")
    base = place_of(("gx", "gy"))

    @pl.when(y_place > 0)
    def _():
        blocks[base - 1] = blocks[base - 1] + fold_border(border, True)

    @pl.when(y_place < y_size - 1)
    def _():
        blocks[base + 1] = blocks[base + 1] + fold_border(border, False)


def neighbour_borders(blocks):
    y_place, y_size = place_of(("gy",)), lax.axis_size("gy")
    base = place_of(("gx", "gy"))
    before = blocks[jnp.maximum(base - 1, 0)]
    before = unfold_border(jnp.where(y_place > 0, before, 0.0), 1)
    after = blocks[jnp.minimum(base + 1, blocks.shape[0] - 1)]
    after = unfold_border(jnp.where(y_place < y_size - 1, after, 0.0), 0)
    return jnp.where(iota(after.shape, 1) % 2 == 0, after, before)


def border_of(ref, start, stop, border):
    lane = iota(border.shape, 1)
    for k in range(start, stop):
        moved = pltpu.roll(ref[k], (2 * k + 1) % LANES, 1)
        border = jnp.where(lane // 2 == k, moved, border)
    return border


def pack_blocks(rows, count, blocks, bank):
    height, size = blocks.shape[1], LANES // (2 * blocks.shape[1])
    above = jnp.zeros((FIELD_LANE, LANES), jnp.float32)
    below = jnp.zeros((LANES - FIELD_LANE - rows.shape[0], LANES), jnp.float32)
    turned = jnp.concatenate([above, rows, below], axis=0).T
    for b in range(size):
        upper = turned[2 * b * height : (2 * b + 1) * height]
        lower = turned[(2 * b + 1) * height : (2 * b + 2) * height]
        blocks[bank * size + b] = upper + pltpu.roll(lower, count, 1)


def unpack_blocks(blocks, count, bank, height):
    rows, size = blocks.shape[1], LANES // (2 * blocks.shape[1])
    pieces = []
    for b in range(size):
        block = blocks[bank * size + b]
        pieces += [block, pltpu.roll(block, LANES - count, 1)]
    turned = jnp.concatenate(pieces, axis=0).T
    return turned[FIELD_LANE : FIELD_LANE + height]


def front_kernel(top, *refs):
    fields, grids, extra = refs[:4], refs[4:7], refs[7:9]
    sent, head, alpha, conduct, wet_out, sat, border_out = refs[9:16]
    extra_out, (fields_in, perm, sent_in, small_sems, sems, sent_sem) = refs[16:18], refs[18:]
    layers, width_x, width_y = head.shape
    small = [pltpu.make_async_copy(fields[i], fields_in[i], small_sems.at[i]) for i in range(4)]
    extras = [pltpu.make_async_copy(extra[i], extra_out[i], small_sems.at[4 + i]) for i in range(2)]
    parts = parts_of(layers, FRONT_CHUNK)
    large = []
    for i, (start, stop) in enumerate(parts):
        rows = pl.ds(start, stop - start)
        large.append(
            [
                pltpu.make_async_copy(source.at[rows], target.at[rows], sems.at[i, j])
                for j, (source, target) in enumerate(zip(grids, (head, alpha, perm)))
            ]
        )
    for copy in (*small, *(copies[j] for j in range(3) for copies in large), *extras):
        copy.start()
    for copy in small:
        copy.wait()
    for bank in range(fields_in[0].shape[0]):
        rows = [ref[bank : bank + 1, :].astype(jnp.float32) for ref in fields_in]
        rows.append(jnp.zeros((4, LANES), jnp.float32))
        pack_blocks(jnp.concatenate(rows, axis=0), 4, sent_in, bank)
    border = jnp.zeros((width_x, width_y), jnp.float32)
    for i, (start, stop) in enumerate(parts):
        large[i][0].wait()
        border = border_of(head, start, stop, border)
    border_out[...] = border
    add_border(sent_in, border)
    send = pltpu.make_async_copy(sent_in, sent, sent_sem)
    send.start()
    for i, (start, stop) in enumerate(parts):
        large[i][1].wait()
        large[i][2].wait()
        part = slice(start, stop)
        wet = saturation(head[part], alpha[part])
        conduct[part] = perm[part] * wet * wet * wet
        wet_out[part] = wet
        if start < top:
            last = min(stop, top)
            kept = wet[: last - start].reshape((last - start) * width_x, width_y)
            sat[start * width_x : last * width_x, :] = kept.astype(jnp.bfloat16)
    for copy in (*extras, send):
        copy.wait()


def edge_kernel(axes_x, head, conduct, x_first, x_second, border_out):
    layers, width_x, width_y = head.shape
    border = jnp.zeros((width_x, width_y), jnp.float32)
    border_out[...] = border_of(conduct, 0, layers, border)
    even = place_of(axes_x) % 2 == 0
    for field, ref in enumerate((head, conduct)):
        rows = slice(field * layers, (field + 1) * layers)
        low, high = ref[:, 0, :], ref[:, width_x - 1, :]
        x_first[rows, :] = jnp.where(even, high, low)
        x_second[rows, :] = jnp.where(even, low, high)


def hot(ids, size):
    return iota((size, LANES), 0) == ids


def pick_kernel(top, width_x, got, sat, border, back, patch_sat, fields):
    width_y = sat.shape[1]
    for bank in range(fields.shape[0]):
        rows = unpack_blocks(got, 4, bank, 8)
        fields[bank] = rows
        ids = rows[0:1].astype(jnp.int32)
        lane_hot = hot(lax.rem(ids, width_y), width_y).astype(jnp.float32).astype(jnp.bfloat16)
        row_hot = hot(lax.div(ids, width_y), width_x)
        picked = jnp.dot(sat[...], lane_hot, preferred_element_type=jnp.float32)
        patch_sat[bank] = jnp.zeros(patch_sat.shape[1:], jnp.float32)
        for k in range(top):
            one = picked[k * width_x : (k + 1) * width_x]
            patch_sat[bank, k : k + 1, :] = jnp.sum(
                jnp.where(row_hot, one, 0.0), axis=0, keepdims=True
            )
        pack_blocks(patch_sat[bank], top, back, bank)
    add_border(back, border[...])


def column_sources(top, width_x, width_y, fields, patch_sat, root_decay):
    total = jnp.zeros((top * width_x, width_y), jnp.float32)
    table = root_decay[...]
    for h in range(fields.shape[0]):
        ids, crop, weight, rain = (fields[h, i : i + 1, :] for i in range(4))
        ids = ids.astype(jnp.int32)
        crop = crop.astype(jnp.int32)
        decay = jnp.zeros((1, LANES), jnp.float32)
        for kind in range(table.shape[1]):
            decay = jnp.where(crop == kind, table[:, kind : kind + 1], decay)
        level = iota((top, LANES), 0)
        profile = jnp.exp(-(level.astype(jnp.float32) + 0.5) * decay)
        profile = profile / jnp.sum(profile, axis=0, keepdims=True)
        sat = patch_sat[h][:top]
        inflow = jnp.where(level == 0, rain * (1.0 - sat), 0.0)
        sources = inflow - weight * profile * sat
        lane_hot = hot(lax.rem(ids, width_y), width_y).astype(jnp.float32)
        row_hot = hot(lax.div(ids, width_y), width_x)
        spread = jnp.concatenate(
            [jnp.where(row_hot, sources[k : k + 1], 0.0) for k in range(top)], axis=0
        )
        total = total + lax.dot_general(
            spread,
            lane_hot,
            (((1,), (1,)), ((), ())),
            precision=lax.Precision.HIGHEST,
            preferred_element_type=jnp.float32,
        )
    return total


def balance_kernel(top, axes_x, *refs):
    head_old, porosity = refs[:2]
    head, alpha, conduct, wet, fields, patch_sat, root_decay, land = refs[2:10]
    x_sent, x_got, out = refs[10:12], refs[12:14], refs[14]
    x_faces = refs[15]
    layers, width_x, width_y = head.shape
    parts = parts_of(layers)
    sources = column_sources(top, width_x, width_y, fields, patch_sat, root_decay)
    sources = sources.reshape(top, width_x, width_y) * land[...].astype(jnp.float32)[None]

    even = place_of(axes_x) % 2 == 0
    faces = []
    for rows in (slice(0, layers), slice(layers, 2 * layers)):
        first, second = (r[rows, :] for r in x_sent)
        low, high = jnp.where(even, second, first), jnp.where(even, first, second)
        first, second = (r[rows, :] for r in x_got)
        before, after = jnp.where(even, second, first), jnp.where(even, first, second)
        faces.append((low, high, before, after))
    heads, conds = faces
    x_faces[0] = 0.5 * (conds[2] + conds[0]) * (heads[2] - heads[0])
    x_faces[1] = 0.5 * (conds[1] + conds[3]) * (heads[1] - heads[3])
    for i, (start, stop) in enumerate(parts):
        shape = (stop - start, width_x, width_y)
        part, cond = head[start:stop], conduct[start:stop]
        row, lane = iota(shape, 1), iota(shape, 2)
        wet_old = saturation(head_old[start:stop], alpha[start:stop])
        total = porosity[start:stop] * (wet[start:stop] - wet_old)
        for axis, place, size in ((1, row, width_x), (2, lane, width_y)):
            face = (
                0.5
                * (cond + pltpu.roll(cond, size - 1, axis))
                * (part - pltpu.roll(part, size - 1, axis))
            )
            face = jnp.where(place == size - 1, 0.0, face)
            total = total + (face - pltpu.roll(face, 1, axis))
        below = min(layers, stop + 1)
        part, cond = head[max(0, start - 1) : below], conduct[max(0, start - 1) : below]
        down = 0.5 * (cond[:-1] + cond[1:]) * (part[:-1] - part[1:] + 1.0)
        if start == 0:
            down = jnp.concatenate([jnp.zeros_like(cond[:1]), down], 0)
        if stop == layers:
            down = jnp.concatenate([down, cond[-1:]], 0)
        total = total + (down[1:] - down[:-1])
        row = row[0]
        for k in range(start, stop):
            edge = jnp.where(row == 0, -x_faces[0, k : k + 1, :], 0.0)
            edge = edge + jnp.where(row == width_x - 1, x_faces[1, k : k + 1, :], 0.0)
            one = total[k - start] + edge
            out[k] = one - sources[k] if k < top else one


def last_kernel(back, got, heads, conds, partial, nitrate, residual, nitrate_out, out, value_out, sems):
    layers, width_x, width_y = partial.shape
    top = nitrate.shape[0]
    head, cond = heads[...], conds[...]
    flux = 0.5 * (cond + neighbour_borders(back)) * (head - neighbour_borders(got))
    lane = iota(flux.shape, 1)
    on_border = (lane == 0) | (lane == width_y - 1)
    parts = parts_of(layers, 2 * CHUNK)
    writes = []
    for i, (start, stop) in enumerate(parts):
        for k in range(start, stop):
            edge = pltpu.roll(flux, width_y - 1 - 2 * k, 1)
            out[k] = partial[k] + jnp.where(on_border, edge, 0.0)
        rows = pl.ds(start, stop - start)
        copy = pltpu.make_async_copy(out.at[rows], residual.at[rows], sems.at[i])
        copy.start()
        writes.append(copy)
    for bank in range(nitrate.shape[1] // LANES):
        sat = unpack_blocks(back, top, bank, 16)[:top]
        lanes = slice(bank * LANES, (bank + 1) * LANES)
        loss = 0.3 * sat * sat
        value = nitrate[:, lanes]
        for _ in range(NSUB):
            upper = jnp.concatenate([value[:1], value[:-1]], 0)
            lower = jnp.concatenate([value[1:], value[-1:]], 0)
            value = value + 0.2 * (upper + lower - 2.0 * value) - loss * value
        value_out[:, lanes] = value
    copy = pltpu.make_async_copy(value_out, nitrate_out, sems.at[len(parts)])
    copy.start()
    writes.append(copy)
    for copy in writes:
        copy.wait()


def swap_pairs(size, first):
    pairs = []
    for i in range(first, size - 1, 2):
        pairs += [(i, i + 1), (i + 1, i)]
    return pairs


def call(body, name, ins, outs, scratch=(), cost=1000):
    space = {"V": pltpu.VMEM, "S": pltpu.SMEM, "H": pltpu.HBM}
    kernel = pl.pallas_call(
        body,
        out_shape=tuple(shape for shape, _ in outs),
        in_specs=[pl.BlockSpec(memory_space=space[i]) for i in ins],
        out_specs=tuple(pl.BlockSpec(memory_space=space[i]) for _, i in outs),
        scratch_shapes=scratch,
        name=name,
        compiler_params=pltpu.CompilerParams(vmem_limit_bytes=VMEM_LIMIT),
        cost_estimate=pl.CostEstimate(flops=1000000000 if cost>1000 else 1000, bytes_accessed=cost, transcendentals=0),
    )

    def run(*args):
        return kernel(
            *(
                pltpu.with_memory_space_constraint(arg, pltpu.HBM) if i == "H" else arg
                for i, arg in zip(ins, args)
            )
        )

    return run


def per_device(
    pressure,
    pressure_old,
    conductivity,
    vg_alpha,
    porosity,
    land_mask,
    nitrate,
    patch_column,
    crop_type,
    patch_weight,
    rain,
    root_decay,
):
    layers, width_x, width_y = pressure.shape
    top, slots = nitrate.shape
    group, axes_x = ("gx", "gy"), ("sec", "gx")
    owners = lax.axis_size(group)
    per_block = slots // owners
    if LANES % per_block or slots % LANES or per_block != width_x:
        raise ValueError("block size")
    if width_y != LANES or width_x != 16 or 2 * layers > FIELD_LANE or FIELD_LANE + 2 * top > LANES:
        raise ValueError("grid size")
    half = width_x // 2
    banks = slots // LANES
    f32 = jnp.float32
    shape, dma = jax.ShapeDtypeStruct, pltpu.SemaphoreType.DMA
    field = shape((layers, width_x, width_y), f32)
    field_in = pltpu.VMEM((layers, width_x, width_y), f32)
    count, halves = len(parts_of(layers)), len(parts_of(layers, 2 * CHUNK))
    blocks = shape((owners, half, LANES), f32)
    border = shape((width_x, width_y), f32)

    flat = [v.reshape(banks, LANES) for v in (patch_column, crop_type, patch_weight, rain)]
    x_edge = shape((2 * layers, width_y), f32)
    sent, head, alpha, conduct, wet, sat, head_border, land, table = call(
        functools.partial(front_kernel, top),
        "front",
        "HHHHHHHHH",
        (
            (blocks, "H"),
            (field, "V"),
            (field, "V"),
            (field, "V"),
            (field, "V"),
            (shape((top * width_x, width_y), jnp.bfloat16), "V"),
            (border, "V"),
            (shape((width_x, width_y), land_mask.dtype), "V"),
            (shape((1, root_decay.shape[0]), f32), "V"),
        ),
        (
            [pltpu.VMEM((banks, LANES), v.dtype) for v in flat],
            field_in,
            pltpu.VMEM((owners, half, LANES), f32),
            dma((6,)),
            dma((len(parts_of(layers, FRONT_CHUNK)), 3)),
            dma,
        ),
    )(*flat, pressure, vg_alpha, conductivity, land_mask, root_decay.reshape(1, -1))
    got = lax.all_to_all(sent, group, split_axis=0, concat_axis=0, tiled=True)
    *x_sent, cond_border = call(
        functools.partial(edge_kernel, axes_x),
        "edge",
        "VV",
        ((x_edge, "V"), (x_edge, "V"), (border, "V")),
    )(head, conduct)

    x_size = lax.axis_size(axes_x)
    x_got = [lax.ppermute(x_sent[i], axes_x, swap_pairs(x_size, i)) for i in (0, 1)]

    back, patch_sat, fields = call(
        functools.partial(pick_kernel, top, width_x),
        "pick",
        "VVV",
        (
            (blocks, "V"),
            (shape((banks, 16, LANES), f32), "V"),
            (shape((banks, 8, LANES), f32), "V"),
        ),
    )(got, sat, cond_border)
    back = lax.all_to_all(back, group, split_axis=0, concat_axis=0, tiled=True)

    (partial,) = call(
        functools.partial(balance_kernel, top, axes_x),
        "balance",
        "VVVVVVVVVVVVVV",
        ((field, "V"),),
        (pltpu.VMEM((2, layers, width_y), f32),),
        cost=3000000,
    )(
        pressure_old, porosity, head, alpha, conduct, wet, fields, patch_sat,
        table, land, *x_sent, *x_got,
    )
    residual, nitrate_out = call(
        last_kernel,
        "last",
        "VVVVVV",
        ((field, "H"), (shape((top, slots), f32), "H")),
        (field_in, pltpu.VMEM((top, slots), f32), dma((halves + 1,))),
    )(back, got, head_border, cond_border, partial, nitrate)
    return (residual, nitrate_out)


def solution(mesh):
    placed = (
        P(None, ("sec", "gx"), "gy"),
        P(None, ("sec", "gx"), "gy"),
        P(None, ("sec", "gx"), "gy"),
        P(None, ("sec", "gx"), "gy"),
        P(None, ("sec", "gx"), "gy"),
        P(("sec", "gx"), "gy"),
        P(None, ("sec", "gx", "gy")),
        P(("sec", "gx", "gy")),
        P(("sec", "gx", "gy")),
        P(("sec", "gx", "gy")),
        P(("sec", "gx", "gy")),
        P(),
    )
    return jax.shard_map(
        per_device,
        mesh=mesh,
        in_specs=placed,
        out_specs=(P(None, ("sec", "gx"), "gy"), P(None, ("sec", "gx", "gy"))),
        check_vma=False,
    )
```

time: 34.8 us -> 29.6 us (0.85)
  local copies, waits for them, and re-layouts: 4.36 us -> 0.02 us
  Pallas kernels: 9.26 us -> 5.67 us
  waiting for transfers between devices: 7.85 us -> 10.8 us
    unnamed x24 -> x6, local copies, waits for them, and re-layouts: 4.36 us -> 0.02 us
    all_to_all x1, waiting for transfers between devices: 1.57 us -> 5.57 us  [per_device(): back = lax.all_to_all(back, group, split_axis=0, concat_axis=0, tiled=True)]
    pallas_call x4 -> x5, Pallas kernels: 9.26 us -> 5.67 us  [run(): kernel(*(pltpu.with_memory_space_constraint(arg, pltpu.HBM) if i == 'H' e...]
    all_to_all x1, waiting for transfers between devices: 6.28 us -> 5.24 us  [per_device(): got = lax.all_to_all(sent, group, split_axis=0, concat_axis=0, tiled=True)]
  transfers between devices with their start and end apart: 4 -> 4, of which waited for: 2 -> 2; matrix products, arithmetic and copies ran while one was open for 0% -> 0% of each run, Pallas kernels for 15% -> 8%
where the time goes in v5:
time: 29.6 us; the launch traced here: 29.3 us
  starting transfers between devices  12 us (41%)
  waiting for transfers between devices  10.8 us (36%)
  Pallas kernels  5.67 us (19%)
  between operations  0.73 us (2%)
    all_to_all x1, starting transfers between devices, per_device(): got = lax.all_to_all(sent, group, split_axis=0, concat_axis=0, tiled=True)  7.4 us
    pallas_call x5, Pallas kernels, run(): kernel(*(pltpu.with_memory_space_constraint(arg, pltpu.HBM) if i == 'H' e...  5.67 us
    all_to_all x1, waiting for transfers between devices, per_device(): back = lax.all_to_all(back, group, split_axis=0, concat_axis=0, tiled=True)  5.57 us
    all_to_all x1, waiting for transfers between devices, per_device(): got = lax.all_to_all(sent, group, split_axis=0, concat_axis=0, tiled=True)  5.24 us
    all_to_all x1, starting transfers between devices, per_device(): back = lax.all_to_all(back, group, split_axis=0, concat_axis=0, tiled=True)  3.5 us
    ppermute x2, starting transfers between devices, per_device(): lax.ppermute(x_sent[i], axes_x, swap_pairs(x_size, i))  1.12 us
  transfers between devices with their start and end apart: 4, of which 2 were waited for; matrix products, arithmetic and copies ran while one was open for 0% of the time, Pallas kernels for 8%

profile of v5, /device:TPU:0, one launch (start us, length us, event | category | flops | bytes accessed | tf_op | source)
XLA Modules:
  0.0 29.3 jit_solution(6340284365073379905)
XLA Ops:
  0.6 2.2 %front.1 = (f32[16,8,128]{2,1,0:T(8,128)}, f32[50,16,128]{2,1,0:T(8,128)S(1)}, f32[50,16,128]{2,1,0:T(8,128)S(1)}, f32[50,16,128]{2,1,0:T(8,128)S(1)}, f32[50,16...) custom-call(s32[2,128]{1,0:T(2,128)} %bitcast.5, ...), custom_call_target="tpu_custom_call" | custom-call | flops 1000 | bytes 1000 | tf_op jit(solution)/shard_map/front/pallas_call | solution.py:327
  2.9 7.4 %all-to-all-start = ((f32[16,8,128]{2,1,0:T(8,128)}), f32[16,8,128]{2,1,0:T(8,128)S(1)}, u32[]{:S(2)}, u32[]{:S(2)}) async-start(f32[16,8,128]{2,1,0:T(8,128)} %get-tuple-element.17), calls=%async_computation | async-start | bytes 131072 | tf_op jit(solution)/shard_map/all_to_all | solution.py:396
  10.3 0.0 copy-start.1
  10.3 0.0 copy-start.2
  10.3 0.2 edge.1
  10.6 0.5 %collective-permute-start = (f32[100,128]{1,0:T(8,128)S(1)}, f32[100,128]{1,0:T(8,128)S(1)}, u32[]{:S(2)}, u32[]{:S(2)}) collective-permute-start(f32[100,128]{1,0:T(8,128)S(1)} %get-tuple-element.30.refs_10_), channel_id=1, source_target_pairs={{0,4},{4,0},{8,12},{12,8},{16,20},{20,16},{24,28},{28,24},{1,5},{5... | collective-permute-start | bytes 153608 | tf_op jit(solution)/shard_map/ppermute | solution.py:405
  11.0 0.7 %collective-permute-start.1 = (f32[100,128]{1,0:T(8,128)S(1)}, f32[100,128]{1,0:T(8,128)S(1)}, u32[]{:S(2)}, u32[]{:S(2)}) collective-permute-start(f32[100,128]{1,0:T(8,128)S(1)} %get-tuple-element.31.refs_11_), channel_id=1, source_target_pairs={{4,8},{8,4},{12,16},{16,12},{20,24},{24,20},{5,9},{9,5},{13,17},{1... | collective-permute-start | bytes 153608 | tf_op jit(solution)/shard_map/ppermute | solution.py:405
  11.7 5.2 %all-to-all-done.got = f32[16,8,128]{2,1,0:T(8,128)S(1)} async-done(((f32[16,8,128]{2,1,0:T(8,128)}), f32[16,8,128]{2,1,0:T(8,128)S(1)}, u32[]{:S(2)}, u32[]{:S(2)}) %all-to-all-start) | async-done | bytes 65568 | tf_op jit(solution)/shard_map/all_to_all | solution.py:396
  16.9 1.2 %pick.1 = (f32[16,8,128]{2,1,0:T(8,128)}, f32[2,16,128]{2,1,0:T(8,128)S(1)}, f32[2,8,128]{2,1,0:T(8,128)S(1)}) custom-call(f32[16,8,128]{2,1,0:T(8,128)S(1)} %all-to-all-done.got, bf16[160,128]{1,0:T(8,128)(2,1)S(1)} %get-tuple-element.18.sat, f32[16,128]{1,0:T(8,128)S(1)} %get-tuple-element.21.border.conds), custom_call_target="tpu_custom_call" | custom-call | flops 1000 | bytes 1000 | tf_op jit(solution)/shard_map/pick/pallas_call | solution.py:327
  18.1 3.5 %all-to-all-start.1 = ((f32[16,8,128]{2,1,0:T(8,128)}), f32[16,8,128]{2,1,0:T(8,128)S(1)}, u32[]{:S(2)}, u32[]{:S(2)}) async-start(f32[16,8,128]{2,1,0:T(8,128)} %get-tuple-element.22), calls=%async_computation.1 | async-start | bytes 131072 | tf_op jit(solution)/shard_map/all_to_all | solution.py:417
  21.6 0.0 collective-permute-done.refs_12_
  21.6 0.0 collective-permute-done.1.refs_13_
  21.6 0.0 copy-done.1
  21.7 0.0 copy-done.2
  21.7 0.0 copy-start
  21.7 0.9 %balance.1.partial = f32[50,16,128]{2,1,0:T(8,128)S(1)} custom-call(f32[50,16,128]{2,1,0:T(8,128)S(1)} %copy-done.1, f32[50,16,128]{2,1,0:T(8,128)S(1)} %copy-done.2, f32[50,16,128]{2,1,0:T(8,128)S(1)} %get-tuple-element.19.head.refs_2_, f32[50,16,128]{2,1,0:T(8,128)S(1)} %get-tuple-element.24.refs_3_, f32[50,16,128]{2,1,0:T(8,128)S(1)} %get-tuple-element.20.conduct.refs_4_, ...), custom_call_target="tpu_custom_call" | custom-call | flops 1000000000 | bytes 3000000 | tf_op jit(solution)/shard_map/balance/pallas_call | solution.py:327
  22.6 5.6 %all-to-all-done.1.back = f32[16,8,128]{2,1,0:T(8,128)S(1)} async-done(((f32[16,8,128]{2,1,0:T(8,128)}), f32[16,8,128]{2,1,0:T(8,128)S(1)}, u32[]{:S(2)}, u32[]{:S(2)}) %all-to-all-start.1) | async-done | bytes 65568 | tf_op jit(solution)/shard_map/all_to_all | solution.py:417
  28.2 0.0 copy-done
  28.2 1.1 %last.1 = (f32[50,16,128]{2,1,0:T(8,128)}, f32[10,256]{1,0:T(8,128)}) custom-call(f32[16,8,128]{2,1,0:T(8,128)S(1)} %all-to-all-done.1.back, f32[16,8,128]{2,1,0:T(8,128)S(1)} %all-to-all-done.got, f32[16,128]{1,0:T(8,128)S(1)} %get-tuple-element.23.heads, f32[16,128]{1,0:T(8,128)S(1)} %get-tuple-element.21.border.conds, f32[50,16,128]{2,1,0:T(8,128)S(1)} %balance.1.partial, ...), custom_call_target="tpu_custom_call" | custom-call | flops 1000 | bytes 1000 | tf_op jit(solution)/shard_map/last/pallas_call | solution.py:327
Async XLA Ops:
  2.9 14.0 %all-to-all-start = ((f32[16,8,128]{2,1,0:T(8,128)}), f32[16,8,128]{2,1,0:T(8,128)S(1)}, u32[]{:S(2)}, u32[]{:S(2)}) async-start(f32[16,8,128]{2,1,0:T(8,128)} %get-tuple-element.17), calls=%async_computation | async-start | bytes 131072 | tf_op jit(solution)/shard_map/all_to_all | solution.py:396
  10.3 11.4 %copy-start.1 = (f32[50,16,128]{2,1,0:T(8,128)S(1)}, f32[50,16,128]{2,1,0:T(8,128)}, u32[]{:S(2)}) copy-start(f32[50,16,128]{2,1,0:T(8,128)} %refs_0_.1) | copy-start | bytes 1228804
  10.3 11.4 %copy-start.2 = (f32[50,16,128]{2,1,0:T(8,128)S(1)}, f32[50,16,128]{2,1,0:T(8,128)}, u32[]{:S(2)}) copy-start(f32[50,16,128]{2,1,0:T(8,128)} %refs_1_.1) | copy-start | bytes 1228804
  10.6 11.1 %collective-permute-start = (f32[100,128]{1,0:T(8,128)S(1)}, f32[100,128]{1,0:T(8,128)S(1)}, u32[]{:S(2)}, u32[]{:S(2)}) collective-permute-start(f32[100,128]{1,0:T(8,128)S(1)} %get-tuple-element.30.refs_10_), channel_id=1, source_target_pairs={{0,4},{4,0},{8,12},{12,8},{16,20},{20,16},{24,28},{28,24},{1,5},{5... | collective-permute-start | bytes 153608 | tf_op jit(solution)/shard_map/ppermute | solution.py:405
  11.0 10.6 %collective-permute-start.1 = (f32[100,128]{1,0:T(8,128)S(1)}, f32[100,128]{1,0:T(8,128)S(1)}, u32[]{:S(2)}, u32[]{:S(2)}) collective-permute-start(f32[100,128]{1,0:T(8,128)S(1)} %get-tuple-element.31.refs_11_), channel_id=1, source_target_pairs={{4,8},{8,4},{12,16},{16,12},{20,24},{24,20},{5,9},{9,5},{13,17},{1... | collective-permute-start | bytes 153608 | tf_op jit(solution)/shard_map/ppermute | solution.py:405
  18.1 10.1 %all-to-all-start.1 = ((f32[16,8,128]{2,1,0:T(8,128)}), f32[16,8,128]{2,1,0:T(8,128)S(1)}, u32[]{:S(2)}, u32[]{:S(2)}) async-start(f32[16,8,128]{2,1,0:T(8,128)} %get-tuple-element.22), calls=%async_computation.1 | async-start | bytes 131072 | tf_op jit(solution)/shard_map/all_to_all | solution.py:417
  21.7 6.5 %copy-start = (f32[10,256]{1,0:T(8,128)S(1)}, f32[10,256]{1,0:T(8,128)}, u32[]{:S(2)}) copy-start(f32[10,256]{1,0:T(8,128)} %nitrate.1) | copy-start | bytes 30724

commit v6 on v5

--- a/solution.py
+++ b/solution.py
@@ -106,8 +106,8 @@
 
 def front_kernel(top, *refs):
     fields, grids, extra = refs[:4], refs[4:7], refs[7:9]
-    sent, head, alpha, conduct, wet_out, sat, border_out = refs[9:16]
-    extra_out, (fields_in, perm, sent_in, small_sems, sems, sent_sem) = refs[16:18], refs[18:]
+    sent, head, alpha, conduct, wet_out, sat, head_border, cond_border = refs[9:17]
+    extra_out, (fields_in, perm, small_sems, sems) = refs[17:19], refs[19:]
     layers, width_x, width_y = head.shape
     small = [pltpu.make_async_copy(fields[i], fields_in[i], small_sems.at[i]) for i in range(4)]
     extras = [pltpu.make_async_copy(extra[i], extra_out[i], small_sems.at[4 + i]) for i in range(2)]
@@ -121,25 +121,19 @@
                 for j, (source, target) in enumerate(zip(grids, (head, alpha, perm)))
             ]
         )
-    for copy in (*small, *(copies[j] for j in range(3) for copies in large), *extras):
+    for copy in (*small, *(copy for copies in large for copy in copies), *extras):
         copy.start()
     for copy in small:
         copy.wait()
     for bank in range(fields_in[0].shape[0]):
         rows = [ref[bank : bank + 1, :].astype(jnp.float32) for ref in fields_in]
         rows.append(jnp.zeros((4, LANES), jnp.float32))
-        pack_blocks(jnp.concatenate(rows, axis=0), 4, sent_in, bank)
-    border = jnp.zeros((width_x, width_y), jnp.float32)
-    for i, (start, stop) in enumerate(parts):
-        large[i][0].wait()
-        border = border_of(head, start, stop, border)
-    border_out[...] = border
-    add_border(sent_in, border)
-    send = pltpu.make_async_copy(sent_in, sent, sent_sem)
-    send.start()
-    for i, (start, stop) in enumerate(parts):
-        large[i][1].wait()
-        large[i][2].wait()
+        pack_blocks(jnp.concatenate(rows, axis=0), 4, sent, bank)
+    heads = jnp.zeros((width_x, width_y), jnp.float32)
+    conds = jnp.zeros((width_x, width_y), jnp.float32)
+    for copies, (start, stop) in zip(large, parts):
+        for copy in copies:
+            copy.wait()
         part = slice(start, stop)
         wet = saturation(head[part], alpha[part])
         conduct[part] = perm[part] * wet * wet * wet
@@ -148,14 +142,17 @@
             last = min(stop, top)
             kept = wet[: last - start].reshape((last - start) * width_x, width_y)
             sat[start * width_x : last * width_x, :] = kept.astype(jnp.bfloat16)
-    for copy in (*extras, send):
+        heads = border_of(head, start, stop, heads)
+        conds = border_of(conduct, start, stop, conds)
+    head_border[...] = heads
+    cond_border[...] = conds
+    add_border(sent, heads)
+    for copy in extras:
         copy.wait()
 
 
-def edge_kernel(axes_x, head, conduct, x_first, x_second, border_out):
+def edge_kernel(axes_x, head, conduct, order, x_first, x_second):
     layers, width_x, width_y = head.shape
-    border = jnp.zeros((width_x, width_y), jnp.float32)
-    border_out[...] = border_of(conduct, 0, layers, border)
     even = place_of(axes_x) % 2 == 0
     for field, ref in enumerate((head, conduct)):
         rows = slice(field * layers, (field + 1) * layers)
@@ -218,28 +215,13 @@
     return total
 
 
-def balance_kernel(top, axes_x, *refs):
-    head_old, porosity = refs[:2]
-    head, alpha, conduct, wet, fields, patch_sat, root_decay, land = refs[2:10]
-    x_sent, x_got, out = refs[10:12], refs[12:14], refs[14]
-    x_faces = refs[15]
+def interior_kernel(top, *refs):
+    head_old, porosity, head, alpha, conduct, wet = refs[:6]
+    fields, patch_sat, root_decay, land, order, out = refs[6:]
     layers, width_x, width_y = head.shape
-    parts = parts_of(layers)
     sources = column_sources(top, width_x, width_y, fields, patch_sat, root_decay)
     sources = sources.reshape(top, width_x, width_y) * land[...].astype(jnp.float32)[None]
-
-    even = place_of(axes_x) % 2 == 0
-    faces = []
-    for rows in (slice(0, layers), slice(layers, 2 * layers)):
-        first, second = (r[rows, :] for r in x_sent)
-        low, high = jnp.where(even, second, first), jnp.where(even, first, second)
-        first, second = (r[rows, :] for r in x_got)
-        before, after = jnp.where(even, second, first), jnp.where(even, first, second)
-        faces.append((low, high, before, after))
-    heads, conds = faces
-    x_faces[0] = 0.5 * (conds[2] + conds[0]) * (heads[2] - heads[0])
-    x_faces[1] = 0.5 * (conds[1] + conds[3]) * (heads[1] - heads[3])
-    for i, (start, stop) in enumerate(parts):
+    for start, stop in parts_of(layers):
         shape = (stop - start, width_x, width_y)
         part, cond = head[start:stop], conduct[start:stop]
         row, lane = iota(shape, 1), iota(shape, 2)
@@ -261,27 +243,42 @@
         if stop == layers:
             down = jnp.concatenate([down, cond[-1:]], 0)
         total = total + (down[1:] - down[:-1])
-        row = row[0]
-        for k in range(start, stop):
-            edge = jnp.where(row == 0, -x_faces[0, k : k + 1, :], 0.0)
-            edge = edge + jnp.where(row == width_x - 1, x_faces[1, k : k + 1, :], 0.0)
-            one = total[k - start] + edge
-            out[k] = one - sources[k] if k < top else one
-
-
-def last_kernel(back, got, heads, conds, partial, nitrate, residual, nitrate_out, out, value_out, sems):
+        if start < top:
+            last = min(stop, top)
+            own = total[: last - start] - sources[start:last]
+            total = jnp.concatenate([own, total[last - start :]], 0) if last < stop else own
+        out[start:stop] = total
+
+
+def last_kernel(axes_x, *refs):
+    back, got, y_heads, y_conds, partial, nitrate = refs[:6]
+    x_sent, x_got = refs[6:8], refs[8:10]
+    residual, nitrate_out, out, value_out, x_faces, sems = refs[10:]
     layers, width_x, width_y = partial.shape
     top = nitrate.shape[0]
-    head, cond = heads[...], conds[...]
-    flux = 0.5 * (cond + neighbour_borders(back)) * (head - neighbour_borders(got))
-    lane = iota(flux.shape, 1)
+    even = place_of(axes_x) % 2 == 0
+    faces = []
+    for rows in (slice(0, layers), slice(layers, 2 * layers)):
+        first, second = (r[rows, :] for r in x_sent)
+        low, high = jnp.where(even, second, first), jnp.where(even, first, second)
+        first, second = (r[rows, :] for r in x_got)
+        before, after = jnp.where(even, second, first), jnp.where(even, first, second)
+        faces.append((low, high, before, after))
+    heads, conds = faces
+    x_faces[0] = 0.5 * (conds[0] + conds[2]) * (heads[0] - heads[2])
+    x_faces[1] = 0.5 * (conds[1] + conds[3]) * (heads[1] - heads[3])
+    flux = 0.5 * (y_conds[...] + neighbour_borders(back)) * (y_heads[...] - neighbour_borders(got))
+    row, lane = iota(flux.shape, 0), iota(flux.shape, 1)
     on_border = (lane == 0) | (lane == width_y - 1)
     parts = parts_of(layers, 2 * CHUNK)
     writes = []
     for i, (start, stop) in enumerate(parts):
         for k in range(start, stop):
             edge = pltpu.roll(flux, width_y - 1 - 2 * k, 1)
-            out[k] = partial[k] + jnp.where(on_border, edge, 0.0)
+            one = partial[k] + jnp.where(on_border, edge, 0.0)
+            one = one + jnp.where(row == 0, x_faces[0, k : k + 1, :], 0.0)
+            one = one + jnp.where(row == width_x - 1, x_faces[1, k : k + 1, :], 0.0)
+            out[k] = one
         rows = pl.ds(start, stop - start)
         copy = pltpu.make_async_copy(out.at[rows], residual.at[rows], sems.at[i])
         copy.start()
@@ -320,7 +317,7 @@
         scratch_shapes=scratch,
         name=name,
         compiler_params=pltpu.CompilerParams(vmem_limit_bytes=VMEM_LIMIT),
-        cost_estimate=pl.CostEstimate(flops=1000000000 if cost>1000 else 1000, bytes_accessed=cost, transcendentals=0),
+        cost_estimate=pl.CostEstimate(flops=cost, bytes_accessed=cost, transcendentals=0),
     )
 
     def run(*args):
@@ -369,17 +366,18 @@
 
     flat = [v.reshape(banks, LANES) for v in (patch_column, crop_type, patch_weight, rain)]
     x_edge = shape((2 * layers, width_y), f32)
-    sent, head, alpha, conduct, wet, sat, head_border, land, table = call(
+    sent, head, alpha, conduct, wet, sat, head_border, cond_border, land, table = call(
         functools.partial(front_kernel, top),
         "front",
         "HHHHHHHHH",
         (
-            (blocks, "H"),
+            (blocks, "V"),
             (field, "V"),
             (field, "V"),
             (field, "V"),
             (field, "V"),
             (shape((top * width_x, width_y), jnp.bfloat16), "V"),
+            (border, "V"),
             (border, "V"),
             (shape((width_x, width_y), land_mask.dtype), "V"),
             (shape((1, root_decay.shape[0]), f32), "V"),
@@ -387,23 +385,11 @@
         (
             [pltpu.VMEM((banks, LANES), v.dtype) for v in flat],
             field_in,
-            pltpu.VMEM((owners, half, LANES), f32),
             dma((6,)),
             dma((len(parts_of(layers, FRONT_CHUNK)), 3)),
-            dma,
         ),
     )(*flat, pressure, vg_alpha, conductivity, land_mask, root_decay.reshape(1, -1))
     got = lax.all_to_all(sent, group, split_axis=0, concat_axis=0, tiled=True)
-    *x_sent, cond_border = call(
-        functools.partial(edge_kernel, axes_x),
-        "edge",
-        "VV",
-        ((x_edge, "V"), (x_edge, "V"), (border, "V")),
-    )(head, conduct)
-
-    x_size = lax.axis_size(axes_x)
-    x_got = [lax.ppermute(x_sent[i], axes_x, swap_pairs(x_size, i)) for i in (0, 1)]
-
     back, patch_sat, fields = call(
         functools.partial(pick_kernel, top, width_x),
         "pick",
@@ -416,24 +402,32 @@
     )(got, sat, cond_border)
     back = lax.all_to_all(back, group, split_axis=0, concat_axis=0, tiled=True)
 
+    x_sent = call(
+        functools.partial(edge_kernel, axes_x), "edge", "VVV", ((x_edge, "V"), (x_edge, "V"))
+    )(head, conduct, patch_sat)
+    x_size = lax.axis_size(axes_x)
+    x_got = [lax.ppermute(x_sent[i], axes_x, swap_pairs(x_size, i)) for i in (0, 1)]
     (partial,) = call(
-        functools.partial(balance_kernel, top, axes_x),
-        "balance",
-        "VVVVVVVVVVVVVV",
-        ((field, "V"),),
-        (pltpu.VMEM((2, layers, width_y), f32),),
-        cost=3000000,
+        functools.partial(interior_kernel, top), "interior", "VVVVVVVVVVV", ((field, "V"),)
     )(
-        pressure_old, porosity, head, alpha, conduct, wet, fields, patch_sat,
-        table, land, *x_sent, *x_got,
+        pressure_old, porosity, head, alpha, conduct, wet, fields, patch_sat, table, land,
+        x_sent[0],
     )
+
     residual, nitrate_out = call(
-        last_kernel,
+        functools.partial(last_kernel, axes_x),
         "last",
-        "VVVVVV",
+        "VVVVVVVVVV",
         ((field, "H"), (shape((top, slots), f32), "H")),
-        (field_in, pltpu.VMEM((top, slots), f32), dma((halves + 1,))),
-    )(back, got, head_border, cond_border, partial, nitrate)
+        (
+            field_in,
+            pltpu.VMEM((top, slots), f32),
+            pltpu.VMEM((2, layers, width_y), f32),
+            dma((halves + 1,)),
+        ),
+    )(
+        back, got, head_border, cond_border, partial, nitrate, *x_sent, *x_got,
+    )
     return (residual, nitrate_out)
 
 

time: 29.6 us -> 28.9 us (0.976)
  blocking collectives: 0 us -> 13.8 us
  waiting for transfers between devices: 10.8 us -> 1.44 us
  starting transfers between devices: 12 us -> 7.57 us
  Pallas kernels: 5.67 us -> 5.13 us
    all_to_all x0 -> x1, blocking collectives: none -> 13.8 us  [per_device(): got = lax.all_to_all(sent, group, split_axis=0, concat_axis=0, tiled=True)]
    all_to_all x1 -> x0, starting transfers between devices: 7.4 us -> none  [per_device(): got = lax.all_to_all(sent, group, split_axis=0, concat_axis=0, tiled=True)]
    all_to_all x1 -> x0, waiting for transfers between devices: 5.24 us -> none  [per_device(): got = lax.all_to_all(sent, group, split_axis=0, concat_axis=0, tiled=True)]
    all_to_all x1, waiting for transfers between devices: 5.57 us -> 1.44 us  [per_device(): back = lax.all_to_all(back, group, split_axis=0, concat_axis=0, tiled=True)]
    ppermute x2, starting transfers between devices: 1.12 us -> 4.07 us  [per_device(): lax.ppermute(x_sent[i], axes_x, swap_pairs(x_size, i))]
    pallas_call x5, Pallas kernels: 5.67 us -> 5.13 us  [run(): kernel(*(pltpu.with_memory_space_constraint(arg, pltpu.HBM) if i == 'H' e...]
  transfers between devices with their start and end apart: 4 -> 3, of which waited for: 2 -> 1; matrix products, arithmetic and copies ran while one was open for 0% -> 0% of each run, Pallas kernels for 8% -> 3%
where the time goes in v6:
time: 28.9 us; the launch traced here: 28.6 us
  blocking collectives  13.8 us (48%)
  starting transfers between devices  7.57 us (26%)
  Pallas kernels  5.13 us (18%)
  waiting for transfers between devices  1.44 us (5%)
  between operations  0.71 us (2%)
    all_to_all x1, blocking collectives, per_device(): got = lax.all_to_all(sent, group, split_axis=0, concat_axis=0, tiled=True)  13.8 us
    pallas_call x5, Pallas kernels, run(): kernel(*(pltpu.with_memory_space_constraint(arg, pltpu.HBM) if i == 'H' e...  5.13 us
    ppermute x2, starting transfers between devices, per_device(): lax.ppermute(x_sent[i], axes_x, swap_pairs(x_size, i))  4.07 us
    all_to_all x1, starting transfers between devices, per_device(): back = lax.all_to_all(back, group, split_axis=0, concat_axis=0, tiled=True)  3.5 us
    all_to_all x1, waiting for transfers between devices, per_device(): back = lax.all_to_all(back, group, split_axis=0, concat_axis=0, tiled=True)  1.44 us
  transfers between devices with their start and end apart: 3, of which 1 were waited for; matrix products, arithmetic and copies ran while one was open for 0% of the time, Pallas kernels for 3%

profile of v6, /device:TPU:0, one launch (start us, length us, event | category | flops | bytes accessed | tf_op | source)
XLA Modules:
  0.0 28.6 jit_solution(236421475671389604)
XLA Ops:
  0.6 1.9 %front.1 = (f32[16,8,128]{2,1,0:T(8,128)S(1)}, f32[50,16,128]{2,1,0:T(8,128)S(1)}, f32[50,16,128]{2,1,0:T(8,128)S(1)}, f32[50,16,128]{2,1,0:T(8,128)S(1)}, f32[5...) custom-call(s32[2,128]{1,0:T(2,128)} %bitcast.5, ...), custom_call_target="tpu_custom_call" | custom-call | flops 1000 | bytes 1000 | tf_op jit(solution)/shard_map/front/pallas_call | solution.py:324
  2.5 13.8 %all_to_all.10.got.refs_1_ = f32[16,8,128]{2,1,0:T(8,128)S(1)} all-to-all(f32[16,8,128]{2,1,0:T(8,128)S(1)} %get-tuple-element.17), channel_id=1, replica_groups=mesh['sec'=2,'gx'=4,'gy'=4] {'gx','gy'}, dimensions={0} | all-to-all | bytes 131072 | tf_op jit(solution)/shard_map/all_to_all | solution.py:392
  16.3 1.2 %pick.1 = (f32[16,8,128]{2,1,0:T(8,128)}, f32[2,16,128]{2,1,0:T(8,128)S(1)}, f32[2,8,128]{2,1,0:T(8,128)S(1)}) custom-call(f32[16,8,128]{2,1,0:T(8,128)S(1)} %all_to_all.10.got.refs_1_, bf16[160,128]{1,0:T(8,128)(2,1)S(1)} %get-tuple-element.18.sat, f32[16,128]{1,0:T(8,128)S(1)} %get-tuple-element.19.border.refs_3_), custom_call_target="tpu_custom_call" | custom-call | flops 1000 | bytes 1000 | tf_op jit(solution)/shard_map/pick/pallas_call | solution.py:324
  17.5 3.5 %all-to-all-start.1 = ((f32[16,8,128]{2,1,0:T(8,128)}), f32[16,8,128]{2,1,0:T(8,128)S(1)}, u32[]{:S(2)}, u32[]{:S(2)}) async-start(f32[16,8,128]{2,1,0:T(8,128)} %get-tuple-element.20), calls=%async_computation.1 | async-start | bytes 131072 | tf_op jit(solution)/shard_map/all_to_all | solution.py:403
  21.0 0.0 copy-start
  21.0 0.0 copy-start.1
  21.0 0.1 edge.1
  21.1 0.8 %collective-permute-start.1 = (f32[100,128]{1,0:T(8,128)S(1)}, f32[100,128]{1,0:T(8,128)S(1)}, u32[]{:S(2)}, u32[]{:S(2)}) collective-permute-start(f32[100,128]{1,0:T(8,128)S(1)} %get-tuple-element.31.refs_7_), channel_id=1, source_target_pairs={{4,8},{8,4},{12,16},{16,12},{20,24},{24,20},{5,9},{9,5},{13,17},{1... | collective-permute-start | bytes 153608 | tf_op jit(solution)/shard_map/ppermute | solution.py:409
  21.9 3.3 %collective-permute-start = (f32[100,128]{1,0:T(8,128)S(1)}, f32[100,128]{1,0:T(8,128)S(1)}, u32[]{:S(2)}, u32[]{:S(2)}) collective-permute-start(f32[100,128]{1,0:T(8,128)S(1)} %get-tuple-element.30.refs_10_.refs_6_), channel_id=1, source_target_pairs={{0,4},{4,0},{8,12},{12,8},{16,20},{20,16},{24,28},{28,24},{1,5},{5... | collective-permute-start | bytes 153608 | tf_op jit(solution)/shard_map/ppermute | solution.py:409
  25.2 0.0 copy-done
  25.2 0.0 copy-done.1
  25.2 0.0 copy-start.2
  25.2 0.9 %interior.1.refs_4_ = f32[50,16,128]{2,1,0:T(8,128)S(1)} custom-call(f32[50,16,128]{2,1,0:T(8,128)S(1)} %copy-done, f32[50,16,128]{2,1,0:T(8,128)S(1)} %copy-done.1, f32[50,16,128]{2,1,0:T(8,128)S(1)} %get-tuple-element.22.head.refs_2_, f32[50,16,128]{2,1,0:T(8,128)S(1)} %get-tuple-element.23.refs_3_, f32[50,16,128]{2,1,0:T(8,128)S(1)} %get-tuple-element.24.conduct.refs_4_, ...), custom_call_target="tpu_custom_call" | custom-call | flops 1000 | bytes 1000 | tf_op jit(solution)/shard_map/interior/pallas_call | solution.py:324
  26.1 0.0 collective-permute-done.1.refs_9_
  26.1 0.0 collective-permute-done.refs_8_
  26.1 1.4 %all-to-all-done.1.refs_0_ = f32[16,8,128]{2,1,0:T(8,128)S(1)} async-done(((f32[16,8,128]{2,1,0:T(8,128)}), f32[16,8,128]{2,1,0:T(8,128)S(1)}, u32[]{:S(2)}, u32[]{:S(2)}) %all-to-all-start.1) | async-done | bytes 65568 | tf_op jit(solution)/shard_map/all_to_all | solution.py:403
  27.5 0.0 copy-done.2
  27.6 1.1 %last.1 = (f32[50,16,128]{2,1,0:T(8,128)}, f32[10,256]{1,0:T(8,128)}) custom-call(f32[16,8,128]{2,1,0:T(8,128)S(1)} %all-to-all-done.1.refs_0_, f32[16,8,128]{2,1,0:T(8,128)S(1)} %all_to_all.10.got.refs_1_, f32[16,128]{1,0:T(8,128)S(1)} %get-tuple-element.21.refs_2_, f32[16,128]{1,0:T(8,128)S(1)} %get-tuple-element.19.border.refs_3_, ...), custom_call_target="tpu_custom_call" | custom-call | flops 1000 | bytes 1000 | tf_op jit(solution)/shard_map/last/pallas_call | solution.py:324
Async XLA Ops:
  17.5 10.1 %all-to-all-start.1 = ((f32[16,8,128]{2,1,0:T(8,128)}), f32[16,8,128]{2,1,0:T(8,128)S(1)}, u32[]{:S(2)}, u32[]{:S(2)}) async-start(f32[16,8,128]{2,1,0:T(8,128)} %get-tuple-element.20), calls=%async_computation.1 | async-start | bytes 131072 | tf_op jit(solution)/shard_map/all_to_all | solution.py:403
  21.0 4.2 %copy-start = (f32[50,16,128]{2,1,0:T(8,128)S(1)}, f32[50,16,128]{2,1,0:T(8,128)}, u32[]{:S(2)}) copy-start(f32[50,16,128]{2,1,0:T(8,128)} %refs_0_.1) | copy-start | bytes 1228804
  21.0 4.2 %copy-start.1 = (f32[50,16,128]{2,1,0:T(8,128)S(1)}, f32[50,16,128]{2,1,0:T(8,128)}, u32[]{:S(2)}) copy-start(f32[50,16,128]{2,1,0:T(8,128)} %refs_1_.1) | copy-start | bytes 1228804
  21.1 5.0 %collective-permute-start.1 = (f32[100,128]{1,0:T(8,128)S(1)}, f32[100,128]{1,0:T(8,128)S(1)}, u32[]{:S(2)}, u32[]{:S(2)}) collective-permute-start(f32[100,128]{1,0:T(8,128)S(1)} %get-tuple-element.31.refs_7_), channel_id=1, source_target_pairs={{4,8},{8,4},{12,16},{16,12},{20,24},{24,20},{5,9},{9,5},{13,17},{1... | collective-permute-start | bytes 153608 | tf_op jit(solution)/shard_map/ppermute | solution.py:409
  21.9 4.2 %collective-permute-start = (f32[100,128]{1,0:T(8,128)S(1)}, f32[100,128]{1,0:T(8,128)S(1)}, u32[]{:S(2)}, u32[]{:S(2)}) collective-permute-start(f32[100,128]{1,0:T(8,128)S(1)} %get-tuple-element.30.refs_10_.refs_6_), channel_id=1, source_target_pairs={{0,4},{4,0},{8,12},{12,8},{16,20},{20,16},{24,28},{28,24},{1,5},{5... | collective-permute-start | bytes 153608 | tf_op jit(solution)/shard_map/ppermute | solution.py:409
  25.2 2.4 %copy-start.2 = (f32[10,256]{1,0:T(8,128)S(1)}, f32[10,256]{1,0:T(8,128)}, u32[]{:S(2)}) copy-start(f32[10,256]{1,0:T(8,128)} %refs_5_.3) | copy-start | bytes 30724

commit v7 on v6

--- a/solution.py
+++ b/solution.py
@@ -104,10 +104,10 @@
     return turned[FIELD_LANE : FIELD_LANE + height]
 
 
-def front_kernel(top, *refs):
-    fields, grids, extra = refs[:4], refs[4:7], refs[7:9]
-    sent, head, alpha, conduct, wet_out, sat, head_border, cond_border = refs[9:17]
-    extra_out, (fields_in, perm, small_sems, sems) = refs[17:19], refs[19:]
+def front_kernel(*refs):
+    fields, grid, extra = refs[:4], refs[4], refs[5:7]
+    sent, head, head_border, *extra_out = refs[7:12]
+    fields_in, small_sems, sems = refs[12:]
     layers, width_x, width_y = head.shape
     small = [pltpu.make_async_copy(fields[i], fields_in[i], small_sems.at[i]) for i in range(4)]
     extras = [pltpu.make_async_copy(extra[i], extra_out[i], small_sems.at[4 + i]) for i in range(2)]
@@ -115,13 +115,8 @@
     large = []
     for i, (start, stop) in enumerate(parts):
         rows = pl.ds(start, stop - start)
-        large.append(
-            [
-                pltpu.make_async_copy(source.at[rows], target.at[rows], sems.at[i, j])
-                for j, (source, target) in enumerate(zip(grids, (head, alpha, perm)))
-            ]
-        )
-    for copy in (*small, *(copy for copies in large for copy in copies), *extras):
+        large.append(pltpu.make_async_copy(grid.at[rows], head.at[rows], sems.at[i]))
+    for copy in (*small, *large, *extras):
         copy.start()
     for copy in small:
         copy.wait()
@@ -130,29 +125,22 @@
         rows.append(jnp.zeros((4, LANES), jnp.float32))
         pack_blocks(jnp.concatenate(rows, axis=0), 4, sent, bank)
     heads = jnp.zeros((width_x, width_y), jnp.float32)
-    conds = jnp.zeros((width_x, width_y), jnp.float32)
-    for copies, (start, stop) in zip(large, parts):
-        for copy in copies:
-            copy.wait()
+    for copy, (start, stop) in zip(large, parts):
+        copy.wait()
+        heads = border_of(head, start, stop, heads)
+    head_border[...] = heads
+    add_border(sent, heads)
+    for copy in extras:
+        copy.wait()
+
+
+def edge_kernel(axes_x, head, alpha, perm, order, x_first, x_second, conduct, wet_out):
+    layers, width_x, width_y = head.shape
+    for start, stop in parts_of(layers):
         part = slice(start, stop)
         wet = saturation(head[part], alpha[part])
         conduct[part] = perm[part] * wet * wet * wet
         wet_out[part] = wet
-        if start < top:
-            last = min(stop, top)
-            kept = wet[: last - start].reshape((last - start) * width_x, width_y)
-            sat[start * width_x : last * width_x, :] = kept.astype(jnp.bfloat16)
-        heads = border_of(head, start, stop, heads)
-        conds = border_of(conduct, start, stop, conds)
-    head_border[...] = heads
-    cond_border[...] = conds
-    add_border(sent, heads)
-    for copy in extras:
-        copy.wait()
-
-
-def edge_kernel(axes_x, head, conduct, order, x_first, x_second):
-    layers, width_x, width_y = head.shape
     even = place_of(axes_x) % 2 == 0
     for field, ref in enumerate((head, conduct)):
         rows = slice(field * layers, (field + 1) * layers)
@@ -165,15 +153,20 @@
     return iota((size, LANES), 0) == ids
 
 
-def pick_kernel(top, width_x, got, sat, border, back, patch_sat, fields):
-    width_y = sat.shape[1]
+def pick_kernel(top, got, head, alpha, perm, head_border, back, patch_sat, fields, cond_border):
+    layers, width_x, width_y = head.shape
+    sat = saturation(head[:top], alpha[:top]).reshape(top * width_x, width_y).astype(jnp.bfloat16)
+    zero = jnp.zeros((width_x, width_y), jnp.float32)
+    wet = saturation(head_border[...], border_of(alpha, 0, layers, zero))
+    border = border_of(perm, 0, layers, zero) * wet * wet * wet
+    cond_border[...] = border
     for bank in range(fields.shape[0]):
         rows = unpack_blocks(got, 4, bank, 8)
         fields[bank] = rows
         ids = rows[0:1].astype(jnp.int32)
         lane_hot = hot(lax.rem(ids, width_y), width_y).astype(jnp.float32).astype(jnp.bfloat16)
         row_hot = hot(lax.div(ids, width_y), width_x)
-        picked = jnp.dot(sat[...], lane_hot, preferred_element_type=jnp.float32)
+        picked = jnp.dot(sat, lane_hot, preferred_element_type=jnp.float32)
         patch_sat[bank] = jnp.zeros(patch_sat.shape[1:], jnp.float32)
         for k in range(top):
             one = picked[k * width_x : (k + 1) * width_x]
@@ -181,7 +174,7 @@
                 jnp.where(row_hot, one, 0.0), axis=0, keepdims=True
             )
         pack_blocks(patch_sat[bank], top, back, bank)
-    add_border(back, border[...])
+    add_border(back, border)
 
 
 def column_sources(top, width_x, width_y, fields, patch_sat, root_decay):
@@ -366,51 +359,50 @@
 
     flat = [v.reshape(banks, LANES) for v in (patch_column, crop_type, patch_weight, rain)]
     x_edge = shape((2 * layers, width_y), f32)
-    sent, head, alpha, conduct, wet, sat, head_border, cond_border, land, table = call(
-        functools.partial(front_kernel, top),
+    sent, head, head_border, table, land = call(
+        front_kernel,
         "front",
-        "HHHHHHHHH",
+        "HHHHHHH",
         (
             (blocks, "V"),
             (field, "V"),
-            (field, "V"),
-            (field, "V"),
-            (field, "V"),
-            (shape((top * width_x, width_y), jnp.bfloat16), "V"),
             (border, "V"),
-            (border, "V"),
+            (shape((1, root_decay.shape[0]), f32), "V"),
             (shape((width_x, width_y), land_mask.dtype), "V"),
-            (shape((1, root_decay.shape[0]), f32), "V"),
         ),
         (
             [pltpu.VMEM((banks, LANES), v.dtype) for v in flat],
-            field_in,
             dma((6,)),
-            dma((len(parts_of(layers, FRONT_CHUNK)), 3)),
+            dma((len(parts_of(layers, FRONT_CHUNK)),)),
         ),
-    )(*flat, pressure, vg_alpha, conductivity, land_mask, root_decay.reshape(1, -1))
+        cost=1000000000,
+    )(*flat, pressure, root_decay.reshape(1, -1), land_mask)
     got = lax.all_to_all(sent, group, split_axis=0, concat_axis=0, tiled=True)
-    back, patch_sat, fields = call(
-        functools.partial(pick_kernel, top, width_x),
+    back, patch_sat, fields, cond_border = call(
+        functools.partial(pick_kernel, top),
         "pick",
-        "VVV",
+        "VVVVV",
         (
             (blocks, "V"),
             (shape((banks, 16, LANES), f32), "V"),
             (shape((banks, 8, LANES), f32), "V"),
+            (border, "V"),
         ),
-    )(got, sat, cond_border)
+    )(got, head, vg_alpha, conductivity, head_border)
     back = lax.all_to_all(back, group, split_axis=0, concat_axis=0, tiled=True)
 
-    x_sent = call(
-        functools.partial(edge_kernel, axes_x), "edge", "VVV", ((x_edge, "V"), (x_edge, "V"))
-    )(head, conduct, patch_sat)
+    *x_sent, conduct, wet = call(
+        functools.partial(edge_kernel, axes_x),
+        "edge",
+        "VVVV",
+        ((x_edge, "V"), (x_edge, "V"), (field, "V"), (field, "V")),
+    )(head, vg_alpha, conductivity, patch_sat)
     x_size = lax.axis_size(axes_x)
     x_got = [lax.ppermute(x_sent[i], axes_x, swap_pairs(x_size, i)) for i in (0, 1)]
     (partial,) = call(
         functools.partial(interior_kernel, top), "interior", "VVVVVVVVVVV", ((field, "V"),)
     )(
-        pressure_old, porosity, head, alpha, conduct, wet, fields, patch_sat, table, land,
+        pressure_old, porosity, head, vg_alpha, conduct, wet, fields, patch_sat, table, land,
         x_sent[0],
     )
 

time: 28.9 us -> 28.6 us (0.990)
  transfers between devices with their start and end apart: 3 -> 3, of which waited for: 1 -> 1; matrix products, arithmetic and copies ran while one was open for 0% -> 0% of each run, Pallas kernels for 3% -> 5%
where the time goes in v7:
time: 28.6 us; the launch traced here: 28.3 us
  blocking collectives  13.8 us (48%)
  starting transfers between devices  7.44 us (26%)
  Pallas kernels  5.08 us (18%)
  waiting for transfers between devices  1.23 us (4%)
  between operations  0.72 us (3%)
    all_to_all x1, blocking collectives, per_device(): got = lax.all_to_all(sent, group, split_axis=0, concat_axis=0, tiled=True)  13.8 us
    pallas_call x5, Pallas kernels, run(): kernel(*(pltpu.with_memory_space_constraint(arg, pltpu.HBM) if i == 'H' e...  5.08 us
    ppermute x2, starting transfers between devices, per_device(): lax.ppermute(x_sent[i], axes_x, swap_pairs(x_size, i))  3.94 us
    all_to_all x1, starting transfers between devices, per_device(): back = lax.all_to_all(back, group, split_axis=0, concat_axis=0, tiled=True)  3.5 us
    all_to_all x1, waiting for transfers between devices, per_device(): back = lax.all_to_all(back, group, split_axis=0, concat_axis=0, tiled=True)  1.22 us
  transfers between devices with their start and end apart: 3, of which 1 were waited for; matrix products, arithmetic and copies ran while one was open for 0% of the time, Pallas kernels for 5%

profile of v7, /device:TPU:0, one launch (start us, length us, event | category | flops | bytes accessed | tf_op | source)
XLA Modules:
  0.0 28.3 jit_solution(1889776296327838515)
XLA Ops:
  0.6 0.0 copy-start
  0.6 0.0 copy-start.1
  0.7 1.5 %front.1 = (f32[16,8,128]{2,1,0:T(8,128)S(1)}, f32[50,16,128]{2,1,0:T(8,128)S(1)}, f32[16,128]{1,0:T(8,128)S(1)}, f32[1,8]{1,0:T(1,128)S(1)}, s32[16,128]{1,0:T(8,128)S(1)}) custom-call(s32[2,128]{1,0:T(2,128)} %bitcast.5, s32[2,128]{1,0:T(2,128)} %bitcast.6, f32[2,128]{1,0:T(2,128)} %bitcast.7, f32[2,128]{1,0:T(2,128)} %bitcast.8, f32[50,16,128]{2,1,0:T(8,128)} %refs_4_.1, ...), custom_call_target="tpu_custom_call" | custom-call | flops 1000000000 | bytes 1000000000 | tf_op jit(solution)/shard_map/front/pallas_call | solution.py:317
  2.1 13.8 %all_to_all.10.got.refs_1_ = f32[16,8,128]{2,1,0:T(8,128)S(1)} all-to-all(f32[16,8,128]{2,1,0:T(8,128)S(1)} %get-tuple-element.15), channel_id=1, replica_groups=mesh['sec'=2,'gx'=4,'gy'=4] {'gx','gy'}, dimensions={0} | all-to-all | bytes 131072 | tf_op jit(solution)/shard_map/all_to_all | solution.py:380
  15.9 0.0 copy-done
  15.9 0.0 copy-done.1
  15.9 1.2 %pick.1 = (f32[16,8,128]{2,1,0:T(8,128)}, f32[2,16,128]{2,1,0:T(8,128)S(1)}, f32[2,8,128]{2,1,0:T(8,128)S(1)}, f32[16,128]{1,0:T(8,128)S(1)}) custom-call(f32[16,8,128]{2,1,0:T(8,128)S(1)} %all_to_all.10.got.refs_1_, f32[50,16,128]{2,1,0:T(8,128)S(1)} %get-tuple-element.16.head.refs_2_, f32[50,16,128]{2,1,0:T(8,128)S(1)} %copy-done, ...), custom_call_target="tpu_custom_call" | custom-call | flops 1000 | bytes 1000 | tf_op jit(solution)/shard_map/pick/pallas_call | solution.py:317
  17.2 3.5 %all-to-all-start.1 = ((f32[16,8,128]{2,1,0:T(8,128)}), f32[16,8,128]{2,1,0:T(8,128)S(1)}, u32[]{:S(2)}, u32[]{:S(2)}) async-start(f32[16,8,128]{2,1,0:T(8,128)} %get-tuple-element.18), calls=%async_computation.1 | async-start | bytes 131072 | tf_op jit(solution)/shard_map/all_to_all | solution.py:392
  20.7 0.0 copy-start.2
  20.7 0.0 copy-start.3
  20.7 0.4 %edge.1 = (f32[100,128]{1,0:T(8,128)S(1)}, f32[100,128]{1,0:T(8,128)S(1)}, f32[50,16,128]{2,1,0:T(8,128)S(1)}, f32[50,16,128]{2,1,0:T(8,128)S(1)}) custom-call(f32[50,16,128]{2,1,0:T(8,128)S(1)} %get-tuple-element.16.head.refs_2_, f32[50,16,128]{2,1,0:T(8,128)S(1)} %copy-done, f32[50,16,128]{2,1,0:T(8,128)S(1)} %copy-done.1, ...), custom_call_target="tpu_custom_call" | custom-call | flops 1000 | bytes 1000 | tf_op jit(solution)/shard_map/edge/pallas_call | solution.py:317
  21.1 0.7 %collective-permute-start.1 = (f32[100,128]{1,0:T(8,128)S(1)}, f32[100,128]{1,0:T(8,128)S(1)}, u32[]{:S(2)}, u32[]{:S(2)}) collective-permute-start(f32[100,128]{1,0:T(8,128)S(1)} %get-tuple-element.27.refs_7_), channel_id=1, source_target_pairs={{4,8},{8,4},{12,16},{16,12},{20,24},{24,20},{5,9},{9,5},{13,17},{1... | collective-permute-start | bytes 153608 | tf_op jit(solution)/shard_map/ppermute | solution.py:401
  21.8 3.3 %collective-permute-start = (f32[100,128]{1,0:T(8,128)S(1)}, f32[100,128]{1,0:T(8,128)S(1)}, u32[]{:S(2)}, u32[]{:S(2)}) collective-permute-start(f32[100,128]{1,0:T(8,128)S(1)} %get-tuple-element.26.refs_10_.refs_6_), channel_id=1, source_target_pairs={{0,4},{4,0},{8,12},{12,8},{16,20},{20,16},{24,28},{28,24},{1,5},{5... | collective-permute-start | bytes 153608 | tf_op jit(solution)/shard_map/ppermute | solution.py:401
  25.1 0.0 copy-done.2
  25.1 0.0 copy-done.3
  25.1 0.0 copy-start.4
  25.1 0.9 %interior.1.refs_4_ = f32[50,16,128]{2,1,0:T(8,128)S(1)} custom-call(f32[50,16,128]{2,1,0:T(8,128)S(1)} %copy-done.2, f32[50,16,128]{2,1,0:T(8,128)S(1)} %copy-done.3, f32[50,16,128]{2,1,0:T(8,128)S(1)} %get-tuple-element.16.head.refs_2_, f32[50,16,128]{2,1,0:T(8,128)S(1)} %copy-done, f32[50,16,128]{2,1,0:T(8,128)S(1)} %get-tuple-element.21.refs_4_, ...), custom_call_target="tpu_custom_call" | custom-call | flops 1000 | bytes 1000 | tf_op jit(solution)/shard_map/interior/pallas_call | solution.py:317
  26.0 0.0 collective-permute-done.1.refs_9_
  26.0 0.0 collective-permute-done.refs_8_
  26.0 1.2 %all-to-all-done.1.refs_0_ = f32[16,8,128]{2,1,0:T(8,128)S(1)} async-done(((f32[16,8,128]{2,1,0:T(8,128)}), f32[16,8,128]{2,1,0:T(8,128)S(1)}, u32[]{:S(2)}, u32[]{:S(2)}) %all-to-all-start.1) | async-done | bytes 65568 | tf_op jit(solution)/shard_map/all_to_all | solution.py:392
  27.2 0.0 copy-done.4
  27.2 1.1 %last.1 = (f32[50,16,128]{2,1,0:T(8,128)}, f32[10,256]{1,0:T(8,128)}) custom-call(f32[16,8,128]{2,1,0:T(8,128)S(1)} %all-to-all-done.1.refs_0_, f32[16,8,128]{2,1,0:T(8,128)S(1)} %all_to_all.10.got.refs_1_, f32[16,128]{1,0:T(8,128)S(1)} %get-tuple-element.17.head_border.refs_2_, f32[16,128]{1,0:T(8,128)S(1)} %get-tuple-element.19.refs_3_, ...), custom_call_target="tpu_custom_call" | custom-call | flops 1000 | bytes 1000 | tf_op jit(solution)/shard_map/last/pallas_call | solution.py:317
Async XLA Ops:
  0.6 15.3 %copy-start = (f32[50,16,128]{2,1,0:T(8,128)S(1)}, f32[50,16,128]{2,1,0:T(8,128)}, u32[]{:S(2)}) copy-start(f32[50,16,128]{2,1,0:T(8,128)} %refs_3_.1) | copy-start | bytes 1228804
  0.6 15.3 %copy-start.1 = (f32[50,16,128]{2,1,0:T(8,128)S(1)}, f32[50,16,128]{2,1,0:T(8,128)}, u32[]{:S(2)}) copy-start(f32[50,16,128]{2,1,0:T(8,128)} %perm.3) | copy-start | bytes 1228804
  17.2 10.1 %all-to-all-start.1 = ((f32[16,8,128]{2,1,0:T(8,128)}), f32[16,8,128]{2,1,0:T(8,128)S(1)}, u32[]{:S(2)}, u32[]{:S(2)}) async-start(f32[16,8,128]{2,1,0:T(8,128)} %get-tuple-element.18), calls=%async_computation.1 | async-start | bytes 131072 | tf_op jit(solution)/shard_map/all_to_all | solution.py:392
  20.7 4.4 %copy-start.2 = (f32[50,16,128]{2,1,0:T(8,128)S(1)}, f32[50,16,128]{2,1,0:T(8,128)}, u32[]{:S(2)}) copy-start(f32[50,16,128]{2,1,0:T(8,128)} %refs_0_.1) | copy-start | bytes 1228804
  20.7 4.4 %copy-start.3 = (f32[50,16,128]{2,1,0:T(8,128)S(1)}, f32[50,16,128]{2,1,0:T(8,128)}, u32[]{:S(2)}) copy-start(f32[50,16,128]{2,1,0:T(8,128)} %refs_1_.1) | copy-start | bytes 1228804
  21.1 4.9 %collective-permute-start.1 = (f32[100,128]{1,0:T(8,128)S(1)}, f32[100,128]{1,0:T(8,128)S(1)}, u32[]{:S(2)}, u32[]{:S(2)}) collective-permute-start(f32[100,128]{1,0:T(8,128)S(1)} %get-tuple-element.27.refs_7_), channel_id=1, source_target_pairs={{4,8},{8,4},{12,16},{16,12},{20,24},{24,20},{5,9},{9,5},{13,17},{1... | collective-permute-start | bytes 153608 | tf_op jit(solution)/shard_map/ppermute | solution.py:401
  21.8 4.2 %collective-permute-start = (f32[100,128]{1,0:T(8,128)S(1)}, f32[100,128]{1,0:T(8,128)S(1)}, u32[]{:S(2)}, u32[]{:S(2)}) collective-permute-start(f32[100,128]{1,0:T(8,128)S(1)} %get-tuple-element.26.refs_10_.refs_6_), channel_id=1, source_target_pairs={{0,4},{4,0},{8,12},{12,8},{16,20},{20,16},{24,28},{28,24},{1,5},{5... | collective-permute-start | bytes 153608 | tf_op jit(solution)/shard_map/ppermute | solution.py:401
  25.1 2.2 %copy-start.4 = (f32[10,256]{1,0:T(8,128)S(1)}, f32[10,256]{1,0:T(8,128)}, u32[]{:S(2)}) copy-start(f32[10,256]{1,0:T(8,128)} %refs_5_.1) | copy-start | bytes 30724

commit v8 on v7

--- a/solution.py
+++ b/solution.py
@@ -11,7 +11,7 @@
 LANES = 128
 CHUNK = 10
 FRONT_CHUNK = 25
-FIELD_LANE = 104
+EXTRA_LANE, MAIN_LANE = 104, 112
 VMEM_LIMIT = 24 * 1024 * 1024
 
 
@@ -83,25 +83,45 @@
     return border
 
 
-def pack_blocks(rows, count, blocks, bank):
-    height, size = blocks.shape[1], LANES // (2 * blocks.shape[1])
-    above = jnp.zeros((FIELD_LANE, LANES), jnp.float32)
-    below = jnp.zeros((LANES - FIELD_LANE - rows.shape[0], LANES), jnp.float32)
-    turned = jnp.concatenate([above, rows, below], axis=0).T
+def pack_blocks(rows, blocks, bank):
+    width = LANES - MAIN_LANE
+    size = LANES // width
+    main = rows[:8]
+    lane = iota((8, LANES), 1)
+    pieces = []
+    for i in range(8, rows.shape[0]):
+        row = rows[i : i + 1]
+        pieces += [row, pltpu.roll(row, LANES - width // 2, 1)]
+    if pieces:
+        pieces.append(jnp.zeros((8 - len(pieces), LANES), jnp.float32))
+        extra = jnp.concatenate(pieces, axis=0)
     for b in range(size):
-        upper = turned[2 * b * height : (2 * b + 1) * height]
-        lower = turned[(2 * b + 1) * height : (2 * b + 2) * height]
-        blocks[bank * size + b] = upper + pltpu.roll(lower, count, 1)
-
-
-def unpack_blocks(blocks, count, bank, height):
-    rows, size = blocks.shape[1], LANES // (2 * blocks.shape[1])
-    pieces = []
+        block = jnp.where(lane >= MAIN_LANE, pltpu.roll(main, (MAIN_LANE - width * b) % LANES, 1), 0.0)
+        if pieces:
+            moved = pltpu.roll(extra, (EXTRA_LANE - width * b) % LANES, 1)
+            block = jnp.where((lane >= EXTRA_LANE) & (lane < MAIN_LANE), moved, block)
+        blocks[bank * size + b] = block
+
+
+def unpack_blocks(blocks, count, bank):
+    width = LANES - MAIN_LANE
+    size = LANES // width
+    lane = iota((8, LANES), 1)
+    main = jnp.zeros((8, LANES), jnp.float32)
+    extra = jnp.zeros((8, LANES), jnp.float32)
     for b in range(size):
         block = blocks[bank * size + b]
-        pieces += [block, pltpu.roll(block, LANES - count, 1)]
-    turned = jnp.concatenate(pieces, axis=0).T
-    return turned[FIELD_LANE : FIELD_LANE + height]
+        moved = pltpu.roll(block, (width * b - MAIN_LANE) % LANES, 1)
+        main = jnp.where(lane // width == b, moved, main)
+        if count > 8:
+            moved = pltpu.roll(block, (width * b - EXTRA_LANE) % LANES, 1)
+            extra = jnp.where(lane // width == b, moved, extra)
+    rows = [main]
+    first = lane[:1] % width < width // 2
+    for i in range(count - 8):
+        second = pltpu.roll(extra[2 * i + 1 : 2 * i + 2], width // 2, 1)
+        rows.append(jnp.where(first, extra[2 * i : 2 * i + 1], second))
+    return jnp.concatenate(rows, axis=0) if count > 8 else main
 
 
 def front_kernel(*refs):
@@ -123,7 +143,7 @@
     for bank in range(fields_in[0].shape[0]):
         rows = [ref[bank : bank + 1, :].astype(jnp.float32) for ref in fields_in]
         rows.append(jnp.zeros((4, LANES), jnp.float32))
-        pack_blocks(jnp.concatenate(rows, axis=0), 4, sent, bank)
+        pack_blocks(jnp.concatenate(rows, axis=0), sent, bank)
     heads = jnp.zeros((width_x, width_y), jnp.float32)
     for copy, (start, stop) in zip(large, parts):
         copy.wait()
@@ -161,7 +181,7 @@
     border = border_of(perm, 0, layers, zero) * wet * wet * wet
     cond_border[...] = border
     for bank in range(fields.shape[0]):
-        rows = unpack_blocks(got, 4, bank, 8)
+        rows = unpack_blocks(got, 8, bank)
         fields[bank] = rows
         ids = rows[0:1].astype(jnp.int32)
         lane_hot = hot(lax.rem(ids, width_y), width_y).astype(jnp.float32).astype(jnp.bfloat16)
@@ -173,7 +193,7 @@
             patch_sat[bank, k : k + 1, :] = jnp.sum(
                 jnp.where(row_hot, one, 0.0), axis=0, keepdims=True
             )
-        pack_blocks(patch_sat[bank], top, back, bank)
+        pack_blocks(patch_sat[bank][:top], back, bank)
     add_border(back, border)
 
 
@@ -277,7 +297,7 @@
         copy.start()
         writes.append(copy)
     for bank in range(nitrate.shape[1] // LANES):
-        sat = unpack_blocks(back, top, bank, 16)[:top]
+        sat = unpack_blocks(back, top, bank)
         lanes = slice(bank * LANES, (bank + 1) * LANES)
         loss = 0.3 * sat * sat
         value = nitrate[:, lanes]
@@ -345,7 +365,7 @@
     per_block = slots // owners
     if LANES % per_block or slots % LANES or per_block != width_x:
         raise ValueError("block size")
-    if width_y != LANES or width_x != 16 or 2 * layers > FIELD_LANE or FIELD_LANE + 2 * top > LANES:
+    if width_y != LANES or width_x != LANES - MAIN_LANE or 2 * layers > EXTRA_LANE or not 8 <= top <= 11:
         raise ValueError("grid size")
     half = width_x // 2
     banks = slots // LANES

time: 28.6 us -> 28.4 us (level)
  no operation moved by 1% of the time
where the time goes in v8:
time: 28.4 us; the launch traced here: 28.1 us
  blocking collectives  13.8 us (49%)
  starting transfers between devices  7.44 us (26%)
  Pallas kernels  4.91 us (17%)
  waiting for transfers between devices  1.23 us (4%)
  between operations  0.72 us (3%)
    all_to_all x1, blocking collectives, per_device(): got = lax.all_to_all(sent, group, split_axis=0, concat_axis=0, tiled=True)  13.8 us
    pallas_call x5, Pallas kernels, run(): kernel(*(pltpu.with_memory_space_constraint(arg, pltpu.HBM) if i == 'H' e...  4.91 us
    ppermute x2, starting transfers between devices, per_device(): lax.ppermute(x_sent[i], axes_x, swap_pairs(x_size, i))  3.94 us
    all_to_all x1, starting transfers between devices, per_device(): back = lax.all_to_all(back, group, split_axis=0, concat_axis=0, tiled=True)  3.5 us
    all_to_all x1, waiting for transfers between devices, per_device(): back = lax.all_to_all(back, group, split_axis=0, concat_axis=0, tiled=True)  1.22 us
  transfers between devices with their start and end apart: 3, of which 1 were waited for; matrix products, arithmetic and copies ran while one was open for 0% of the time, Pallas kernels for 5%

profile of v8, /device:TPU:0, one launch (start us, length us, event | category | flops | bytes accessed | tf_op | source)
XLA Modules:
  0.0 28.1 jit_solution(8507604125396850345)
XLA Ops:
  0.6 0.0 copy-start
  0.6 0.0 copy-start.1
  0.7 1.5 %front.1 = (f32[16,8,128]{2,1,0:T(8,128)S(1)}, f32[50,16,128]{2,1,0:T(8,128)S(1)}, f32[16,128]{1,0:T(8,128)S(1)}, f32[1,8]{1,0:T(1,128)S(1)}, s32[16,128]{1,0:T(8,128)S(1)}) custom-call(s32[2,128]{1,0:T(2,128)} %bitcast.5, s32[2,128]{1,0:T(2,128)} %bitcast.6, f32[2,128]{1,0:T(2,128)} %bitcast.7, f32[2,128]{1,0:T(2,128)} %bitcast.8, f32[50,16,128]{2,1,0:T(8,128)} %refs_4_.1, ...), custom_call_target="tpu_custom_call" | custom-call | flops 1000000000 | bytes 1000000000 | tf_op jit(solution)/shard_map/front/pallas_call | solution.py:337
  2.1 13.8 %all_to_all.10.got.refs_1_ = f32[16,8,128]{2,1,0:T(8,128)S(1)} all-to-all(f32[16,8,128]{2,1,0:T(8,128)S(1)} %get-tuple-element.15), channel_id=1, replica_groups=mesh['sec'=2,'gx'=4,'gy'=4] {'gx','gy'}, dimensions={0} | all-to-all | bytes 131072 | tf_op jit(solution)/shard_map/all_to_all | solution.py:400
  15.9 0.0 copy-done
  15.9 0.0 copy-done.1
  15.9 1.1 %pick.1 = (f32[16,8,128]{2,1,0:T(8,128)}, f32[2,16,128]{2,1,0:T(8,128)S(1)}, f32[2,8,128]{2,1,0:T(8,128)S(1)}, f32[16,128]{1,0:T(8,128)S(1)}) custom-call(f32[16,8,128]{2,1,0:T(8,128)S(1)} %all_to_all.10.got.refs_1_, f32[50,16,128]{2,1,0:T(8,128)S(1)} %get-tuple-element.16.head.refs_2_, f32[50,16,128]{2,1,0:T(8,128)S(1)} %copy-done, ...), custom_call_target="tpu_custom_call" | custom-call | flops 1000 | bytes 1000 | tf_op jit(solution)/shard_map/pick/pallas_call | solution.py:337
  17.1 3.5 %all-to-all-start.1 = ((f32[16,8,128]{2,1,0:T(8,128)}), f32[16,8,128]{2,1,0:T(8,128)S(1)}, u32[]{:S(2)}, u32[]{:S(2)}) async-start(f32[16,8,128]{2,1,0:T(8,128)} %get-tuple-element.18), calls=%async_computation.1 | async-start | bytes 131072 | tf_op jit(solution)/shard_map/all_to_all | solution.py:412
  20.6 0.0 copy-start.2
  20.6 0.0 copy-start.3
  20.6 0.4 %edge.1 = (f32[100,128]{1,0:T(8,128)S(1)}, f32[100,128]{1,0:T(8,128)S(1)}, f32[50,16,128]{2,1,0:T(8,128)S(1)}, f32[50,16,128]{2,1,0:T(8,128)S(1)}) custom-call(f32[50,16,128]{2,1,0:T(8,128)S(1)} %get-tuple-element.16.head.refs_2_, f32[50,16,128]{2,1,0:T(8,128)S(1)} %copy-done, f32[50,16,128]{2,1,0:T(8,128)S(1)} %copy-done.1, ...), custom_call_target="tpu_custom_call" | custom-call | flops 1000 | bytes 1000 | tf_op jit(solution)/shard_map/edge/pallas_call | solution.py:337
  21.0 0.7 %collective-permute-start.1 = (f32[100,128]{1,0:T(8,128)S(1)}, f32[100,128]{1,0:T(8,128)S(1)}, u32[]{:S(2)}, u32[]{:S(2)}) collective-permute-start(f32[100,128]{1,0:T(8,128)S(1)} %get-tuple-element.27.refs_7_), channel_id=1, source_target_pairs={{4,8},{8,4},{12,16},{16,12},{20,24},{24,20},{5,9},{9,5},{13,17},{1... | collective-permute-start | bytes 153608 | tf_op jit(solution)/shard_map/ppermute | solution.py:421
  21.7 3.3 %collective-permute-start = (f32[100,128]{1,0:T(8,128)S(1)}, f32[100,128]{1,0:T(8,128)S(1)}, u32[]{:S(2)}, u32[]{:S(2)}) collective-permute-start(f32[100,128]{1,0:T(8,128)S(1)} %get-tuple-element.26.refs_10_.refs_6_), channel_id=1, source_target_pairs={{0,4},{4,0},{8,12},{12,8},{16,20},{20,16},{24,28},{28,24},{1,5},{5... | collective-permute-start | bytes 153608 | tf_op jit(solution)/shard_map/ppermute | solution.py:421
  25.0 0.0 copy-done.2
  25.0 0.0 copy-done.3
  25.0 0.0 copy-start.4
  25.0 0.9 %interior.1.refs_4_ = f32[50,16,128]{2,1,0:T(8,128)S(1)} custom-call(f32[50,16,128]{2,1,0:T(8,128)S(1)} %copy-done.2, f32[50,16,128]{2,1,0:T(8,128)S(1)} %copy-done.3, f32[50,16,128]{2,1,0:T(8,128)S(1)} %get-tuple-element.16.head.refs_2_, f32[50,16,128]{2,1,0:T(8,128)S(1)} %copy-done, f32[50,16,128]{2,1,0:T(8,128)S(1)} %get-tuple-element.21.refs_4_, ...), custom_call_target="tpu_custom_call" | custom-call | flops 1000 | bytes 1000 | tf_op jit(solution)/shard_map/interior/pallas_call | solution.py:337
  25.9 0.0 collective-permute-done.1.refs_9_
  25.9 0.0 collective-permute-done.refs_8_
  25.9 1.2 %all-to-all-done.1.refs_0_ = f32[16,8,128]{2,1,0:T(8,128)S(1)} async-done(((f32[16,8,128]{2,1,0:T(8,128)}), f32[16,8,128]{2,1,0:T(8,128)S(1)}, u32[]{:S(2)}, u32[]{:S(2)}) %all-to-all-start.1) | async-done | bytes 65568 | tf_op jit(solution)/shard_map/all_to_all | solution.py:412
  27.1 0.0 copy-done.4
  27.2 1.0 %last.1 = (f32[50,16,128]{2,1,0:T(8,128)}, f32[10,256]{1,0:T(8,128)}) custom-call(f32[16,8,128]{2,1,0:T(8,128)S(1)} %all-to-all-done.1.refs_0_, f32[16,8,128]{2,1,0:T(8,128)S(1)} %all_to_all.10.got.refs_1_, f32[16,128]{1,0:T(8,128)S(1)} %get-tuple-element.17.head_border.refs_2_, f32[16,128]{1,0:T(8,128)S(1)} %get-tuple-element.19.refs_3_, ...), custom_call_target="tpu_custom_call" | custom-call | flops 1000 | bytes 1000 | tf_op jit(solution)/shard_map/last/pallas_call | solution.py:337
Async XLA Ops:
  0.6 15.3 %copy-start = (f32[50,16,128]{2,1,0:T(8,128)S(1)}, f32[50,16,128]{2,1,0:T(8,128)}, u32[]{:S(2)}) copy-start(f32[50,16,128]{2,1,0:T(8,128)} %refs_3_.1) | copy-start | bytes 1228804
  0.6 15.3 %copy-start.1 = (f32[50,16,128]{2,1,0:T(8,128)S(1)}, f32[50,16,128]{2,1,0:T(8,128)}, u32[]{:S(2)}) copy-start(f32[50,16,128]{2,1,0:T(8,128)} %perm.3) | copy-start | bytes 1228804
  17.1 10.1 %all-to-all-start.1 = ((f32[16,8,128]{2,1,0:T(8,128)}), f32[16,8,128]{2,1,0:T(8,128)S(1)}, u32[]{:S(2)}, u32[]{:S(2)}) async-start(f32[16,8,128]{2,1,0:T(8,128)} %get-tuple-element.18), calls=%async_computation.1 | async-start | bytes 131072 | tf_op jit(solution)/shard_map/all_to_all | solution.py:412
  20.6 4.4 %copy-start.2 = (f32[50,16,128]{2,1,0:T(8,128)S(1)}, f32[50,16,128]{2,1,0:T(8,128)}, u32[]{:S(2)}) copy-start(f32[50,16,128]{2,1,0:T(8,128)} %refs_0_.1) | copy-start | bytes 1228804
  20.6 4.4 %copy-start.3 = (f32[50,16,128]{2,1,0:T(8,128)S(1)}, f32[50,16,128]{2,1,0:T(8,128)}, u32[]{:S(2)}) copy-start(f32[50,16,128]{2,1,0:T(8,128)} %refs_1_.1) | copy-start | bytes 1228804
  21.0 4.9 %collective-permute-start.1 = (f32[100,128]{1,0:T(8,128)S(1)}, f32[100,128]{1,0:T(8,128)S(1)}, u32[]{:S(2)}, u32[]{:S(2)}) collective-permute-start(f32[100,128]{1,0:T(8,128)S(1)} %get-tuple-element.27.refs_7_), channel_id=1, source_target_pairs={{4,8},{8,4},{12,16},{16,12},{20,24},{24,20},{5,9},{9,5},{13,17},{1... | collective-permute-start | bytes 153608 | tf_op jit(solution)/shard_map/ppermute | solution.py:421
  21.7 4.2 %collective-permute-start = (f32[100,128]{1,0:T(8,128)S(1)}, f32[100,128]{1,0:T(8,128)S(1)}, u32[]{:S(2)}, u32[]{:S(2)}) collective-permute-start(f32[100,128]{1,0:T(8,128)S(1)} %get-tuple-element.26.refs_10_.refs_6_), channel_id=1, source_target_pairs={{0,4},{4,0},{8,12},{12,8},{16,20},{20,16},{24,28},{28,24},{1,5},{5... | collective-permute-start | bytes 153608 | tf_op jit(solution)/shard_map/ppermute | solution.py:421
  25.0 2.2 %copy-start.4 = (f32[10,256]{1,0:T(8,128)S(1)}, f32[10,256]{1,0:T(8,128)}, u32[]{:S(2)}) copy-start(f32[10,256]{1,0:T(8,128)} %refs_5_.1) | copy-start | bytes 30724

commit v9 on v8

--- a/solution.py
+++ b/solution.py
@@ -263,12 +263,9 @@
         out[start:stop] = total
 
 
-def last_kernel(axes_x, *refs):
-    back, got, y_heads, y_conds, partial, nitrate = refs[:6]
-    x_sent, x_got = refs[6:8], refs[8:10]
-    residual, nitrate_out, out, value_out, x_faces, sems = refs[10:]
+def faces_kernel(axes_x, partial, *refs):
+    x_sent, x_got, out, x_faces = refs[:2], refs[2:4], refs[4], refs[5]
     layers, width_x, width_y = partial.shape
-    top = nitrate.shape[0]
     even = place_of(axes_x) % 2 == 0
     faces = []
     for rows in (slice(0, layers), slice(layers, 2 * layers)):
@@ -280,18 +277,29 @@
     heads, conds = faces
     x_faces[0] = 0.5 * (conds[0] + conds[2]) * (heads[0] - heads[2])
     x_faces[1] = 0.5 * (conds[1] + conds[3]) * (heads[1] - heads[3])
+    half = width_x // 2
+    row = iota((half, width_y), 0)
+    for k in range(layers):
+        upper = jnp.where(row == 0, x_faces[0, k : k + 1, :], 0.0)
+        lower = jnp.where(row == half - 1, x_faces[1, k : k + 1, :], 0.0)
+        out[k, :half] = partial[k, :half] + upper
+        out[k, half:] = partial[k, half:] + lower
+
+
+def last_kernel(*refs):
+    back, got, y_heads, y_conds, partial, nitrate = refs[:6]
+    residual, nitrate_out, out, value_out, sems = refs[6:]
+    layers, width_x, width_y = partial.shape
+    top = nitrate.shape[0]
     flux = 0.5 * (y_conds[...] + neighbour_borders(back)) * (y_heads[...] - neighbour_borders(got))
-    row, lane = iota(flux.shape, 0), iota(flux.shape, 1)
+    lane = iota(flux.shape, 1)
     on_border = (lane == 0) | (lane == width_y - 1)
     parts = parts_of(layers, 2 * CHUNK)
     writes = []
     for i, (start, stop) in enumerate(parts):
         for k in range(start, stop):
             edge = pltpu.roll(flux, width_y - 1 - 2 * k, 1)
-            one = partial[k] + jnp.where(on_border, edge, 0.0)
-            one = one + jnp.where(row == 0, x_faces[0, k : k + 1, :], 0.0)
-            one = one + jnp.where(row == width_x - 1, x_faces[1, k : k + 1, :], 0.0)
-            out[k] = one
+            out[k] = partial[k] + jnp.where(on_border, edge, 0.0)
         rows = pl.ds(start, stop - start)
         copy = pltpu.make_async_copy(out.at[rows], residual.at[rows], sems.at[i])
         copy.start()
@@ -426,19 +434,25 @@
         x_sent[0],
     )
 
+    (partial,) = call(
+        functools.partial(faces_kernel, axes_x),
+        "faces",
+        "VVVVV",
+        ((field, "V"),),
+        (pltpu.VMEM((2, layers, width_y), f32),),
+    )(partial, *x_sent, *x_got)
     residual, nitrate_out = call(
-        functools.partial(last_kernel, axes_x),
+        last_kernel,
         "last",
-        "VVVVVVVVVV",
+        "VVVVVV",
         ((field, "H"), (shape((top, slots), f32), "H")),
         (
             field_in,
             pltpu.VMEM((top, slots), f32),
-            pltpu.VMEM((2, layers, width_y), f32),
             dma((halves + 1,)),
         ),
     )(
-        back, got, head_border, cond_border, partial, nitrate, *x_sent, *x_got,
+        back, got, head_border, cond_border, partial, nitrate,
     )
     return (residual, nitrate_out)
 

time: 28.4 us -> 28.4 us (level)
    pallas_call x5 -> x6, Pallas kernels: 4.91 us -> 5 us  [run(): kernel(*(pltpu.with_memory_space_constraint(arg, pltpu.HBM) if i == 'H' e...]
where the time goes in v9:
time: 28.4 us; the launch traced here: 28.1 us
  blocking collectives  13.8 us (49%)
  starting transfers between devices  7.44 us (26%)
  Pallas kernels  5 us (18%)
  waiting for transfers between devices  1.12 us (4%)
  between operations  0.73 us (3%)
    all_to_all x1, blocking collectives, per_device(): got = lax.all_to_all(sent, group, split_axis=0, concat_axis=0, tiled=True)  13.8 us
    pallas_call x6, Pallas kernels, run(): kernel(*(pltpu.with_memory_space_constraint(arg, pltpu.HBM) if i == 'H' e...  5 us
    ppermute x2, starting transfers between devices, per_device(): lax.ppermute(x_sent[i], axes_x, swap_pairs(x_size, i))  3.94 us
    all_to_all x1, starting transfers between devices, per_device(): back = lax.all_to_all(back, group, split_axis=0, concat_axis=0, tiled=True)  3.5 us
    all_to_all x1, waiting for transfers between devices, per_device(): back = lax.all_to_all(back, group, split_axis=0, concat_axis=0, tiled=True)  1.12 us
  transfers between devices with their start and end apart: 3, of which 1 were waited for; matrix products, arithmetic and copies ran while one was open for 0% of the time, Pallas kernels for 5%

profile of v9, /device:TPU:0, one launch (start us, length us, event | category | flops | bytes accessed | tf_op | source)
XLA Modules:
  0.0 28.1 jit_solution(6090813877838421119)
XLA Ops:
  0.6 0.0 copy-start
  0.6 0.0 copy-start.1
  0.7 1.5 %front.1 = (f32[16,8,128]{2,1,0:T(8,128)S(1)}, f32[50,16,128]{2,1,0:T(8,128)S(1)}, f32[16,128]{1,0:T(8,128)S(1)}, f32[1,8]{1,0:T(1,128)S(1)}, s32[16,128]{1,0:T(8,128)S(1)}) custom-call(s32[2,128]{1,0:T(2,128)} %bitcast.5, s32[2,128]{1,0:T(2,128)} %bitcast.6, f32[2,128]{1,0:T(2,128)} %bitcast.7, f32[2,128]{1,0:T(2,128)} %bitcast.8, f32[50,16,128]{2,1,0:T(8,128)} %refs_4_.1, ...), custom_call_target="tpu_custom_call" | custom-call | flops 1000000000 | bytes 1000000000 | tf_op jit(solution)/shard_map/front/pallas_call | solution.py:345
  2.1 13.8 %all_to_all.10.got.refs_1_ = f32[16,8,128]{2,1,0:T(8,128)S(1)} all-to-all(f32[16,8,128]{2,1,0:T(8,128)S(1)} %get-tuple-element.15), channel_id=1, replica_groups=mesh['sec'=2,'gx'=4,'gy'=4] {'gx','gy'}, dimensions={0} | all-to-all | bytes 131072 | tf_op jit(solution)/shard_map/all_to_all | solution.py:408
  15.9 0.0 copy-done
  15.9 0.0 copy-done.1
  15.9 1.1 %pick.1 = (f32[16,8,128]{2,1,0:T(8,128)}, f32[2,16,128]{2,1,0:T(8,128)S(1)}, f32[2,8,128]{2,1,0:T(8,128)S(1)}, f32[16,128]{1,0:T(8,128)S(1)}) custom-call(f32[16,8,128]{2,1,0:T(8,128)S(1)} %all_to_all.10.got.refs_1_, f32[50,16,128]{2,1,0:T(8,128)S(1)} %get-tuple-element.16.head.refs_2_, f32[50,16,128]{2,1,0:T(8,128)S(1)} %copy-done, ...), custom_call_target="tpu_custom_call" | custom-call | flops 1000 | bytes 1000 | tf_op jit(solution)/shard_map/pick/pallas_call | solution.py:345
  17.1 3.5 %all-to-all-start.1 = ((f32[16,8,128]{2,1,0:T(8,128)}), f32[16,8,128]{2,1,0:T(8,128)S(1)}, u32[]{:S(2)}, u32[]{:S(2)}) async-start(f32[16,8,128]{2,1,0:T(8,128)} %get-tuple-element.18), calls=%async_computation.1 | async-start | bytes 131072 | tf_op jit(solution)/shard_map/all_to_all | solution.py:420
  20.6 0.0 copy-start.2
  20.6 0.0 copy-start.3
  20.6 0.4 %edge.1 = (f32[100,128]{1,0:T(8,128)S(1)}, f32[100,128]{1,0:T(8,128)S(1)}, f32[50,16,128]{2,1,0:T(8,128)S(1)}, f32[50,16,128]{2,1,0:T(8,128)S(1)}) custom-call(f32[50,16,128]{2,1,0:T(8,128)S(1)} %get-tuple-element.16.head.refs_2_, f32[50,16,128]{2,1,0:T(8,128)S(1)} %copy-done, f32[50,16,128]{2,1,0:T(8,128)S(1)} %copy-done.1, ...), custom_call_target="tpu_custom_call" | custom-call | flops 1000 | bytes 1000 | tf_op jit(solution)/shard_map/edge/pallas_call | solution.py:345
  21.0 0.7 %collective-permute-start.1 = (f32[100,128]{1,0:T(8,128)S(1)}, f32[100,128]{1,0:T(8,128)S(1)}, u32[]{:S(2)}, u32[]{:S(2)}) collective-permute-start(f32[100,128]{1,0:T(8,128)S(1)} %get-tuple-element.27.refs_1_), channel_id=1, source_target_pairs={{4,8},{8,4},{12,16},{16,12},{20,24},{24,20},{5,9},{9,5},{13,17},{1... | collective-permute-start | bytes 153608 | tf_op jit(solution)/shard_map/ppermute | solution.py:429
  21.7 3.3 %collective-permute-start = (f32[100,128]{1,0:T(8,128)S(1)}, f32[100,128]{1,0:T(8,128)S(1)}, u32[]{:S(2)}, u32[]{:S(2)}) collective-permute-start(f32[100,128]{1,0:T(8,128)S(1)} %get-tuple-element.26.refs_10_.refs_0_), channel_id=1, source_target_pairs={{0,4},{4,0},{8,12},{12,8},{16,20},{20,16},{24,28},{28,24},{1,5},{5... | collective-permute-start | bytes 153608 | tf_op jit(solution)/shard_map/ppermute | solution.py:429
  25.0 0.0 copy-done.2
  25.0 0.0 copy-done.3
  25.0 0.9 %interior.1.partial = f32[50,16,128]{2,1,0:T(8,128)S(1)} custom-call(f32[50,16,128]{2,1,0:T(8,128)S(1)} %copy-done.2, f32[50,16,128]{2,1,0:T(8,128)S(1)} %copy-done.3, f32[50,16,128]{2,1,0:T(8,128)S(1)} %get-tuple-element.16.head.refs_2_, f32[50,16,128]{2,1,0:T(8,128)S(1)} %copy-done, f32[50,16,128]{2,1,0:T(8,128)S(1)} %get-tuple-element.21.refs_4_, ...), custom_call_target="tpu_custom_call" | custom-call | flops 1000 | bytes 1000 | tf_op jit(solution)/shard_map/interior/pallas_call | solution.py:345
  25.9 0.0 copy-start.4
  25.9 0.0 collective-permute-done.1.refs_3_
  25.9 0.0 collective-permute-done.refs_2_
  25.9 0.1 faces.1.refs_4_
  26.0 1.1 %all-to-all-done.1.refs_0_ = f32[16,8,128]{2,1,0:T(8,128)S(1)} async-done(((f32[16,8,128]{2,1,0:T(8,128)}), f32[16,8,128]{2,1,0:T(8,128)S(1)}, u32[]{:S(2)}, u32[]{:S(2)}) %all-to-all-start.1) | async-done | bytes 65568 | tf_op jit(solution)/shard_map/all_to_all | solution.py:420
  27.1 0.0 copy-done.4
  27.2 1.0 %last.1 = (f32[50,16,128]{2,1,0:T(8,128)}, f32[10,256]{1,0:T(8,128)}) custom-call(f32[16,8,128]{2,1,0:T(8,128)S(1)} %all-to-all-done.1.refs_0_, f32[16,8,128]{2,1,0:T(8,128)S(1)} %all_to_all.10.got.refs_1_, f32[16,128]{1,0:T(8,128)S(1)} %get-tuple-element.17.head_border.refs_2_, f32[16,128]{1,0:T(8,128)S(1)} %get-tuple-element.19.refs_3_, ...), custom_call_target="tpu_custom_call" | custom-call | flops 1000 | bytes 1000 | tf_op jit(solution)/shard_map/last/pallas_call | solution.py:345
Async XLA Ops:
  0.6 15.3 %copy-start = (f32[50,16,128]{2,1,0:T(8,128)S(1)}, f32[50,16,128]{2,1,0:T(8,128)}, u32[]{:S(2)}) copy-start(f32[50,16,128]{2,1,0:T(8,128)} %refs_3_.1) | copy-start | bytes 1228804
  0.6 15.3 %copy-start.1 = (f32[50,16,128]{2,1,0:T(8,128)S(1)}, f32[50,16,128]{2,1,0:T(8,128)}, u32[]{:S(2)}) copy-start(f32[50,16,128]{2,1,0:T(8,128)} %perm.3) | copy-start | bytes 1228804
  17.1 10.1 %all-to-all-start.1 = ((f32[16,8,128]{2,1,0:T(8,128)}), f32[16,8,128]{2,1,0:T(8,128)S(1)}, u32[]{:S(2)}, u32[]{:S(2)}) async-start(f32[16,8,128]{2,1,0:T(8,128)} %get-tuple-element.18), calls=%async_computation.1 | async-start | bytes 131072 | tf_op jit(solution)/shard_map/all_to_all | solution.py:420
  20.6 4.4 %copy-start.2 = (f32[50,16,128]{2,1,0:T(8,128)S(1)}, f32[50,16,128]{2,1,0:T(8,128)}, u32[]{:S(2)}) copy-start(f32[50,16,128]{2,1,0:T(8,128)} %refs_0_.1) | copy-start | bytes 1228804
  20.6 4.4 %copy-start.3 = (f32[50,16,128]{2,1,0:T(8,128)S(1)}, f32[50,16,128]{2,1,0:T(8,128)}, u32[]{:S(2)}) copy-start(f32[50,16,128]{2,1,0:T(8,128)} %refs_1_.1) | copy-start | bytes 1228804
  21.0 4.9 %collective-permute-start.1 = (f32[100,128]{1,0:T(8,128)S(1)}, f32[100,128]{1,0:T(8,128)S(1)}, u32[]{:S(2)}, u32[]{:S(2)}) collective-permute-start(f32[100,128]{1,0:T(8,128)S(1)} %get-tuple-element.27.refs_1_), channel_id=1, source_target_pairs={{4,8},{8,4},{12,16},{16,12},{20,24},{24,20},{5,9},{9,5},{13,17},{1... | collective-permute-start | bytes 153608 | tf_op jit(solution)/shard_map/ppermute | solution.py:429
  21.7 4.2 %collective-permute-start = (f32[100,128]{1,0:T(8,128)S(1)}, f32[100,128]{1,0:T(8,128)S(1)}, u32[]{:S(2)}, u32[]{:S(2)}) collective-permute-start(f32[100,128]{1,0:T(8,128)S(1)} %get-tuple-element.26.refs_10_.refs_0_), channel_id=1, source_target_pairs={{0,4},{4,0},{8,12},{12,8},{16,20},{20,16},{24,28},{28,24},{1,5},{5... | collective-permute-start | bytes 153608 | tf_op jit(solution)/shard_map/ppermute | solution.py:429
  25.9 1.2 %copy-start.4 = (f32[10,256]{1,0:T(8,128)S(1)}, f32[10,256]{1,0:T(8,128)}, u32[]{:S(2)}) copy-start(f32[10,256]{1,0:T(8,128)} %refs_5_.1) | copy-start | bytes 30724

commit v10 on v8

--- a/solution.py
+++ b/solution.py
@@ -188,11 +188,8 @@
         row_hot = hot(lax.div(ids, width_y), width_x)
         picked = jnp.dot(sat, lane_hot, preferred_element_type=jnp.float32)
         patch_sat[bank] = jnp.zeros(patch_sat.shape[1:], jnp.float32)
-        for k in range(top):
-            one = picked[k * width_x : (k + 1) * width_x]
-            patch_sat[bank, k : k + 1, :] = jnp.sum(
-                jnp.where(row_hot, one, 0.0), axis=0, keepdims=True
-            )
+        chosen = jnp.where(row_hot[None], picked.reshape(top, width_x, LANES), 0.0)
+        patch_sat[bank, :top, :] = jnp.sum(chosen, axis=1)
         pack_blocks(patch_sat[bank][:top], back, bank)
     add_border(back, border)
 
@@ -283,7 +280,7 @@
     flux = 0.5 * (y_conds[...] + neighbour_borders(back)) * (y_heads[...] - neighbour_borders(got))
     row, lane = iota(flux.shape, 0), iota(flux.shape, 1)
     on_border = (lane == 0) | (lane == width_y - 1)
-    parts = parts_of(layers, 2 * CHUNK)
+    parts = parts_of(layers)
     writes = []
     for i, (start, stop) in enumerate(parts):
         for k in range(start, stop):
@@ -373,7 +370,7 @@
     shape, dma = jax.ShapeDtypeStruct, pltpu.SemaphoreType.DMA
     field = shape((layers, width_x, width_y), f32)
     field_in = pltpu.VMEM((layers, width_x, width_y), f32)
-    count, halves = len(parts_of(layers)), len(parts_of(layers, 2 * CHUNK))
+    count, halves = len(parts_of(layers)), len(parts_of(layers))
     blocks = shape((owners, half, LANES), f32)
     border = shape((width_x, width_y), f32)
 

time: 28.4 us -> 28.4 us (level)
  no operation moved by 1% of the time
where the time goes in v10:
time: 28.4 us; the launch traced here: 28.1 us
  blocking collectives  13.8 us (49%)
  starting transfers between devices  7.44 us (26%)
  Pallas kernels  4.91 us (17%)
  waiting for transfers between devices  1.23 us (4%)
  between operations  0.72 us (3%)
    all_to_all x1, blocking collectives, per_device(): got = lax.all_to_all(sent, group, split_axis=0, concat_axis=0, tiled=True)  13.8 us
    pallas_call x5, Pallas kernels, run(): kernel(*(pltpu.with_memory_space_constraint(arg, pltpu.HBM) if i == 'H' e...  4.91 us
    ppermute x2, starting transfers between devices, per_device(): lax.ppermute(x_sent[i], axes_x, swap_pairs(x_size, i))  3.94 us
    all_to_all x1, starting transfers between devices, per_device(): back = lax.all_to_all(back, group, split_axis=0, concat_axis=0, tiled=True)  3.5 us
    all_to_all x1, waiting for transfers between devices, per_device(): back = lax.all_to_all(back, group, split_axis=0, concat_axis=0, tiled=True)  1.22 us
  transfers between devices with their start and end apart: 3, of which 1 were waited for; matrix products, arithmetic and copies ran while one was open for 0% of the time, Pallas kernels for 5%

profile of v10, /device:TPU:0, one launch (start us, length us, event | category | flops | bytes accessed | tf_op | source)
XLA Modules:
  0.0 28.1 jit_solution(5017462763774759770)
XLA Ops:
  0.6 0.0 copy-start
  0.6 0.0 copy-start.1
  0.7 1.5 %front.1 = (f32[16,8,128]{2,1,0:T(8,128)S(1)}, f32[50,16,128]{2,1,0:T(8,128)S(1)}, f32[16,128]{1,0:T(8,128)S(1)}, f32[1,8]{1,0:T(1,128)S(1)}, s32[16,128]{1,0:T(8,128)S(1)}) custom-call(s32[2,128]{1,0:T(2,128)} %bitcast.5, s32[2,128]{1,0:T(2,128)} %bitcast.6, f32[2,128]{1,0:T(2,128)} %bitcast.7, f32[2,128]{1,0:T(2,128)} %bitcast.8, f32[50,16,128]{2,1,0:T(8,128)} %refs_4_.1, ...), custom_call_target="tpu_custom_call" | custom-call | flops 1000000000 | bytes 1000000000 | tf_op jit(solution)/shard_map/front/pallas_call | solution.py:334
  2.1 13.8 %all_to_all.10.got.refs_1_ = f32[16,8,128]{2,1,0:T(8,128)S(1)} all-to-all(f32[16,8,128]{2,1,0:T(8,128)S(1)} %get-tuple-element.15), channel_id=1, replica_groups=mesh['sec'=2,'gx'=4,'gy'=4] {'gx','gy'}, dimensions={0} | all-to-all | bytes 131072 | tf_op jit(solution)/shard_map/all_to_all | solution.py:397
  15.9 0.0 copy-done
  15.9 0.0 copy-done.1
  15.9 1.1 %pick.1 = (f32[16,8,128]{2,1,0:T(8,128)}, f32[2,16,128]{2,1,0:T(8,128)S(1)}, f32[2,8,128]{2,1,0:T(8,128)S(1)}, f32[16,128]{1,0:T(8,128)S(1)}) custom-call(f32[16,8,128]{2,1,0:T(8,128)S(1)} %all_to_all.10.got.refs_1_, f32[50,16,128]{2,1,0:T(8,128)S(1)} %get-tuple-element.16.head.refs_2_, f32[50,16,128]{2,1,0:T(8,128)S(1)} %copy-done, ...), custom_call_target="tpu_custom_call" | custom-call | flops 1000 | bytes 1000 | tf_op jit(solution)/shard_map/pick/pallas_call | solution.py:334
  17.1 3.5 %all-to-all-start.1 = ((f32[16,8,128]{2,1,0:T(8,128)}), f32[16,8,128]{2,1,0:T(8,128)S(1)}, u32[]{:S(2)}, u32[]{:S(2)}) async-start(f32[16,8,128]{2,1,0:T(8,128)} %get-tuple-element.18), calls=%async_computation.1 | async-start | bytes 131072 | tf_op jit(solution)/shard_map/all_to_all | solution.py:409
  20.6 0.0 copy-start.2
  20.6 0.0 copy-start.3
  20.6 0.4 %edge.1 = (f32[100,128]{1,0:T(8,128)S(1)}, f32[100,128]{1,0:T(8,128)S(1)}, f32[50,16,128]{2,1,0:T(8,128)S(1)}, f32[50,16,128]{2,1,0:T(8,128)S(1)}) custom-call(f32[50,16,128]{2,1,0:T(8,128)S(1)} %get-tuple-element.16.head.refs_2_, f32[50,16,128]{2,1,0:T(8,128)S(1)} %copy-done, f32[50,16,128]{2,1,0:T(8,128)S(1)} %copy-done.1, ...), custom_call_target="tpu_custom_call" | custom-call | flops 1000 | bytes 1000 | tf_op jit(solution)/shard_map/edge/pallas_call | solution.py:334
  21.0 0.7 %collective-permute-start.1 = (f32[100,128]{1,0:T(8,128)S(1)}, f32[100,128]{1,0:T(8,128)S(1)}, u32[]{:S(2)}, u32[]{:S(2)}) collective-permute-start(f32[100,128]{1,0:T(8,128)S(1)} %get-tuple-element.27.refs_7_), channel_id=1, source_target_pairs={{4,8},{8,4},{12,16},{16,12},{20,24},{24,20},{5,9},{9,5},{13,17},{1... | collective-permute-start | bytes 153608 | tf_op jit(solution)/shard_map/ppermute | solution.py:418
  21.7 3.3 %collective-permute-start = (f32[100,128]{1,0:T(8,128)S(1)}, f32[100,128]{1,0:T(8,128)S(1)}, u32[]{:S(2)}, u32[]{:S(2)}) collective-permute-start(f32[100,128]{1,0:T(8,128)S(1)} %get-tuple-element.26.refs_10_.refs_6_), channel_id=1, source_target_pairs={{0,4},{4,0},{8,12},{12,8},{16,20},{20,16},{24,28},{28,24},{1,5},{5... | collective-permute-start | bytes 153608 | tf_op jit(solution)/shard_map/ppermute | solution.py:418
  25.0 0.0 copy-done.2
  25.0 0.0 copy-done.3
  25.0 0.0 copy-start.4
  25.0 0.9 %interior.1.refs_4_ = f32[50,16,128]{2,1,0:T(8,128)S(1)} custom-call(f32[50,16,128]{2,1,0:T(8,128)S(1)} %copy-done.2, f32[50,16,128]{2,1,0:T(8,128)S(1)} %copy-done.3, f32[50,16,128]{2,1,0:T(8,128)S(1)} %get-tuple-element.16.head.refs_2_, f32[50,16,128]{2,1,0:T(8,128)S(1)} %copy-done, f32[50,16,128]{2,1,0:T(8,128)S(1)} %get-tuple-element.21.refs_4_, ...), custom_call_target="tpu_custom_call" | custom-call | flops 1000 | bytes 1000 | tf_op jit(solution)/shard_map/interior/pallas_call | solution.py:334
  25.9 0.0 collective-permute-done.1.refs_9_
  25.9 0.0 collective-permute-done.refs_8_
  25.9 1.2 %all-to-all-done.1.refs_0_ = f32[16,8,128]{2,1,0:T(8,128)S(1)} async-done(((f32[16,8,128]{2,1,0:T(8,128)}), f32[16,8,128]{2,1,0:T(8,128)S(1)}, u32[]{:S(2)}, u32[]{:S(2)}) %all-to-all-start.1) | async-done | bytes 65568 | tf_op jit(solution)/shard_map/all_to_all | solution.py:409
  27.2 0.0 copy-done.4
  27.2 1.0 %last.1 = (f32[50,16,128]{2,1,0:T(8,128)}, f32[10,256]{1,0:T(8,128)}) custom-call(f32[16,8,128]{2,1,0:T(8,128)S(1)} %all-to-all-done.1.refs_0_, f32[16,8,128]{2,1,0:T(8,128)S(1)} %all_to_all.10.got.refs_1_, f32[16,128]{1,0:T(8,128)S(1)} %get-tuple-element.17.head_border.refs_2_, f32[16,128]{1,0:T(8,128)S(1)} %get-tuple-element.19.refs_3_, ...), custom_call_target="tpu_custom_call" | custom-call | flops 1000 | bytes 1000 | tf_op jit(solution)/shard_map/last/pallas_call | solution.py:334
Async XLA Ops:
  0.6 15.3 %copy-start = (f32[50,16,128]{2,1,0:T(8,128)S(1)}, f32[50,16,128]{2,1,0:T(8,128)}, u32[]{:S(2)}) copy-start(f32[50,16,128]{2,1,0:T(8,128)} %refs_3_.1) | copy-start | bytes 1228804
  0.6 15.3 %copy-start.1 = (f32[50,16,128]{2,1,0:T(8,128)S(1)}, f32[50,16,128]{2,1,0:T(8,128)}, u32[]{:S(2)}) copy-start(f32[50,16,128]{2,1,0:T(8,128)} %perm.3) | copy-start | bytes 1228804
  17.1 10.1 %all-to-all-start.1 = ((f32[16,8,128]{2,1,0:T(8,128)}), f32[16,8,128]{2,1,0:T(8,128)S(1)}, u32[]{:S(2)}, u32[]{:S(2)}) async-start(f32[16,8,128]{2,1,0:T(8,128)} %get-tuple-element.18), calls=%async_computation.1 | async-start | bytes 131072 | tf_op jit(solution)/shard_map/all_to_all | solution.py:409
  20.6 4.4 %copy-start.2 = (f32[50,16,128]{2,1,0:T(8,128)S(1)}, f32[50,16,128]{2,1,0:T(8,128)}, u32[]{:S(2)}) copy-start(f32[50,16,128]{2,1,0:T(8,128)} %refs_0_.1) | copy-start | bytes 1228804
  20.6 4.4 %copy-start.3 = (f32[50,16,128]{2,1,0:T(8,128)S(1)}, f32[50,16,128]{2,1,0:T(8,128)}, u32[]{:S(2)}) copy-start(f32[50,16,128]{2,1,0:T(8,128)} %refs_1_.1) | copy-start | bytes 1228804
  21.0 4.9 %collective-permute-start.1 = (f32[100,128]{1,0:T(8,128)S(1)}, f32[100,128]{1,0:T(8,128)S(1)}, u32[]{:S(2)}, u32[]{:S(2)}) collective-permute-start(f32[100,128]{1,0:T(8,128)S(1)} %get-tuple-element.27.refs_7_), channel_id=1, source_target_pairs={{4,8},{8,4},{12,16},{16,12},{20,24},{24,20},{5,9},{9,5},{13,17},{1... | collective-permute-start | bytes 153608 | tf_op jit(solution)/shard_map/ppermute | solution.py:418
  21.7 4.2 %collective-permute-start = (f32[100,128]{1,0:T(8,128)S(1)}, f32[100,128]{1,0:T(8,128)S(1)}, u32[]{:S(2)}, u32[]{:S(2)}) collective-permute-start(f32[100,128]{1,0:T(8,128)S(1)} %get-tuple-element.26.refs_10_.refs_6_), channel_id=1, source_target_pairs={{0,4},{4,0},{8,12},{12,8},{16,20},{20,16},{24,28},{28,24},{1,5},{5... | collective-permute-start | bytes 153608 | tf_op jit(solution)/shard_map/ppermute | solution.py:418
  25.0 2.2 %copy-start.4 = (f32[10,256]{1,0:T(8,128)S(1)}, f32[10,256]{1,0:T(8,128)}, u32[]{:S(2)}) copy-start(f32[10,256]{1,0:T(8,128)} %refs_5_.1) | copy-start | bytes 30724

commit v11 on v10

--- a/solution.py
+++ b/solution.py
@@ -136,7 +136,7 @@
     for i, (start, stop) in enumerate(parts):
         rows = pl.ds(start, stop - start)
         large.append(pltpu.make_async_copy(grid.at[rows], head.at[rows], sems.at[i]))
-    for copy in (*small, *large, *extras):
+    for copy in (*large, *small, *extras):
         copy.start()
     for copy in small:
         copy.wait()

time: 28.4 us -> 28.4 us (level)
  no operation moved by 1% of the time
where the time goes in v11:
time: 28.4 us; the launch traced here: 28.1 us
  blocking collectives  13.8 us (49%)
  starting transfers between devices  7.44 us (26%)
  Pallas kernels  4.91 us (17%)
  waiting for transfers between devices  1.23 us (4%)
  between operations  0.72 us (3%)
    all_to_all x1, blocking collectives, per_device(): got = lax.all_to_all(sent, group, split_axis=0, concat_axis=0, tiled=True)  13.8 us
    pallas_call x5, Pallas kernels, run(): kernel(*(pltpu.with_memory_space_constraint(arg, pltpu.HBM) if i == 'H' e...  4.91 us
    ppermute x2, starting transfers between devices, per_device(): lax.ppermute(x_sent[i], axes_x, swap_pairs(x_size, i))  3.94 us
    all_to_all x1, starting transfers between devices, per_device(): back = lax.all_to_all(back, group, split_axis=0, concat_axis=0, tiled=True)  3.5 us
    all_to_all x1, waiting for transfers between devices, per_device(): back = lax.all_to_all(back, group, split_axis=0, concat_axis=0, tiled=True)  1.22 us
  transfers between devices with their start and end apart: 3, of which 1 were waited for; matrix products, arithmetic and copies ran while one was open for 0% of the time, Pallas kernels for 5%

profile of v11, /device:TPU:0, one launch (start us, length us, event | category | flops | bytes accessed | tf_op | source)
XLA Modules:
  0.0 28.1 jit_solution(5017462763774759770)
XLA Ops:
  0.6 0.0 copy-start
  0.6 0.0 copy-start.1
  0.7 1.5 %front.1 = (f32[16,8,128]{2,1,0:T(8,128)S(1)}, f32[50,16,128]{2,1,0:T(8,128)S(1)}, f32[16,128]{1,0:T(8,128)S(1)}, f32[1,8]{1,0:T(1,128)S(1)}, s32[16,128]{1,0:T(8,128)S(1)}) custom-call(s32[2,128]{1,0:T(2,128)} %bitcast.5, s32[2,128]{1,0:T(2,128)} %bitcast.6, f32[2,128]{1,0:T(2,128)} %bitcast.7, f32[2,128]{1,0:T(2,128)} %bitcast.8, f32[50,16,128]{2,1,0:T(8,128)} %refs_4_.1, ...), custom_call_target="tpu_custom_call" | custom-call | flops 1000000000 | bytes 1000000000 | tf_op jit(solution)/shard_map/front/pallas_call | solution.py:334
  2.1 13.8 %all_to_all.10.got.refs_1_ = f32[16,8,128]{2,1,0:T(8,128)S(1)} all-to-all(f32[16,8,128]{2,1,0:T(8,128)S(1)} %get-tuple-element.15), channel_id=1, replica_groups=mesh['sec'=2,'gx'=4,'gy'=4] {'gx','gy'}, dimensions={0} | all-to-all | bytes 131072 | tf_op jit(solution)/shard_map/all_to_all | solution.py:397
  15.9 0.0 copy-done
  15.9 0.0 copy-done.1
  15.9 1.1 %pick.1 = (f32[16,8,128]{2,1,0:T(8,128)}, f32[2,16,128]{2,1,0:T(8,128)S(1)}, f32[2,8,128]{2,1,0:T(8,128)S(1)}, f32[16,128]{1,0:T(8,128)S(1)}) custom-call(f32[16,8,128]{2,1,0:T(8,128)S(1)} %all_to_all.10.got.refs_1_, f32[50,16,128]{2,1,0:T(8,128)S(1)} %get-tuple-element.16.head.refs_2_, f32[50,16,128]{2,1,0:T(8,128)S(1)} %copy-done, ...), custom_call_target="tpu_custom_call" | custom-call | flops 1000 | bytes 1000 | tf_op jit(solution)/shard_map/pick/pallas_call | solution.py:334
  17.1 3.5 %all-to-all-start.1 = ((f32[16,8,128]{2,1,0:T(8,128)}), f32[16,8,128]{2,1,0:T(8,128)S(1)}, u32[]{:S(2)}, u32[]{:S(2)}) async-start(f32[16,8,128]{2,1,0:T(8,128)} %get-tuple-element.18), calls=%async_computation.1 | async-start | bytes 131072 | tf_op jit(solution)/shard_map/all_to_all | solution.py:409
  20.6 0.0 copy-start.2
  20.6 0.0 copy-start.3
  20.6 0.4 %edge.1 = (f32[100,128]{1,0:T(8,128)S(1)}, f32[100,128]{1,0:T(8,128)S(1)}, f32[50,16,128]{2,1,0:T(8,128)S(1)}, f32[50,16,128]{2,1,0:T(8,128)S(1)}) custom-call(f32[50,16,128]{2,1,0:T(8,128)S(1)} %get-tuple-element.16.head.refs_2_, f32[50,16,128]{2,1,0:T(8,128)S(1)} %copy-done, f32[50,16,128]{2,1,0:T(8,128)S(1)} %copy-done.1, ...), custom_call_target="tpu_custom_call" | custom-call | flops 1000 | bytes 1000 | tf_op jit(solution)/shard_map/edge/pallas_call | solution.py:334
  21.0 0.7 %collective-permute-start.1 = (f32[100,128]{1,0:T(8,128)S(1)}, f32[100,128]{1,0:T(8,128)S(1)}, u32[]{:S(2)}, u32[]{:S(2)}) collective-permute-start(f32[100,128]{1,0:T(8,128)S(1)} %get-tuple-element.27.refs_7_), channel_id=1, source_target_pairs={{4,8},{8,4},{12,16},{16,12},{20,24},{24,20},{5,9},{9,5},{13,17},{1... | collective-permute-start | bytes 153608 | tf_op jit(solution)/shard_map/ppermute | solution.py:418
  21.7 3.3 %collective-permute-start = (f32[100,128]{1,0:T(8,128)S(1)}, f32[100,128]{1,0:T(8,128)S(1)}, u32[]{:S(2)}, u32[]{:S(2)}) collective-permute-start(f32[100,128]{1,0:T(8,128)S(1)} %get-tuple-element.26.refs_10_.refs_6_), channel_id=1, source_target_pairs={{0,4},{4,0},{8,12},{12,8},{16,20},{20,16},{24,28},{28,24},{1,5},{5... | collective-permute-start | bytes 153608 | tf_op jit(solution)/shard_map/ppermute | solution.py:418
  25.0 0.0 copy-done.2
  25.0 0.0 copy-done.3
  25.0 0.0 copy-start.4
  25.0 0.9 %interior.1.refs_4_ = f32[50,16,128]{2,1,0:T(8,128)S(1)} custom-call(f32[50,16,128]{2,1,0:T(8,128)S(1)} %copy-done.2, f32[50,16,128]{2,1,0:T(8,128)S(1)} %copy-done.3, f32[50,16,128]{2,1,0:T(8,128)S(1)} %get-tuple-element.16.head.refs_2_, f32[50,16,128]{2,1,0:T(8,128)S(1)} %copy-done, f32[50,16,128]{2,1,0:T(8,128)S(1)} %get-tuple-element.21.refs_4_, ...), custom_call_target="tpu_custom_call" | custom-call | flops 1000 | bytes 1000 | tf_op jit(solution)/shard_map/interior/pallas_call | solution.py:334
  25.9 0.0 collective-permute-done.1.refs_9_
  25.9 0.0 collective-permute-done.refs_8_
  25.9 1.2 %all-to-all-done.1.refs_0_ = f32[16,8,128]{2,1,0:T(8,128)S(1)} async-done(((f32[16,8,128]{2,1,0:T(8,128)}), f32[16,8,128]{2,1,0:T(8,128)S(1)}, u32[]{:S(2)}, u32[]{:S(2)}) %all-to-all-start.1) | async-done | bytes 65568 | tf_op jit(solution)/shard_map/all_to_all | solution.py:409
  27.2 0.0 copy-done.4
  27.2 1.0 %last.1 = (f32[50,16,128]{2,1,0:T(8,128)}, f32[10,256]{1,0:T(8,128)}) custom-call(f32[16,8,128]{2,1,0:T(8,128)S(1)} %all-to-all-done.1.refs_0_, f32[16,8,128]{2,1,0:T(8,128)S(1)} %all_to_all.10.got.refs_1_, f32[16,128]{1,0:T(8,128)S(1)} %get-tuple-element.17.head_border.refs_2_, f32[16,128]{1,0:T(8,128)S(1)} %get-tuple-element.19.refs_3_, ...), custom_call_target="tpu_custom_call" | custom-call | flops 1000 | bytes 1000 | tf_op jit(solution)/shard_map/last/pallas_call | solution.py:334
Async XLA Ops:
  0.6 15.3 %copy-start = (f32[50,16,128]{2,1,0:T(8,128)S(1)}, f32[50,16,128]{2,1,0:T(8,128)}, u32[]{:S(2)}) copy-start(f32[50,16,128]{2,1,0:T(8,128)} %refs_3_.1) | copy-start | bytes 1228804
  0.6 15.3 %copy-start.1 = (f32[50,16,128]{2,1,0:T(8,128)S(1)}, f32[50,16,128]{2,1,0:T(8,128)}, u32[]{:S(2)}) copy-start(f32[50,16,128]{2,1,0:T(8,128)} %perm.3) | copy-start | bytes 1228804
  17.1 10.1 %all-to-all-start.1 = ((f32[16,8,128]{2,1,0:T(8,128)}), f32[16,8,128]{2,1,0:T(8,128)S(1)}, u32[]{:S(2)}, u32[]{:S(2)}) async-start(f32[16,8,128]{2,1,0:T(8,128)} %get-tuple-element.18), calls=%async_computation.1 | async-start | bytes 131072 | tf_op jit(solution)/shard_map/all_to_all | solution.py:409
  20.6 4.4 %copy-start.2 = (f32[50,16,128]{2,1,0:T(8,128)S(1)}, f32[50,16,128]{2,1,0:T(8,128)}, u32[]{:S(2)}) copy-start(f32[50,16,128]{2,1,0:T(8,128)} %refs_0_.1) | copy-start | bytes 1228804
  20.6 4.4 %copy-start.3 = (f32[50,16,128]{2,1,0:T(8,128)S(1)}, f32[50,16,128]{2,1,0:T(8,128)}, u32[]{:S(2)}) copy-start(f32[50,16,128]{2,1,0:T(8,128)} %refs_1_.1) | copy-start | bytes 1228804
  21.0 4.9 %collective-permute-start.1 = (f32[100,128]{1,0:T(8,128)S(1)}, f32[100,128]{1,0:T(8,128)S(1)}, u32[]{:S(2)}, u32[]{:S(2)}) collective-permute-start(f32[100,128]{1,0:T(8,128)S(1)} %get-tuple-element.27.refs_7_), channel_id=1, source_target_pairs={{4,8},{8,4},{12,16},{16,12},{20,24},{24,20},{5,9},{9,5},{13,17},{1... | collective-permute-start | bytes 153608 | tf_op jit(solution)/shard_map/ppermute | solution.py:418
  21.7 4.2 %collective-permute-start = (f32[100,128]{1,0:T(8,128)S(1)}, f32[100,128]{1,0:T(8,128)S(1)}, u32[]{:S(2)}, u32[]{:S(2)}) collective-permute-start(f32[100,128]{1,0:T(8,128)S(1)} %get-tuple-element.26.refs_10_.refs_6_), channel_id=1, source_target_pairs={{0,4},{4,0},{8,12},{12,8},{16,20},{20,16},{24,28},{28,24},{1,5},{5... | collective-permute-start | bytes 153608 | tf_op jit(solution)/shard_map/ppermute | solution.py:418
  25.0 2.2 %copy-start.4 = (f32[10,256]{1,0:T(8,128)S(1)}, f32[10,256]{1,0:T(8,128)}, u32[]{:S(2)}) copy-start(f32[10,256]{1,0:T(8,128)} %refs_5_.1) | copy-start | bytes 30724
